TPU v7x, 512 devices: a whole 4x4x16 slice. The times are simulated.
512 devices in a mesh: lat: 64 (over z, y), ord: 2 (over core), orb: 4 (over x).
Axes of the slice: x: 4, y: 4, z: 16, core: 2. Of those that a mesh axis runs over, the one named last changes fastest.
Arguments:
- anomaly: bfloat16 [2, 1024, 4320], P(None, 'lat'), may hold values from -6 to 6
- row_weight: float32 [2, 1024], replicated, may hold values from 0.2 to 1
- panel: bfloat16 [4, 64, 1024, 2, 640], P('orb', None, 'lat', 'ord'), may hold values from -0.125 to 0.125
- order_value: int32 [4, 64], P('orb'), may hold values from 0 to 2159
- deg_first: int32 [4, 64], P('orb', 'lat'), may hold values from 0 to 2190
- sat_rows: bfloat16 [131072, 256], P(('lat', 'ord', 'orb')), may hold values from -0.25 to 0.25
- sat_slot: int32 [131072, 1], P(('lat', 'ord', 'orb')), may hold values from 0 to 255; in each aligned block of 256 rows (0 to 255, 256 to 511, ...) at most 2 rows name the same one
Outputs:
- normals: float32 [4, 64, 2, 640, 2, 640], P('orb', 'lat', 'ord')
- right_side: float32 [4, 64, 2, 2, 640], P('orb', 'lat', None, 'ord')
Inputs may be any that keep to these rules, and one draw needn't show every extreme that they name: `sat_slot`: among the 256 rows of one device no order slot appears more than 2 times.
All inputs are finite; a program needn't handle non-finite values.
Results may differ from a plain program's by a relative error of at most 0.0029.
Values may be sent and summed in bfloat16 or wider, within the bound.
No kernel may reach another device: no remote copies, remote signals or barrier semaphores. Data moves between devices by JAX's collectives and lax.ppermute only.
A program may use at most 64 MiB of HBM per device.

v0:
```python
import math

import jax
import jax.numpy as jnp
from jax import lax
from jax.experimental import pallas as pl
from jax.experimental.pallas import tpu as pltpu
from jax.sharding import PartitionSpec as P


LMAX = 2190
F32 = jnp.float32
BF16 = jnp.bfloat16
I32 = jnp.int32
STEP = 144


def iota(shape, dim):
    return lax.broadcasted_iota(I32, shape, dim)


def dot(left, right, dims):
    return lax.dot_general(left, right, (dims, ((), ())), preferred_element_type=F32)


def turn(product, length):
    whole = jnp.floor(product * (1.0 / length))
    return (product - whole * length) * (2.0 * math.pi / length)


def prepare_kernel(place, anomaly, weight, order, rows, slot, out, table_high, table_low):
    y, x = place[1], place[2]
    length = anomaly.shape[2]
    order_pair = jnp.concatenate([order[...], order[...]], axis=1).astype(F32)
    fine = turn(iota((STEP, 128), 0).astype(F32) * order_pair, length)
    coarse_count = length // STEP
    coarse_rows = -(-coarse_count // 8) * 8
    coarse = turn(iota((coarse_rows, 128), 0).astype(F32) * (order_pair * STEP), length)
    cos_fine, sin_fine = jnp.cos(fine), jnp.sin(fine)
    cos_coarse, sin_coarse = jnp.cos(coarse), jnp.sin(coarse)
    left = iota((coarse_rows, 128), 1) < 64
    by_cos = jnp.where(left, cos_coarse, sin_coarse)
    by_sin = jnp.where(left, -sin_coarse, cos_coarse)
    for k in range(coarse_count):
        value = by_cos[k : k + 1] * cos_fine + by_sin[k : k + 1] * sin_fine
        high = value.astype(BF16)
        table_high[k * STEP : (k + 1) * STEP] = high
        table_low[k * STEP : (k + 1) * STEP] = (value - high.astype(F32)).astype(BF16)
    samples = anomaly[...].reshape(32, length)
    spectra = dot(samples, table_high[...], ((1,), (0,))) + dot(samples, table_low[...], ((1,), (0,)))
    coef = (spectra * math.sqrt(2.0 / length) * weight[...]).astype(BF16)
    at, own = iota((64, 64), 0), iota((64, 64), 1)

    def position(slot_in_group):
        side = ((slot_in_group & 3) - y) & 3
        return side * 16 + (slot_in_group >> 2)

    pick = (position(own) == at).astype(F32).astype(BF16)
    out[:, 2048:2176] = jnp.concatenate(
        [
            dot(pick, coef[:, :64], ((1,), (1,))),
            dot(pick, coef[:, 64:], ((1,), (1,))),
            jnp.zeros((64, 64), F32),
        ],
        axis=1,
    ).astype(BF16)
    col, to = iota((256, 256), 0), iota((256, 256), 1)
    apart = ((col & 1) * 128 + (col >> 1) == to).astype(F32).astype(BF16)
    split_rows = dot(rows[...], apart, ((1,), (0,))).astype(BF16)
    slot_row = jnp.broadcast_to(slot[...], (256, 256))
    slot_col = slot_row.T
    earlier = (slot_col == slot_row) & (col < to)
    rank = jnp.sum(jnp.where(earlier, 1.0, 0.0), axis=0, keepdims=True).astype(I32)
    slot_now = slot[...]
    bucket = ((((slot_now >> 6) - x) & 3) * 2 + rank) * 64 + position(slot_now & 63)
    chosen = (jnp.broadcast_to(bucket, (512, 256)) == iota((512, 256), 0)).astype(F32).astype(BF16)
    placed = dot(chosen, split_rows, ((1,), (0,))).astype(BF16)
    for q in range(8):
        out[:, q * 256 : (q + 1) * 256] = placed[q * 64 : (q + 1) * 64]


def gather_kernel(place, sat, coef_out, sent, kept):
    y, p = place[1], place[3]
    gram = jnp.zeros((256, 256), F32)
    for c in range(8):
        block = sat[:, c * 256 : (c + 1) * 256]
        gram = gram + dot(block, block, ((0,), (0,)))
    kept[...] = jnp.where(p == 0, gram[:128], gram[128:])
    sent[...] = jnp.where(p == 0, gram[128:], gram[:128])
    index = iota((64, 1024), 0)
    source = (index & 60) + ((y - index) & 3)
    mine = source == (iota((64, 1024), 1) >> 4)
    spread = ((iota((16, 1024), 1) & 15) == iota((16, 1024), 0)).astype(F32).astype(BF16)
    lines = []
    for c in range(4):
        wide = dot(sat[:, 2048 + c * 16 : 2048 + (c + 1) * 16], spread, ((1,), (0,)))
        lines.append(jnp.sum(jnp.where(mine, wide, 0.0), axis=0, keepdims=True))
    lines.append(jnp.zeros((4, 1024), F32))
    coef_out[...] = jnp.concatenate(lines, axis=0).astype(BF16)


def weight_kernel(weight, plus_out, minus_out):
    plus = weight[0:1] + weight[1:2]
    minus = weight[0:1] - weight[1:2]
    plus_out[...] = jnp.broadcast_to(plus, (128, 1024)).T
    minus_out[...] = jnp.broadcast_to(minus, (128, 1024)).T


def live_row(first, parity, half):
    return (first + 2 * iota((1, half), 1) + parity <= LMAX).astype(F32)


def same_kernel(place, own, plus, turned, same):
    p, first = place[3], place[4]
    half = own.shape[1]
    wide = own[...].astype(F32) * live_row(first, p, half)
    turned_now = wide.astype(BF16).T
    turned[...] = turned_now
    scale = jnp.concatenate([plus[...]] * (half // 128), axis=1)
    same[...] = dot(turned_now, (wide * scale).astype(BF16), ((1,), (0,)))


def cross_kernel(place, turned, other, minus, same, out, scaled):
    p, first = place[3], place[4]
    half = other.shape[1]

    @pl.when(pl.program_id(0) == 0)
    def _():
        live_other = live_row(first, 1 - p, half)
        scale = jnp.concatenate([minus[...]] * (half // 128), axis=1)
        scaled[...] = (other[...].astype(F32) * live_other * scale).astype(BF16)

    cross = dot(turned[...], scaled[...], ((1,), (0,)))
    same_now = same[...]
    out[:, 0, :] = jnp.where(p == 0, same_now, cross)
    out[:, 1, :] = jnp.where(p == 0, cross, same_now)


def right_kernel(place, coef, turned, right):
    p, first, order = place[3], place[4], place[5]
    half = turned.shape[0]
    product = dot(coef[...], turned[...], ((1,), (1,)))
    sign = 1.0 - 2.0 * ((first + p + order + iota((1, half), 1) * 2) & 1).astype(F32)
    right[0] = product[0:1] + sign * product[1:2]
    right[1] = product[2:3] + sign * product[3:4]


def add_kernel(place, kept, came, normals, out):
    p, first = place[3], place[4]
    live_left = (first + 2 * iota((128, 128), 0) + p <= LMAX).astype(F32)
    gram = kept[...] + came[...]
    for q in range(2):
        live_top = (first + 2 * iota((128, 128), 1) + q <= LMAX).astype(F32)
        add = gram[:, q * 128 : (q + 1) * 128] * (live_left * live_top)
        out[:, q, :] = normals[:, q, :] + add


def whole(memory_space=pltpu.VMEM):
    return pl.BlockSpec(memory_space=memory_space)


def shards(anomaly, row_weight, panel, order_value, deg_first, sat_rows, sat_slot):
    lat_index = lax.axis_index("lat")
    parity = lax.axis_index("ord")
    orb_index = lax.axis_index("orb")
    row_count = panel.shape[2]
    half = panel.shape[4]
    row_all = row_weight.shape[1]
    z, y = lat_index // 4, lat_index % 4
    smem = whole(pltpu.SMEM)

    arrived = lax.all_to_all(panel, "lat", split_axis=1, concat_axis=2, tiled=True)

    own_order = lax.dynamic_slice_in_dim(order_value[0], lat_index, 1, 0)[0]
    place = jnp.stack([z, y, orb_index, parity, deg_first[0, 0], own_order]).astype(I32)
    local_weight = lax.dynamic_slice_in_dim(row_weight, lat_index * row_count, row_count, 1)
    packed = pl.pallas_call(
        prepare_kernel,
        out_shape=jax.ShapeDtypeStruct((64, 2176), BF16),
        in_specs=[smem] + [whole()] * 5,
        out_specs=whole(),
        scratch_shapes=[pltpu.VMEM((anomaly.shape[2], 128), BF16)] * 2,
        name="prepare",
    )(
        place,
        anomaly,
        local_weight.reshape(2 * row_count, 1),
        order_value,
        sat_rows,
        sat_slot.reshape(1, sat_slot.shape[0]),
    )
    weights = pl.pallas_call(
        weight_kernel,
        out_shape=(jax.ShapeDtypeStruct((row_all, 128), F32),) * 2,
        in_specs=[whole()],
        out_specs=(whole(),) * 2,
        name="weights",
    )
    plus, minus = weights(row_weight)

    width = packed.shape[1]
    blocks = packed.reshape(4, 16, width)
    sides = [blocks[0]]
    for e in (1, 2, 3):
        ring = [(a * 4 + b, a * 4 + (b + e) % 4) for a in range(16) for b in range(4)]
        sides.append(lax.ppermute(blocks[e], "lat", ring))
    sides = jnp.stack(sides, axis=1)
    groups = [sides[:, :, :512]]
    for f in (1, 2, 3):
        ring = [(i, (i + f) % 4) for i in range(4)]
        groups.append(lax.ppermute(sides[:, :, f * 512 : (f + 1) * 512], "orb", ring))
    packed = jnp.concatenate(groups + [sides[:, :, 2048:]], axis=2)
    columns = [[a * 4 + b for a in range(16)] for b in range(4)]
    packed = lax.all_to_all(
        packed, "lat", split_axis=0, concat_axis=0, axis_index_groups=columns, tiled=True
    )
    packed = packed.reshape(64, width)

    own_panel = arrived.reshape(row_all, half)
    other_panel = lax.ppermute(own_panel, "ord", [(0, 1), (1, 0)])
    same_call = pl.pallas_call(
        same_kernel,
        out_shape=(
            jax.ShapeDtypeStruct((half, row_all), BF16),
            jax.ShapeDtypeStruct((half, half), F32),
        ),
        in_specs=[smem] + [whole()] * 2,
        out_specs=(whole(),) * 2,
        name="same",
    )
    turned, same = same_call(place, own_panel, plus)
    cross_call = pl.pallas_call(
        cross_kernel,
        grid=(half // 128,),
        out_shape=jax.ShapeDtypeStruct((half, 2, half), F32),
        in_specs=[
            smem,
            pl.BlockSpec((128, row_all), lambda i: (i, 0)),
            pl.BlockSpec((row_all, half), lambda i: (0, 0)),
            pl.BlockSpec((row_all, 128), lambda i: (0, 0)),
            pl.BlockSpec((128, half), lambda i: (i, 0)),
        ],
        out_specs=pl.BlockSpec((128, 2, half), lambda i: (i, 0, 0)),
        scratch_shapes=[pltpu.VMEM((row_all, half), BF16)],
        name="cross",
    )
    normals = cross_call(place, turned, other_panel, minus, same)

    coef, sent, kept = pl.pallas_call(
        gather_kernel,
        out_shape=(
            jax.ShapeDtypeStruct((8, row_all), BF16),
            jax.ShapeDtypeStruct((128, 256), F32),
            jax.ShapeDtypeStruct((128, 256), F32),
        ),
        in_specs=[smem, whole()],
        out_specs=(whole(),) * 3,
        name="gather",
    )(place, packed)
    came = lax.ppermute(sent, "ord", [(0, 1), (1, 0)])
    right = pl.pallas_call(
        right_kernel,
        out_shape=jax.ShapeDtypeStruct((2, 1, half), F32),
        in_specs=[smem] + [whole()] * 2,
        out_specs=whole(),
        name="right",
    )(place, coef, turned)
    corner = pl.BlockSpec((128, 2, 128), lambda i: (0, 0, 0))
    gram_spec = pl.BlockSpec((128, 256), lambda i: (0, 0))
    normals = pl.pallas_call(
        add_kernel,
        grid=(1,),
        out_shape=jax.ShapeDtypeStruct((half, 2, half), F32),
        in_specs=[smem, gram_spec, gram_spec, corner],
        out_specs=corner,
        input_output_aliases={3: 0},
        name="add",
    )(place, kept, came, normals)
    return (normals[None, None, None], right[None, None])


def solution(mesh):
    in_specs = (
        P(None, "lat", None),
        P(),
        P("orb", None, "lat", "ord", None),
        P("orb", None),
        P("orb", "lat"),
        P(("lat", "ord", "orb"), None),
        P(("lat", "ord", "orb"), None),
    )
    out_specs = (P("orb", "lat", "ord", None, None, None), P("orb", "lat", None, "ord", None))

    return jax.shard_map(shards, mesh=mesh, in_specs=in_specs, out_specs=out_specs, check_vma=False)
```

profile of v0, /device:TPU:1, one launch (start us, length us, event | category | flops | bytes accessed | tf_op | source)
XLA Modules:
  0.0 135.7 jit_solution(9015393108237888726)
XLA Ops:
  0.6 0.0 copy-start.3
  0.6 19.3 %all-to-all-start.1 = ((bf16[1,64,16,1,640]{4,2,3,0,1:T(8,128)(2,1)}), bf16[1,64,16,1,640]{4,2,3,0,1:T(8,128)(2,1)S(1)}, u32[]{:S(2)}, u32[]{:S(2)}) async-start(bf16[1,64,16,1,640]{4,2,3,0,1:T(8,128)(2,1)} %bitcast.20), calls=%async_computation.1 | async-start | bytes 2621440 | tf_op jit(solution)/shard_map/all_to_all | solution.py:172
  20.6 0.8 constant_dynamic-slice_fusion
  21.4 0.7 reshape.34.weight
  22.0 0.0 copy-done.3
  22.0 0.6 constant_dynamic-slice_fusion.1
  22.7 1.3 stack.31.place
  24.0 3.7 %prepare.1 = bf16[64,2176]{1,0:T(8,128)(2,1)} custom-call(s32[6]{0:T(128)} %stack.31.place, bf16[2,16,4320]{2,1,0:T(8,128)(2,1)} %anomaly.1, f32[32,1]{1,0:T(8,128)} %reshape.34.weight, s32[1,64]{1,0:T(1,128)} %order.1, bf16[256,256]{1,0:T(8,128)(2,1)} %rows.1, s32[1,256]{1,0:T(1,128)} %bitcast.28), custom_call_target="tpu_custom_call" | custom-call | tf_op jit(solution)/shard_map/prepare/pallas_call | solution.py:177
  27.6 1.0 slice_bitcast_fusion
  28.6 4.1 %collective-permute-start.2 = (bf16[16,2176]{1,0:T(8,128)(2,1)S(1)}, bf16[16,2176]{1,0:T(8,128)(2,1)S(1)}, u32[]{:S(2)}, u32[]{:S(2)}) collective-permute-start(bf16[16,2176]{1,0:T(8,128)(2,1)S(1)} %get-tuple-element.21), channel_id=1, source_target_pairs={{0,24},{8,0},{16,8},{24,16},{32,56},{40,32},{48,40},{56,48},{64,88... | collective-permute-start | bytes 208904 | tf_op jit(solution)/shard_map/ppermute | solution.py:206
  32.8 1.9 %collective-permute-start = (bf16[16,2176]{1,0:T(8,128)(2,1)S(1)}, bf16[16,2176]{1,0:T(8,128)(2,1)S(1)}, u32[]{:S(2)}, u32[]{:S(2)}) collective-permute-start(bf16[16,2176]{1,0:T(8,128)(2,1)S(1)} %get-tuple-element.23), channel_id=1, source_target_pairs={{0,8},{8,16},{16,24},{24,0},{32,40},{40,48},{48,56},{56,32},{64,72... | collective-permute-start | bytes 208904 | tf_op jit(solution)/shard_map/ppermute | solution.py:206
  34.7 3.7 %collective-permute-start.1 = (bf16[16,2176]{1,0:T(8,128)(2,1)S(1)}, bf16[16,2176]{1,0:T(8,128)(2,1)S(1)}, u32[]{:S(2)}, u32[]{:S(2)}) collective-permute-start(bf16[16,2176]{1,0:T(8,128)(2,1)S(1)} %get-tuple-element.22), channel_id=1, source_target_pairs={{0,16},{8,24},{16,0},{24,8},{32,48},{40,56},{48,32},{56,40},{64,80... | collective-permute-start | bytes 208904 | tf_op jit(solution)/shard_map/ppermute | solution.py:206
  38.4 0.0 collective-permute-done.2
  38.4 1.3 collective-permute-done
  39.7 2.0 %collective-permute-done.1 = bf16[16,2176]{1,0:T(8,128)(2,1)S(1)} collective-permute-done((bf16[16,2176]{1,0:T(8,128)(2,1)S(1)}, bf16[16,2176]{1,0:T(8,128)(2,1)S(1)}, u32[]{:S(2)}, u32[]{:S(2)}) %collective-permute-start.1) | collective-permute-done | bytes 69664 | tf_op jit(solution)/shard_map/ppermute | solution.py:206
  41.7 3.1 %collective-permute-start.3 = (bf16[16,4,512]{2,0,1:T(8,128)(2,1)S(1)}, bf16[16,4,512]{2,0,1:T(8,128)(2,1)S(1)}, u32[]{:S(2)}, u32[]{:S(2)}) collective-permute-start(bf16[16,4,512]{2,0,1:T(8,128)(2,1)S(1)} %get-tuple-element.18), channel_id=1, source_target_pairs={{0,1},{1,2},{2,3},{3,0},{4,5},{5,6},{6,7},{7,4},{8,9},{9,10},{10,1... | collective-permute-start | bytes 196616 | tf_op jit(solution)/shard_map/ppermute | solution.py:211
  44.8 4.4 %collective-permute-start.4 = (bf16[16,4,512]{2,0,1:T(8,128)(2,1)S(1)}, bf16[16,4,512]{2,0,1:T(8,128)(2,1)S(1)}, u32[]{:S(2)}, u32[]{:S(2)}) collective-permute-start(bf16[16,4,512]{2,0,1:T(8,128)(2,1)S(1)} %get-tuple-element.17), channel_id=1, source_target_pairs={{0,2},{1,3},{2,0},{3,1},{4,6},{5,7},{6,4},{7,5},{8,10},{9,11},{10,... | collective-permute-start | bytes 196616 | tf_op jit(solution)/shard_map/ppermute | solution.py:211
  49.2 3.1 %collective-permute-start.5 = (bf16[16,4,512]{2,0,1:T(8,128)(2,1)S(1)}, bf16[16,4,512]{2,0,1:T(8,128)(2,1)S(1)}, u32[]{:S(2)}, u32[]{:S(2)}) collective-permute-start(bf16[16,4,512]{2,0,1:T(8,128)(2,1)S(1)} %get-tuple-element.16), channel_id=1, source_target_pairs={{0,3},{1,0},{2,1},{3,2},{4,7},{5,4},{6,5},{7,6},{8,11},{9,8},{10,9... | collective-permute-start | bytes 196616 | tf_op jit(solution)/shard_map/ppermute | solution.py:211
  52.3 0.0 collective-permute-done.3
  52.3 0.0 collective-permute-done.4
  52.3 30.7 %all-to-all-done.1 = bf16[1,64,16,1,640]{4,2,3,0,1:T(8,128)(2,1)S(1)} async-done(((bf16[1,64,16,1,640]{4,2,3,0,1:T(8,128)(2,1)}), bf16[1,64,16,1,640]{4,2,3,0,1:T(8,128)(2,1)S(1)}, u32[]{:S(2)}, u32[]{:S(2)}) %all-to-all-start.1) | async-done | bytes 1310752 | tf_op jit(solution)/shard_map/all_to_all | solution.py:172
  83.0 0.0 copy-start
  83.0 6.3 %collective-permute-start.7 = (bf16[1024,640]{1,0:T(8,128)(2,1)S(1)}, bf16[1024,640]{1,0:T(8,128)(2,1)S(1)}, u32[]{:S(2)}, u32[]{:S(2)}) collective-permute-start(bf16[1024,640]{1,0:T(8,128)(2,1)S(1)} %bitcast.18), channel_id=1, source_target_pairs={{0,4},{4,0},{1,5},{5,1},{2,6},{6,2},{3,7},{7,3},{8,12},{12,8},{9,1... | collective-permute-start | bytes 3932168 | tf_op jit(solution)/shard_map/ppermute | solution.py:220
  89.3 0.0 collective-permute-done.5
  89.4 0.1 copy.13
  89.5 17.2 %all_to_all.14 = bf16[16,4,2176]{2,1,0:T(4,128)(2,1)S(1)} all-to-all(bf16[16,4,2176]{2,1,0:T(4,128)(2,1)S(1)} %copy.13), channel_id=1, replica_groups={{0,32,64,96,128,160,192,224,256,288,320,352,384,416,448,480},{8,40,72,1..., dimensions={0} | all-to-all | bytes 557056 | tf_op jit(solution)/shard_map/all_to_all | solution.py:214
  106.7 0.8 reshape.32.sat
  107.4 2.3 %gather.1 = (bf16[8,1024]{1,0:T(8,128)(2,1)}, f32[128,256]{1,0:T(8,128)}, f32[128,256]{1,0:T(8,128)}) custom-call(s32[6]{0:T(128)} %stack.31.place, bf16[64,2176]{1,0:T(8,128)(2,1)} %reshape.32.sat), custom_call_target="tpu_custom_call" | custom-call | tf_op jit(solution)/shard_map/gather/pallas_call | solution.py:249
  109.7 7.2 %collective-permute-start.6 = (f32[128,256]{1,0:T(8,128)}, f32[128,256]{1,0:T(8,128)S(1)}, u32[]{:S(2)}, u32[]{:S(2)}) collective-permute-start(f32[128,256]{1,0:T(8,128)} %get-tuple-element.10), channel_id=1, source_target_pairs={{0,4},{4,0},{1,5},{5,1},{2,6},{6,2},{3,7},{7,3},{8,12},{12,8},{9,1... | collective-permute-start | bytes 393224 | tf_op jit(solution)/shard_map/ppermute | solution.py:260
  116.9 1.9 %weights.1 = (f32[1024,128]{1,0:T(8,128)}, f32[1024,128]{1,0:T(8,128)}) custom-call(f32[2,1024]{1,0:T(2,128)} %weight.1), custom_call_target="tpu_custom_call" | custom-call | tf_op jit(solution)/shard_map/weights/pallas_call | solution.py:199
  118.8 0.0 copy-done
  118.8 3.9 %same.1 = (bf16[640,1024]{1,0:T(8,128)(2,1)}, f32[640,640]{1,0:T(8,128)}) custom-call(s32[6]{0:T(128)} %stack.31.place, bf16[1024,640]{1,0:T(8,128)(2,1)} %bitcast.19, f32[1024,128]{1,0:T(8,128)} %get-tuple-element.11.plus), custom_call_target="tpu_custom_call" | custom-call | tf_op jit(solution)/shard_map/same/pallas_call | solution.py:231
  122.7 2.4 %right.1 = f32[2,1,640]{2,1,0:T(1,128)} custom-call(s32[6]{0:T(128)} %stack.31.place, bf16[8,1024]{1,0:T(8,128)(2,1)} %get-tuple-element.15.coef, bf16[640,1024]{1,0:T(8,128)(2,1)} %get-tuple-element.12.turned), custom_call_target="tpu_custom_call" | custom-call | tf_op jit(solution)/shard_map/right/pallas_call | solution.py:261
  125.1 0.0 collective-permute-done.7.other
  125.1 0.0 copy-start.1
  125.1 1.1 copy-done.1
  126.2 7.0 %cross.1.normals = f32[640,2,640]{2,1,0:T(2,128)} custom-call(s32[6]{0:T(128)} %stack.31.place, bf16[640,1024]{1,0:T(8,128)(2,1)} %get-tuple-element.12.turned, bf16[1024,640]{1,0:T(8,128)(2,1)} %copy-done.1, f32[1024,128]{1,0:T(8,128)} %get-tuple-element.13.minus, f32[640,640]{1,0:T(8,128)} %get-tuple-element.14.same), custom_call_target="tpu_custom_call" | custom-call | tf_op jit(solution)/shard_map/cross/pallas_call | solution.py:247
  133.1 0.0 collective-permute-done.6.came
  133.1 0.0 copy-start.2
  133.1 0.7 copy-done.2
  133.8 1.9 %add.15 = f32[640,2,640]{2,1,0:T(2,128)} custom-call(s32[6]{0:T(128)} %stack.31.place, f32[128,256]{1,0:T(8,128)} %get-tuple-element.9.kept, f32[128,256]{1,0:T(8,128)} %copy-done.2, f32[640,2,640]{2,1,0:T(2,128)} %cross.1.normals), custom_call_target="tpu_custom_call", output_to_operand_aliasing={{}: (3, {})} | custom-call | tf_op jit(solution)/shard_map/add/pallas_call | solution.py:270
  (6 shorter events, 0.1 us)
Async XLA Ops:
  0.6 21.4 %copy-start.3 = (s32[1,64]{1,0:T(1,128)S(1)}, s32[1,64]{1,0:T(1,128)}, u32[]{:S(2)}) copy-start(s32[1,64]{1,0:T(1,128)} %order.1) | copy-start | bytes 772
  0.6 82.3 %all-to-all-start.1 = ((bf16[1,64,16,1,640]{4,2,3,0,1:T(8,128)(2,1)}), bf16[1,64,16,1,640]{4,2,3,0,1:T(8,128)(2,1)S(1)}, u32[]{:S(2)}, u32[]{:S(2)}) async-start(bf16[1,64,16,1,640]{4,2,3,0,1:T(8,128)(2,1)} %bitcast.20), calls=%async_computation.1 | async-start | bytes 2621440 | tf_op jit(solution)/shard_map/all_to_all | solution.py:172
  28.6 9.7 %collective-permute-start.2 = (bf16[16,2176]{1,0:T(8,128)(2,1)S(1)}, bf16[16,2176]{1,0:T(8,128)(2,1)S(1)}, u32[]{:S(2)}, u32[]{:S(2)}) collective-permute-start(bf16[16,2176]{1,0:T(8,128)(2,1)S(1)} %get-tuple-element.21), channel_id=1, source_target_pairs={{0,24},{8,0},{16,8},{24,16},{32,56},{40,32},{48,40},{56,48},{64,88... | collective-permute-start | bytes 208904 | tf_op jit(solution)/shard_map/ppermute | solution.py:206
  32.8 6.9 %collective-permute-start = (bf16[16,2176]{1,0:T(8,128)(2,1)S(1)}, bf16[16,2176]{1,0:T(8,128)(2,1)S(1)}, u32[]{:S(2)}, u32[]{:S(2)}) collective-permute-start(bf16[16,2176]{1,0:T(8,128)(2,1)S(1)} %get-tuple-element.23), channel_id=1, source_target_pairs={{0,8},{8,16},{16,24},{24,0},{32,40},{40,48},{48,56},{56,32},{64,72... | collective-permute-start | bytes 208904 | tf_op jit(solution)/shard_map/ppermute | solution.py:206
  34.7 6.9 %collective-permute-start.1 = (bf16[16,2176]{1,0:T(8,128)(2,1)S(1)}, bf16[16,2176]{1,0:T(8,128)(2,1)S(1)}, u32[]{:S(2)}, u32[]{:S(2)}) collective-permute-start(bf16[16,2176]{1,0:T(8,128)(2,1)S(1)} %get-tuple-element.22), channel_id=1, source_target_pairs={{0,16},{8,24},{16,0},{24,8},{32,48},{40,56},{48,32},{56,40},{64,80... | collective-permute-start | bytes 208904 | tf_op jit(solution)/shard_map/ppermute | solution.py:206
  41.7 10.6 %collective-permute-start.3 = (bf16[16,4,512]{2,0,1:T(8,128)(2,1)S(1)}, bf16[16,4,512]{2,0,1:T(8,128)(2,1)S(1)}, u32[]{:S(2)}, u32[]{:S(2)}) collective-permute-start(bf16[16,4,512]{2,0,1:T(8,128)(2,1)S(1)} %get-tuple-element.18), channel_id=1, source_target_pairs={{0,1},{1,2},{2,3},{3,0},{4,5},{5,6},{6,7},{7,4},{8,9},{9,10},{10,1... | collective-permute-start | bytes 196616 | tf_op jit(solution)/shard_map/ppermute | solution.py:211
  44.8 7.5 %collective-permute-start.4 = (bf16[16,4,512]{2,0,1:T(8,128)(2,1)S(1)}, bf16[16,4,512]{2,0,1:T(8,128)(2,1)S(1)}, u32[]{:S(2)}, u32[]{:S(2)}) collective-permute-start(bf16[16,4,512]{2,0,1:T(8,128)(2,1)S(1)} %get-tuple-element.17), channel_id=1, source_target_pairs={{0,2},{1,3},{2,0},{3,1},{4,6},{5,7},{6,4},{7,5},{8,10},{9,11},{10,... | collective-permute-start | bytes 196616 | tf_op jit(solution)/shard_map/ppermute | solution.py:211
  49.2 40.1 %collective-permute-start.5 = (bf16[16,4,512]{2,0,1:T(8,128)(2,1)S(1)}, bf16[16,4,512]{2,0,1:T(8,128)(2,1)S(1)}, u32[]{:S(2)}, u32[]{:S(2)}) collective-permute-start(bf16[16,4,512]{2,0,1:T(8,128)(2,1)S(1)} %get-tuple-element.16), channel_id=1, source_target_pairs={{0,3},{1,0},{2,1},{3,2},{4,7},{5,4},{6,5},{7,6},{8,11},{9,8},{10,9... | collective-permute-start | bytes 196616 | tf_op jit(solution)/shard_map/ppermute | solution.py:211
  83.0 35.8 %copy-start = (bf16[1,64,16,1,640]{4,2,3,0,1:T(8,128)(2,1)}, bf16[1,64,16,1,640]{4,2,3,0,1:T(8,128)(2,1)S(1)}, u32[]{:S(2)}) copy-start(bf16[1,64,16,1,640]{4,2,3,0,1:T(8,128)(2,1)S(1)} %all-to-all-done.1) | copy-start | bytes 3932164
  83.0 42.1 %collective-permute-start.7 = (bf16[1024,640]{1,0:T(8,128)(2,1)S(1)}, bf16[1024,640]{1,0:T(8,128)(2,1)S(1)}, u32[]{:S(2)}, u32[]{:S(2)}) collective-permute-start(bf16[1024,640]{1,0:T(8,128)(2,1)S(1)} %bitcast.18), channel_id=1, source_target_pairs={{0,4},{4,0},{1,5},{5,1},{2,6},{6,2},{3,7},{7,3},{8,12},{12,8},{9,1... | collective-permute-start | bytes 3932168 | tf_op jit(solution)/shard_map/ppermute | solution.py:220
  109.7 23.4 %collective-permute-start.6 = (f32[128,256]{1,0:T(8,128)}, f32[128,256]{1,0:T(8,128)S(1)}, u32[]{:S(2)}, u32[]{:S(2)}) collective-permute-start(f32[128,256]{1,0:T(8,128)} %get-tuple-element.10), channel_id=1, source_target_pairs={{0,4},{4,0},{1,5},{5,1},{2,6},{6,2},{3,7},{7,3},{8,12},{12,8},{9,1... | collective-permute-start | bytes 393224 | tf_op jit(solution)/shard_map/ppermute | solution.py:260
  125.1 1.1 copy-start.1
  133.1 0.7 copy-start.2
where the time goes:
time: 136 us
  starting transfers between devices  53 us (39%)
  waiting for transfers between devices  33.9 us (25%)
  Pallas kernels  23 us (17%)
  blocking collectives  17.2 us (13%)
  local copies, waits for them, and re-layouts  7.04 us (5%)
  between operations  1.48 us (1%)
    all_to_all x1, waiting for transfers between devices, shards(): lax.all_to_all(panel, 'lat', split_axis=1, concat_axis=2, tiled=True)  30.7 us
    all_to_all x1, starting transfers between devices, shards(): lax.all_to_all(panel, 'lat', split_axis=1, concat_axis=2, tiled=True)  19.3 us
    all_to_all x1, blocking collectives, shards(): lax.all_to_all(packed, 'lat', split_axis=0, concat_axis=0, axis_index_gro...  17.2 us
    ppermute x3, starting transfers between devices, shards(): groups.append(lax.ppermute(sides[:, :, f * 512:(f + 1) * 512], 'orb', ring))  10.5 us
    ppermute x3, starting transfers between devices, shards(): sides.append(lax.ppermute(blocks[e], 'lat', ring))  9.71 us
    ppermute x1, starting transfers between devices, shards(): came = lax.ppermute(sent, 'ord', [(0, 1), (1, 0)])  7.17 us
    pallas_call x1, Pallas kernels, shards(): normals = cross_call(place, turned, other_panel, minus, same)  6.97 us
    ppermute x1, starting transfers between devices, shards(): other_panel = lax.ppermute(own_panel, 'ord', [(0, 1), (1, 0)])  6.32 us
  transfers between devices with their start and end apart: 9, of which 3 were waited for; matrix products, arithmetic and copies ran while one was open for 4% of the time, Pallas kernels for 16%

commit v1 on v0

--- a/solution.py
+++ b/solution.py
@@ -79,26 +79,6 @@
         out[:, q * 256 : (q + 1) * 256] = placed[q * 64 : (q + 1) * 64]
 
 
-def gather_kernel(place, sat, coef_out, sent, kept):
-    y, p = place[1], place[3]
-    gram = jnp.zeros((256, 256), F32)
-    for c in range(8):
-        block = sat[:, c * 256 : (c + 1) * 256]
-        gram = gram + dot(block, block, ((0,), (0,)))
-    kept[...] = jnp.where(p == 0, gram[:128], gram[128:])
-    sent[...] = jnp.where(p == 0, gram[128:], gram[:128])
-    index = iota((64, 1024), 0)
-    source = (index & 60) + ((y - index) & 3)
-    mine = source == (iota((64, 1024), 1) >> 4)
-    spread = ((iota((16, 1024), 1) & 15) == iota((16, 1024), 0)).astype(F32).astype(BF16)
-    lines = []
-    for c in range(4):
-        wide = dot(sat[:, 2048 + c * 16 : 2048 + (c + 1) * 16], spread, ((1,), (0,)))
-        lines.append(jnp.sum(jnp.where(mine, wide, 0.0), axis=0, keepdims=True))
-    lines.append(jnp.zeros((4, 1024), F32))
-    coef_out[...] = jnp.concatenate(lines, axis=0).astype(BF16)
-
-
 def weight_kernel(weight, plus_out, minus_out):
     plus = weight[0:1] + weight[1:2]
     minus = weight[0:1] - weight[1:2]
@@ -136,19 +116,44 @@
     out[:, 1, :] = jnp.where(p == 0, cross, same_now)
 
 
+def pack_kernel(*refs):
+    out = refs[-1]
+    at = 0
+    for ref in refs[:-1]:
+        width = ref.shape[2]
+        out[:, :, at : at + width] = ref[...]
+        at += width
+
+
 def right_kernel(place, coef, turned, right):
-    p, first, order = place[3], place[4], place[5]
-    half = turned.shape[0]
-    product = dot(coef[...], turned[...], ((1,), (1,)))
+    y, p, first, order = place[1], place[3], place[4], place[5]
+    half, row_all = turned.shape
+    index = iota((64, row_all), 0)
+    source = (index & 60) + ((y - index) & 3)
+    mine = source == (iota((64, row_all), 1) >> 4)
+    spread = ((iota((16, row_all), 1) & 15) == iota((16, row_all), 0)).astype(F32).astype(BF16)
+    lines = []
+    for c in range(4):
+        wide = dot(coef[:, c * 16 : (c + 1) * 16], spread, ((1,), (0,)))
+        lines.append(jnp.sum(jnp.where(mine, wide, 0.0), axis=0, keepdims=True))
+    lines.append(jnp.zeros((4, row_all), F32))
+    terms = jnp.concatenate(lines, axis=0).astype(BF16)
+    product = dot(terms, turned[...], ((1,), (1,)))
     sign = 1.0 - 2.0 * ((first + p + order + iota((1, half), 1) * 2) & 1).astype(F32)
     right[0] = product[0:1] + sign * product[1:2]
     right[1] = product[2:3] + sign * product[3:4]
 
 
-def add_kernel(place, kept, came, normals, out):
+def add_kernel(place, sat_own, sat_other, normals, out):
     p, first = place[3], place[4]
+    parts = []
+    for sat in (sat_own, sat_other):
+        flat = sat[...].reshape(64, sat.shape[2])
+        parts += [flat[:, c * 256 : (c + 1) * 256] for c in range(8)]
+    block = jnp.concatenate(parts, axis=0)
+    own = jnp.where(p == 0, block[:, :128], block[:, 128:])
+    gram = dot(own, block, ((0,), (0,)))
     live_left = (first + 2 * iota((128, 128), 0) + p <= LMAX).astype(F32)
-    gram = kept[...] + came[...]
     for q in range(2):
         live_top = (first + 2 * iota((128, 128), 1) + q <= LMAX).astype(F32)
         add = gram[:, q * 128 : (q + 1) * 128] * (live_left * live_top)
@@ -209,12 +214,20 @@
     for f in (1, 2, 3):
         ring = [(i, (i + f) % 4) for i in range(4)]
         groups.append(lax.ppermute(sides[:, :, f * 512 : (f + 1) * 512], "orb", ring))
-    packed = jnp.concatenate(groups + [sides[:, :, 2048:]], axis=2)
+    groups.append(sides[:, :, 2048:])
+    pack = pl.pallas_call(
+        pack_kernel,
+        out_shape=jax.ShapeDtypeStruct((16, 4, width), BF16),
+        in_specs=[whole()] * 5,
+        out_specs=whole(),
+        name="pack",
+    )
+    packed = pack(*groups)
     columns = [[a * 4 + b for a in range(16)] for b in range(4)]
-    packed = lax.all_to_all(
+    sat_own = lax.all_to_all(
         packed, "lat", split_axis=0, concat_axis=0, axis_index_groups=columns, tiled=True
     )
-    packed = packed.reshape(64, width)
+    sat_other = lax.ppermute(sat_own, "ord", [(0, 1), (1, 0)])
 
     own_panel = arrived.reshape(row_all, half)
     other_panel = lax.ppermute(own_panel, "ord", [(0, 1), (1, 0)])
@@ -246,36 +259,25 @@
     )
     normals = cross_call(place, turned, other_panel, minus, same)
 
-    coef, sent, kept = pl.pallas_call(
-        gather_kernel,
-        out_shape=(
-            jax.ShapeDtypeStruct((8, row_all), BF16),
-            jax.ShapeDtypeStruct((128, 256), F32),
-            jax.ShapeDtypeStruct((128, 256), F32),
-        ),
-        in_specs=[smem, whole()],
-        out_specs=(whole(),) * 3,
-        name="gather",
-    )(place, packed)
-    came = lax.ppermute(sent, "ord", [(0, 1), (1, 0)])
-    right = pl.pallas_call(
+    right_call = pl.pallas_call(
         right_kernel,
         out_shape=jax.ShapeDtypeStruct((2, 1, half), F32),
         in_specs=[smem] + [whole()] * 2,
         out_specs=whole(),
         name="right",
-    )(place, coef, turned)
+    )
+    right = right_call(place, sat_own.reshape(64, width)[:, 2048:], turned)
     corner = pl.BlockSpec((128, 2, 128), lambda i: (0, 0, 0))
-    gram_spec = pl.BlockSpec((128, 256), lambda i: (0, 0))
+    sat_spec = pl.BlockSpec((16, 4, width), lambda i: (0, 0, 0))
     normals = pl.pallas_call(
         add_kernel,
         grid=(1,),
         out_shape=jax.ShapeDtypeStruct((half, 2, half), F32),
-        in_specs=[smem, gram_spec, gram_spec, corner],
+        in_specs=[smem, sat_spec, sat_spec, corner],
         out_specs=corner,
         input_output_aliases={3: 0},
         name="add",
-    )(place, kept, came, normals)
+    )(place, sat_own, sat_other, normals)
     return (normals[None, None, None], right[None, None])
 
 

time: 136 us -> 132 us (0.971)
  blocking collectives: 17.2 us -> 0 us
  starting transfers between devices: 53 us -> 59.4 us
  waiting for transfers between devices: 33.9 us -> 37.3 us
  local copies, waits for them, and re-layouts: 7.04 us -> 8.62 us
    all_to_all x1 -> x0, blocking collectives: 17.2 us -> none  [shards(): lax.all_to_all(packed, 'lat', split_axis=0, concat_axis=0, axis_index_gro...]
    all_to_all x0 -> x1, waiting for transfers between devices: none -> 8.72 us  [shards(): lax.all_to_all(packed, 'lat', split_axis=0, concat_axis=0, axis_index_gro...]
    all_to_all x1, waiting for transfers between devices: 30.7 us -> 24.5 us  [shards(): lax.all_to_all(panel, 'lat', split_axis=1, concat_axis=2, tiled=True)]
    all_to_all x0 -> x1, starting transfers between devices: none -> 5.72 us  [shards(): lax.all_to_all(packed, 'lat', split_axis=0, concat_axis=0, axis_index_gro...]
    ppermute x1, starting transfers between devices: 7.17 us -> 9.38 us  [shards(): sat_other = lax.ppermute(sat_own, 'ord', [(0, 1), (1, 0)])]
    ppermute x1, starting transfers between devices: 6.32 us -> 4.15 us  [shards(): other_panel = lax.ppermute(own_panel, 'ord', [(0, 1), (1, 0)])]
    ppermute x3, waiting for transfers between devices: 0.01 us -> 1.85 us  [shards(): groups.append(lax.ppermute(sides[:, :, f * 512:(f + 1) * 512], 'orb', ring))]
  transfers between devices with their start and end apart: 9 -> 10, of which waited for: 3 -> 4; matrix products, arithmetic and copies ran while one was open for 4% -> 6% of each run, Pallas kernels for 16% -> 16%
where the time goes in v1:
time: 132 us; the launch traced here: 131 us
  starting transfers between devices  59.4 us (45%)
  waiting for transfers between devices  37.3 us (28%)
  Pallas kernels  22.9 us (17%)
  local copies, waits for them, and re-layouts  8.62 us (7%)
  between operations  1.47 us (1%)
    all_to_all x1, waiting for transfers between devices, shards(): lax.all_to_all(panel, 'lat', split_axis=1, concat_axis=2, tiled=True)  24.5 us
    all_to_all x1, starting transfers between devices, shards(): lax.all_to_all(panel, 'lat', split_axis=1, concat_axis=2, tiled=True)  19.3 us
    ppermute x3, starting transfers between devices, shards(): groups.append(lax.ppermute(sides[:, :, f * 512:(f + 1) * 512], 'orb', ring))  10.5 us
    ppermute x3, starting transfers between devices, shards(): sides.append(lax.ppermute(blocks[e], 'lat', ring))  10.3 us
    ppermute x1, starting transfers between devices, shards(): sat_other = lax.ppermute(sat_own, 'ord', [(0, 1), (1, 0)])  9.38 us
    all_to_all x1, waiting for transfers between devices, shards(): lax.all_to_all(packed, 'lat', split_axis=0, concat_axis=0, axis_index_gro...  8.72 us
    pallas_call x1, Pallas kernels, shards(): normals = cross_call(place, turned, other_panel, minus, same)  6.99 us
    all_to_all x1, starting transfers between devices, shards(): lax.all_to_all(packed, 'lat', split_axis=0, concat_axis=0, axis_index_gro...  5.72 us
  transfers between devices with their start and end apart: 10, of which 4 were waited for; matrix products, arithmetic and copies ran while one was open for 6% of the time, Pallas kernels for 16%

profile of v1, /device:TPU:1, one launch (start us, length us, event | category | flops | bytes accessed | tf_op | source)
XLA Modules:
  0.0 131.0 jit_solution(7828832521841485731)
XLA Ops:
  0.6 0.0 copy-start.7
  0.6 19.3 %all-to-all-start.1 = ((bf16[1,64,16,1,640]{4,2,3,0,1:T(8,128)(2,1)}), bf16[1,64,16,1,640]{4,2,3,0,1:T(8,128)(2,1)S(1)}, u32[]{:S(2)}, u32[]{:S(2)}) async-start(bf16[1,64,16,1,640]{4,2,3,0,1:T(8,128)(2,1)} %bitcast.20), calls=%async_computation.1 | async-start | bytes 2621440 | tf_op jit(solution)/shard_map/all_to_all | solution.py:177
  20.6 0.8 constant_dynamic-slice_fusion
  21.4 0.7 reshape.34.weight
  22.0 0.0 copy-done.7
  22.0 0.6 constant_dynamic-slice_fusion.1
  22.7 1.3 stack.31.place
  24.0 3.7 %prepare.1 = bf16[64,2176]{1,0:T(8,128)(2,1)} custom-call(s32[6]{0:T(128)} %stack.31.place, bf16[2,16,4320]{2,1,0:T(8,128)(2,1)} %anomaly.1, f32[32,1]{1,0:T(8,128)} %reshape.34.weight, s32[1,64]{1,0:T(1,128)} %order.1, bf16[256,256]{1,0:T(8,128)(2,1)} %rows.1, s32[1,256]{1,0:T(1,128)} %bitcast.25), custom_call_target="tpu_custom_call" | custom-call | tf_op jit(solution)/shard_map/prepare/pallas_call | solution.py:182
  27.6 1.0 slice_bitcast_fusion
  28.7 2.9 %collective-permute-start = (bf16[16,2176]{1,0:T(8,128)(2,1)S(1)}, bf16[16,2176]{1,0:T(8,128)(2,1)S(1)}, u32[]{:S(2)}, u32[]{:S(2)}) collective-permute-start(bf16[16,2176]{1,0:T(8,128)(2,1)S(1)} %get-tuple-element.17), channel_id=1, source_target_pairs={{0,8},{8,16},{16,24},{24,0},{32,40},{40,48},{48,56},{56,32},{64,72... | collective-permute-start | bytes 208904 | tf_op jit(solution)/shard_map/ppermute | solution.py:211
  31.6 4.3 %collective-permute-start.1 = (bf16[16,2176]{1,0:T(8,128)(2,1)S(1)}, bf16[16,2176]{1,0:T(8,128)(2,1)S(1)}, u32[]{:S(2)}, u32[]{:S(2)}) collective-permute-start(bf16[16,2176]{1,0:T(8,128)(2,1)S(1)} %get-tuple-element.16), channel_id=1, source_target_pairs={{0,16},{8,24},{16,0},{24,8},{32,48},{40,56},{48,32},{56,40},{64,80... | collective-permute-start | bytes 208904 | tf_op jit(solution)/shard_map/ppermute | solution.py:211
  35.9 3.1 %collective-permute-start.2 = (bf16[16,2176]{1,0:T(8,128)(2,1)S(1)}, bf16[16,2176]{1,0:T(8,128)(2,1)S(1)}, u32[]{:S(2)}, u32[]{:S(2)}) collective-permute-start(bf16[16,2176]{1,0:T(8,128)(2,1)S(1)} %get-tuple-element.15), channel_id=1, source_target_pairs={{0,24},{8,0},{16,8},{24,16},{32,56},{40,32},{48,40},{56,48},{64,88... | collective-permute-start | bytes 208904 | tf_op jit(solution)/shard_map/ppermute | solution.py:211
  39.0 0.1 copy.17
  39.1 0.0 collective-permute-done
  39.1 0.1 copy.18
  39.2 0.0 collective-permute-done.1
  39.3 0.1 copy.19
  39.4 2.2 %collective-permute-done.2 = bf16[16,2176]{1,0:T(8,128)(2,1)S(1)} collective-permute-done((bf16[16,2176]{1,0:T(8,128)(2,1)S(1)}, bf16[16,2176]{1,0:T(8,128)(2,1)S(1)}, u32[]{:S(2)}, u32[]{:S(2)}) %collective-permute-start.2) | collective-permute-done | bytes 69664 | tf_op jit(solution)/shard_map/ppermute | solution.py:211
  41.6 0.1 copy.20
  41.7 0.7 pad_maximum_fusion
  42.4 0.7 fusion
  43.1 3.1 %collective-permute-start.3 = (bf16[16,4,512]{2,1,0:T(4,128)(2,1)S(1)}, bf16[16,4,512]{2,1,0:T(4,128)(2,1)S(1)}, u32[]{:S(2)}, u32[]{:S(2)}) collective-permute-start(bf16[16,4,512]{2,1,0:T(4,128)(2,1)S(1)} %get-tuple-element.12), channel_id=1, source_target_pairs={{0,1},{1,2},{2,3},{3,0},{4,5},{5,6},{6,7},{7,4},{8,9},{9,10},{10,1... | collective-permute-start | bytes 196616 | tf_op jit(solution)/shard_map/ppermute | solution.py:216
  46.2 4.3 %collective-permute-start.4 = (bf16[16,4,512]{2,1,0:T(4,128)(2,1)S(1)}, bf16[16,4,512]{2,1,0:T(4,128)(2,1)S(1)}, u32[]{:S(2)}, u32[]{:S(2)}) collective-permute-start(bf16[16,4,512]{2,1,0:T(4,128)(2,1)S(1)} %get-tuple-element.11), channel_id=1, source_target_pairs={{0,2},{1,3},{2,0},{3,1},{4,6},{5,7},{6,4},{7,5},{8,10},{9,11},{10,... | collective-permute-start | bytes 196616 | tf_op jit(solution)/shard_map/ppermute | solution.py:216
  50.6 3.1 %collective-permute-start.5 = (bf16[16,4,512]{2,1,0:T(4,128)(2,1)S(1)}, bf16[16,4,512]{2,1,0:T(4,128)(2,1)S(1)}, u32[]{:S(2)}, u32[]{:S(2)}) collective-permute-start(bf16[16,4,512]{2,1,0:T(4,128)(2,1)S(1)} %get-tuple-element.10), channel_id=1, source_target_pairs={{0,3},{1,0},{2,1},{3,2},{4,7},{5,4},{6,5},{7,6},{8,11},{9,8},{10,9... | collective-permute-start | bytes 196616 | tf_op jit(solution)/shard_map/ppermute | solution.py:216
  53.7 0.6 pad_maximum_fusion.1.refs_4_
  54.3 0.0 collective-permute-done.3.refs_1_
  54.3 0.0 copy-start.4
  54.3 0.0 collective-permute-done.4.refs_2_
  54.3 0.0 copy-start.5
  54.3 1.8 %collective-permute-done.5.refs_3_ = bf16[16,4,512]{2,1,0:T(4,128)(2,1)S(1)} collective-permute-done((bf16[16,4,512]{2,1,0:T(4,128)(2,1)S(1)}, bf16[16,4,512]{2,1,0:T(4,128)(2,1)S(1)}, u32[]{:S(2)}, u32[]{:S(2)}) %collective-permute-start.5) | collective-permute-done | bytes 65568 | tf_op jit(solution)/shard_map/ppermute | solution.py:216
  56.2 0.0 copy-start.6
  56.2 0.0 copy-done.4
  56.2 0.0 copy-done.5
  56.2 0.6 copy-done.6
  56.8 1.7 %pack.1 = bf16[16,4,2176]{2,1,0:T(4,128)(2,1)} custom-call(bf16[16,4,512]{2,1,0:T(4,128)(2,1)} %get-tuple-element.13.refs_0_, bf16[16,4,512]{2,1,0:T(4,128)(2,1)} %copy-done.4, bf16[16,4,512]{2,1,0:T(4,128)(2,1)} %copy-done.5, bf16[16,4,512]{2,1,0:T(4,128)(2,1)} %copy-done.6, bf16[16,4,128]{2,1,0:T(4,128)(2,1)} %pad_maximum_fusion.1.refs_4_), custom_call_target="tpu_custom_call" | custom-call | tf_op jit(solution)/shard_map/pack/pallas_call | solution.py:225
  58.5 24.5 %all-to-all-done.1 = bf16[1,64,16,1,640]{4,2,3,0,1:T(8,128)(2,1)S(1)} async-done(((bf16[1,64,16,1,640]{4,2,3,0,1:T(8,128)(2,1)}), bf16[1,64,16,1,640]{4,2,3,0,1:T(8,128)(2,1)S(1)}, u32[]{:S(2)}, u32[]{:S(2)}) %all-to-all-start.1) | async-done | bytes 1310752 | tf_op jit(solution)/shard_map/all_to_all | solution.py:177
  83.0 0.0 copy-start
  83.0 5.7 %all-to-all-start = ((bf16[16,4,2176]{2,1,0:T(4,128)(2,1)}), bf16[16,4,2176]{2,1,0:T(4,128)(2,1)S(1)}, u32[]{:S(2)}, u32[]{:S(2)}) async-start(bf16[16,4,2176]{2,1,0:T(4,128)(2,1)} %pack.1), calls=%async_computation | async-start | bytes 557056 | tf_op jit(solution)/shard_map/all_to_all | solution.py:227
  88.7 4.1 %collective-permute-start.7 = (bf16[1024,640]{1,0:T(8,128)(2,1)S(1)}, bf16[1024,640]{1,0:T(8,128)(2,1)S(1)}, u32[]{:S(2)}, u32[]{:S(2)}) collective-permute-start(bf16[1024,640]{1,0:T(8,128)(2,1)S(1)} %bitcast.18), channel_id=1, source_target_pairs={{0,4},{4,0},{1,5},{5,1},{2,6},{6,2},{3,7},{7,3},{8,12},{12,8},{9,1... | collective-permute-start | bytes 3932168 | tf_op jit(solution)/shard_map/ppermute | solution.py:233
  92.9 8.7 %all-to-all-done.sat_own = bf16[16,4,2176]{2,1,0:T(4,128)(2,1)S(1)} async-done(((bf16[16,4,2176]{2,1,0:T(4,128)(2,1)}), bf16[16,4,2176]{2,1,0:T(4,128)(2,1)S(1)}, u32[]{:S(2)}, u32[]{:S(2)}) %all-to-all-start) | async-done | bytes 278560 | tf_op jit(solution)/shard_map/all_to_all | solution.py:227
  101.6 0.0 copy-start.1
  101.6 9.4 %collective-permute-start.6 = (bf16[16,4,2176]{2,1,0:T(4,128)(2,1)S(1)}, bf16[16,4,2176]{2,1,0:T(4,128)(2,1)S(1)}, u32[]{:S(2)}, u32[]{:S(2)}) collective-permute-start(bf16[16,4,2176]{2,1,0:T(4,128)(2,1)S(1)} %all-to-all-done.sat_own), channel_id=1, source_target_pairs={{0,4},{4,0},{1,5},{5,1},{2,6},{6,2},{3,7},{7,3},{8,12},{12,8},{9,1... | collective-permute-start | bytes 835592 | tf_op jit(solution)/shard_map/ppermute | solution.py:230
  111.0 1.9 %weights.1 = (f32[1024,128]{1,0:T(8,128)}, f32[1024,128]{1,0:T(8,128)}) custom-call(f32[2,1024]{1,0:T(2,128)} %weight.1), custom_call_target="tpu_custom_call" | custom-call | tf_op jit(solution)/shard_map/weights/pallas_call | solution.py:204
  112.9 0.1 reshape.33
  113.0 0.6 slice.52.coef
  113.6 0.0 copy-done
  113.6 3.9 %same.1 = (bf16[640,1024]{1,0:T(8,128)(2,1)}, f32[640,640]{1,0:T(8,128)}) custom-call(s32[6]{0:T(128)} %stack.31.place, bf16[1024,640]{1,0:T(8,128)(2,1)} %bitcast.19, f32[1024,128]{1,0:T(8,128)} %get-tuple-element.6.plus), custom_call_target="tpu_custom_call" | custom-call | tf_op jit(solution)/shard_map/same/pallas_call | solution.py:244
  117.5 2.6 %right.1 = f32[2,1,640]{2,1,0:T(1,128)} custom-call(s32[6]{0:T(128)} %stack.31.place, bf16[64,128]{1,0:T(8,128)(2,1)} %slice.52.coef, bf16[640,1024]{1,0:T(8,128)(2,1)} %get-tuple-element.7.turned), custom_call_target="tpu_custom_call" | custom-call | tf_op jit(solution)/shard_map/right/pallas_call | solution.py:269
  120.1 0.0 copy-done.1
  120.1 0.0 collective-permute-done.7.other
  120.2 0.0 copy-start.2
  120.2 1.1 copy-done.2
  121.2 7.0 %cross.1.normals = f32[640,2,640]{2,1,0:T(2,128)} custom-call(s32[6]{0:T(128)} %stack.31.place, bf16[640,1024]{1,0:T(8,128)(2,1)} %get-tuple-element.7.turned, bf16[1024,640]{1,0:T(8,128)(2,1)} %copy-done.2, f32[1024,128]{1,0:T(8,128)} %get-tuple-element.8.minus, f32[640,640]{1,0:T(8,128)} %get-tuple-element.9.same), custom_call_target="tpu_custom_call" | custom-call | tf_op jit(solution)/shard_map/cross/pallas_call | solution.py:260
  128.2 0.0 collective-permute-done.6.sat_other
  128.2 0.0 copy-start.3
  128.2 0.7 copy-done.3
  128.9 2.1 %add.15 = f32[640,2,640]{2,1,0:T(2,128)} custom-call(s32[6]{0:T(128)} %stack.31.place, bf16[16,4,2176]{2,1,0:T(4,128)(2,1)} %copy-done.1, bf16[16,4,2176]{2,1,0:T(4,128)(2,1)} %copy-done.3, f32[640,2,640]{2,1,0:T(2,128)} %cross.1.normals), custom_call_target="tpu_custom_call", output_to_operand_aliasing={{}: (3, {})} | custom-call | tf_op jit(solution)/shard_map/add/pallas_call | solution.py:272
Async XLA Ops:
  0.6 21.4 %copy-start.7 = (s32[1,64]{1,0:T(1,128)S(1)}, s32[1,64]{1,0:T(1,128)}, u32[]{:S(2)}) copy-start(s32[1,64]{1,0:T(1,128)} %order.1) | copy-start | bytes 772
  0.6 82.3 %all-to-all-start.1 = ((bf16[1,64,16,1,640]{4,2,3,0,1:T(8,128)(2,1)}), bf16[1,64,16,1,640]{4,2,3,0,1:T(8,128)(2,1)S(1)}, u32[]{:S(2)}, u32[]{:S(2)}) async-start(bf16[1,64,16,1,640]{4,2,3,0,1:T(8,128)(2,1)} %bitcast.20), calls=%async_computation.1 | async-start | bytes 2621440 | tf_op jit(solution)/shard_map/all_to_all | solution.py:177
  28.7 10.5 %collective-permute-start = (bf16[16,2176]{1,0:T(8,128)(2,1)S(1)}, bf16[16,2176]{1,0:T(8,128)(2,1)S(1)}, u32[]{:S(2)}, u32[]{:S(2)}) collective-permute-start(bf16[16,2176]{1,0:T(8,128)(2,1)S(1)} %get-tuple-element.17), channel_id=1, source_target_pairs={{0,8},{8,16},{16,24},{24,0},{32,40},{40,48},{48,56},{56,32},{64,72... | collective-permute-start | bytes 208904 | tf_op jit(solution)/shard_map/ppermute | solution.py:211
  31.6 7.7 %collective-permute-start.1 = (bf16[16,2176]{1,0:T(8,128)(2,1)S(1)}, bf16[16,2176]{1,0:T(8,128)(2,1)S(1)}, u32[]{:S(2)}, u32[]{:S(2)}) collective-permute-start(bf16[16,2176]{1,0:T(8,128)(2,1)S(1)} %get-tuple-element.16), channel_id=1, source_target_pairs={{0,16},{8,24},{16,0},{24,8},{32,48},{40,56},{48,32},{56,40},{64,80... | collective-permute-start | bytes 208904 | tf_op jit(solution)/shard_map/ppermute | solution.py:211
  35.9 5.7 %collective-permute-start.2 = (bf16[16,2176]{1,0:T(8,128)(2,1)S(1)}, bf16[16,2176]{1,0:T(8,128)(2,1)S(1)}, u32[]{:S(2)}, u32[]{:S(2)}) collective-permute-start(bf16[16,2176]{1,0:T(8,128)(2,1)S(1)} %get-tuple-element.15), channel_id=1, source_target_pairs={{0,24},{8,0},{16,8},{24,16},{32,56},{40,32},{48,40},{56,48},{64,88... | collective-permute-start | bytes 208904 | tf_op jit(solution)/shard_map/ppermute | solution.py:211
  43.1 11.2 %collective-permute-start.3 = (bf16[16,4,512]{2,1,0:T(4,128)(2,1)S(1)}, bf16[16,4,512]{2,1,0:T(4,128)(2,1)S(1)}, u32[]{:S(2)}, u32[]{:S(2)}) collective-permute-start(bf16[16,4,512]{2,1,0:T(4,128)(2,1)S(1)} %get-tuple-element.12), channel_id=1, source_target_pairs={{0,1},{1,2},{2,3},{3,0},{4,5},{5,6},{6,7},{7,4},{8,9},{9,10},{10,1... | collective-permute-start | bytes 196616 | tf_op jit(solution)/shard_map/ppermute | solution.py:216
  46.2 8.1 %collective-permute-start.4 = (bf16[16,4,512]{2,1,0:T(4,128)(2,1)S(1)}, bf16[16,4,512]{2,1,0:T(4,128)(2,1)S(1)}, u32[]{:S(2)}, u32[]{:S(2)}) collective-permute-start(bf16[16,4,512]{2,1,0:T(4,128)(2,1)S(1)} %get-tuple-element.11), channel_id=1, source_target_pairs={{0,2},{1,3},{2,0},{3,1},{4,6},{5,7},{6,4},{7,5},{8,10},{9,11},{10,... | collective-permute-start | bytes 196616 | tf_op jit(solution)/shard_map/ppermute | solution.py:216
  50.6 5.6 %collective-permute-start.5 = (bf16[16,4,512]{2,1,0:T(4,128)(2,1)S(1)}, bf16[16,4,512]{2,1,0:T(4,128)(2,1)S(1)}, u32[]{:S(2)}, u32[]{:S(2)}) collective-permute-start(bf16[16,4,512]{2,1,0:T(4,128)(2,1)S(1)} %get-tuple-element.10), channel_id=1, source_target_pairs={{0,3},{1,0},{2,1},{3,2},{4,7},{5,4},{6,5},{7,6},{8,11},{9,8},{10,9... | collective-permute-start | bytes 196616 | tf_op jit(solution)/shard_map/ppermute | solution.py:216
  54.3 1.9 %copy-start.4 = (bf16[16,4,512]{2,1,0:T(4,128)(2,1)}, bf16[16,4,512]{2,1,0:T(4,128)(2,1)S(1)}, u32[]{:S(2)}) copy-start(bf16[16,4,512]{2,1,0:T(4,128)(2,1)S(1)} %collective-permute-done.3.refs_1_) | copy-start | bytes 196612
  54.3 1.9 %copy-start.5 = (bf16[16,4,512]{2,1,0:T(4,128)(2,1)}, bf16[16,4,512]{2,1,0:T(4,128)(2,1)S(1)}, u32[]{:S(2)}) copy-start(bf16[16,4,512]{2,1,0:T(4,128)(2,1)S(1)} %collective-permute-done.4.refs_2_) | copy-start | bytes 196612
  56.2 0.6 copy-start.6
  83.0 30.6 %copy-start = (bf16[1,64,16,1,640]{4,2,3,0,1:T(8,128)(2,1)}, bf16[1,64,16,1,640]{4,2,3,0,1:T(8,128)(2,1)S(1)}, u32[]{:S(2)}) copy-start(bf16[1,64,16,1,640]{4,2,3,0,1:T(8,128)(2,1)S(1)} %all-to-all-done.1) | copy-start | bytes 3932164
  83.0 18.6 %all-to-all-start = ((bf16[16,4,2176]{2,1,0:T(4,128)(2,1)}), bf16[16,4,2176]{2,1,0:T(4,128)(2,1)S(1)}, u32[]{:S(2)}, u32[]{:S(2)}) async-start(bf16[16,4,2176]{2,1,0:T(4,128)(2,1)} %pack.1), calls=%async_computation | async-start | bytes 557056 | tf_op jit(solution)/shard_map/all_to_all | solution.py:227
  88.7 31.4 %collective-permute-start.7 = (bf16[1024,640]{1,0:T(8,128)(2,1)S(1)}, bf16[1024,640]{1,0:T(8,128)(2,1)S(1)}, u32[]{:S(2)}, u32[]{:S(2)}) collective-permute-start(bf16[1024,640]{1,0:T(8,128)(2,1)S(1)} %bitcast.18), channel_id=1, source_target_pairs={{0,4},{4,0},{1,5},{5,1},{2,6},{6,2},{3,7},{7,3},{8,12},{12,8},{9,1... | collective-permute-start | bytes 3932168 | tf_op jit(solution)/shard_map/ppermute | solution.py:233
  101.6 18.6 %copy-start.1 = (bf16[16,4,2176]{2,1,0:T(4,128)(2,1)}, bf16[16,4,2176]{2,1,0:T(4,128)(2,1)S(1)}, u32[]{:S(2)}) copy-start(bf16[16,4,2176]{2,1,0:T(4,128)(2,1)S(1)} %all-to-all-done.sat_own) | copy-start | bytes 835588
  101.6 26.6 %collective-permute-start.6 = (bf16[16,4,2176]{2,1,0:T(4,128)(2,1)S(1)}, bf16[16,4,2176]{2,1,0:T(4,128)(2,1)S(1)}, u32[]{:S(2)}, u32[]{:S(2)}) collective-permute-start(bf16[16,4,2176]{2,1,0:T(4,128)(2,1)S(1)} %all-to-all-done.sat_own), channel_id=1, source_target_pairs={{0,4},{4,0},{1,5},{5,1},{2,6},{6,2},{3,7},{7,3},{8,12},{12,8},{9,1... | collective-permute-start | bytes 835592 | tf_op jit(solution)/shard_map/ppermute | solution.py:230
  120.2 1.1 copy-start.2
  128.2 0.7 copy-start.3

commit v2 on v1

--- a/solution.py
+++ b/solution.py
@@ -29,7 +29,7 @@
 
 
 def prepare_kernel(place, anomaly, weight, order, rows, slot, out, table_high, table_low):
-    y, x = place[1], place[2]
+    far, x = place[0], place[2]
     length = anomaly.shape[2]
     order_pair = jnp.concatenate([order[...], order[...]], axis=1).astype(F32)
     fine = turn(iota((STEP, 128), 0).astype(F32) * order_pair, length)
@@ -52,8 +52,7 @@
     at, own = iota((64, 64), 0), iota((64, 64), 1)
 
     def position(slot_in_group):
-        side = ((slot_in_group & 3) - y) & 3
-        return side * 16 + (slot_in_group >> 2)
+        return (((slot_in_group >> 4) - far) & 3) * 16 + (slot_in_group & 15)
 
     pick = (position(own) == at).astype(F32).astype(BF16)
     out[:, 2048:2176] = jnp.concatenate(
@@ -90,46 +89,64 @@
     return (first + 2 * iota((1, half), 1) + parity <= LMAX).astype(F32)
 
 
-def same_kernel(place, own, plus, turned, same):
+def gram_kernel(place, own, other, plus, minus, out, own_here, other_here, scaled, stage, sems):
     p, first = place[3], place[4]
-    half = own.shape[1]
-    wide = own[...].astype(F32) * live_row(first, p, half)
-    turned_now = wide.astype(BF16).T
-    turned[...] = turned_now
-    scale = jnp.concatenate([plus[...]] * (half // 128), axis=1)
-    same[...] = dot(turned_now, (wide * scale).astype(BF16), ((1,), (0,)))
-
-
-def cross_kernel(place, turned, other, minus, same, out, scaled):
-    p, first = place[3], place[4]
-    half = other.shape[1]
-
-    @pl.when(pl.program_id(0) == 0)
-    def _():
-        live_other = live_row(first, 1 - p, half)
-        scale = jnp.concatenate([minus[...]] * (half // 128), axis=1)
-        scaled[...] = (other[...].astype(F32) * live_other * scale).astype(BF16)
-
-    cross = dot(turned[...], scaled[...], ((1,), (0,)))
-    same_now = same[...]
-    out[:, 0, :] = jnp.where(p == 0, same_now, cross)
-    out[:, 1, :] = jnp.where(p == 0, cross, same_now)
+    _, half = own.shape
+    tiles = half // 128
+    fetch = [
+        pltpu.make_async_copy(own, own_here, sems.at[0]),
+        pltpu.make_async_copy(other, other_here, sems.at[1]),
+    ]
+    for copy in fetch:
+        copy.start()
+    scaled_as = ((own_here, plus, p), (other_here, minus, 1 - p))
+    for (here, weight, parity), copy in zip(scaled_as, fetch):
+        copy.wait()
+        live = live_row(first, parity, half)
+        scale = jnp.concatenate([weight[...]] * tiles, axis=1)
+        scaled[:, pl.ds(pl.multiple_of(parity * half, 128), half)] = (
+            here[...].astype(F32) * live * scale
+        ).astype(BF16)
+    live = live_row(first, p, half)
+    sent = []
+    for k, (low, high) in enumerate(((0, 3), (3, tiles))):
+        cols = slice(low * 128, high * 128)
+        left = (own_here[:, cols].astype(F32) * live[:, cols]).astype(BF16).T
+        block = dot(left, scaled[...], ((1,), (0,)))
+        count = (high - low) * 128
+        for q in range(2):
+            for tile in range(tiles):
+                at = q * half + tile * 128
+                where = pl.ds((tile * half + low * 128) * 2 + q, count, stride=2)
+                stage[where, :] = block[:, at : at + 128]
+        pairs = stage.reshape(tiles, half, 2, 128)
+        span = pl.ds(low * 128, count)
+        for tile in range(tiles):
+            copy = pltpu.make_async_copy(
+                pairs.at[tile, span],
+                out.at[span, :, pl.ds(tile * 128, 128)],
+                sems.at[2 + k * tiles + tile],
+            )
+            copy.start()
+            sent.append(copy)
+    for copy in sent:
+        copy.wait()
 
 
 def pack_kernel(*refs):
     out = refs[-1]
     at = 0
     for ref in refs[:-1]:
-        width = ref.shape[2]
-        out[:, :, at : at + width] = ref[...]
+        width = ref.shape[1]
+        out[:, at : at + width] = ref[...]
         at += width
 
 
-def right_kernel(place, coef, turned, right):
-    y, p, first, order = place[1], place[3], place[4], place[5]
-    half, row_all = turned.shape
+def right_kernel(place, coef, own, right):
+    far, p, first, order = place[0], place[3], place[4], place[5]
+    row_all, half = own.shape
     index = iota((64, row_all), 0)
-    source = (index & 60) + ((y - index) & 3)
+    source = ((far - index) & 3) * 16 + (index >> 2)
     mine = source == (iota((64, row_all), 1) >> 4)
     spread = ((iota((16, row_all), 1) & 15) == iota((16, row_all), 0)).astype(F32).astype(BF16)
     lines = []
@@ -138,7 +155,7 @@
         lines.append(jnp.sum(jnp.where(mine, wide, 0.0), axis=0, keepdims=True))
     lines.append(jnp.zeros((4, row_all), F32))
     terms = jnp.concatenate(lines, axis=0).astype(BF16)
-    product = dot(terms, turned[...], ((1,), (1,)))
+    product = dot(terms, own[...], ((1,), (0,))) * live_row(first, p, half)
     sign = 1.0 - 2.0 * ((first + p + order + iota((1, half), 1) * 2) & 1).astype(F32)
     right[0] = product[0:1] + sign * product[1:2]
     right[1] = product[2:3] + sign * product[3:4]
@@ -171,13 +188,13 @@
     row_count = panel.shape[2]
     half = panel.shape[4]
     row_all = row_weight.shape[1]
-    z, y = lat_index // 4, lat_index % 4
+    far = lat_index // 16
     smem = whole(pltpu.SMEM)
 
     arrived = lax.all_to_all(panel, "lat", split_axis=1, concat_axis=2, tiled=True)
 
     own_order = lax.dynamic_slice_in_dim(order_value[0], lat_index, 1, 0)[0]
-    place = jnp.stack([z, y, orb_index, parity, deg_first[0, 0], own_order]).astype(I32)
+    place = jnp.stack([far, lat_index % 16, orb_index, parity, deg_first[0, 0], own_order]).astype(I32)
     local_weight = lax.dynamic_slice_in_dim(row_weight, lat_index * row_count, row_count, 1)
     packed = pl.pallas_call(
         prepare_kernel,
@@ -204,61 +221,52 @@
     plus, minus = weights(row_weight)
 
     width = packed.shape[1]
-    blocks = packed.reshape(4, 16, width)
-    sides = [blocks[0]]
-    for e in (1, 2, 3):
-        ring = [(a * 4 + b, a * 4 + (b + e) % 4) for a in range(16) for b in range(4)]
-        sides.append(lax.ppermute(blocks[e], "lat", ring))
-    sides = jnp.stack(sides, axis=1)
-    groups = [sides[:, :, :512]]
+    groups = [packed[:, :512]]
     for f in (1, 2, 3):
         ring = [(i, (i + f) % 4) for i in range(4)]
-        groups.append(lax.ppermute(sides[:, :, f * 512 : (f + 1) * 512], "orb", ring))
-    groups.append(sides[:, :, 2048:])
+        groups.append(lax.ppermute(packed[:, f * 512 : (f + 1) * 512], "orb", ring))
+    groups.append(packed[:, 2048:])
     pack = pl.pallas_call(
         pack_kernel,
-        out_shape=jax.ShapeDtypeStruct((16, 4, width), BF16),
+        out_shape=jax.ShapeDtypeStruct((64, width), BF16),
         in_specs=[whole()] * 5,
         out_specs=whole(),
         name="pack",
     )
     packed = pack(*groups)
-    columns = [[a * 4 + b for a in range(16)] for b in range(4)]
+    fars = [packed[:16]]
+    for h in (1, 2, 3):
+        ring = [(i, (i + 16 * h) % 64) for i in range(64)]
+        fars.append(lax.ppermute(packed[16 * h : 16 * (h + 1)], "lat", ring))
+    blocks = [[16 * g + j for j in range(16)] for g in range(4)]
     sat_own = lax.all_to_all(
-        packed, "lat", split_axis=0, concat_axis=0, axis_index_groups=columns, tiled=True
+        jnp.stack(fars, axis=1),
+        "lat",
+        split_axis=0,
+        concat_axis=0,
+        axis_index_groups=blocks,
+        tiled=True,
     )
     sat_other = lax.ppermute(sat_own, "ord", [(0, 1), (1, 0)])
 
     own_panel = arrived.reshape(row_all, half)
     other_panel = lax.ppermute(own_panel, "ord", [(0, 1), (1, 0)])
-    same_call = pl.pallas_call(
-        same_kernel,
-        out_shape=(
-            jax.ShapeDtypeStruct((half, row_all), BF16),
-            jax.ShapeDtypeStruct((half, half), F32),
-        ),
-        in_specs=[smem] + [whole()] * 2,
-        out_specs=(whole(),) * 2,
-        name="same",
-    )
-    turned, same = same_call(place, own_panel, plus)
-    cross_call = pl.pallas_call(
-        cross_kernel,
-        grid=(half // 128,),
+    lines = half * 2 * (half // 128)
+    gram_call = pl.pallas_call(
+        gram_kernel,
         out_shape=jax.ShapeDtypeStruct((half, 2, half), F32),
-        in_specs=[
-            smem,
-            pl.BlockSpec((128, row_all), lambda i: (i, 0)),
-            pl.BlockSpec((row_all, half), lambda i: (0, 0)),
-            pl.BlockSpec((row_all, 128), lambda i: (0, 0)),
-            pl.BlockSpec((128, half), lambda i: (i, 0)),
+        in_specs=[smem, whole(pl.ANY), whole(pl.ANY), whole(), whole()],
+        out_specs=whole(pl.ANY),
+        scratch_shapes=[
+            pltpu.VMEM((row_all, half), BF16),
+            pltpu.VMEM((row_all, half), BF16),
+            pltpu.VMEM((row_all, 2 * half), BF16),
+            pltpu.VMEM((lines, 128), F32),
+            pltpu.SemaphoreType.DMA((2 + 2 * (half // 128),)),
         ],
-        out_specs=pl.BlockSpec((128, 2, half), lambda i: (i, 0, 0)),
-        scratch_shapes=[pltpu.VMEM((row_all, half), BF16)],
-        name="cross",
-    )
-    normals = cross_call(place, turned, other_panel, minus, same)
-
+        name="gram",
+    )
+    normals = gram_call(place, own_panel, other_panel, plus, minus)
     right_call = pl.pallas_call(
         right_kernel,
         out_shape=jax.ShapeDtypeStruct((2, 1, half), F32),
@@ -266,7 +274,7 @@
         out_specs=whole(),
         name="right",
     )
-    right = right_call(place, sat_own.reshape(64, width)[:, 2048:], turned)
+    right = right_call(place, sat_own[:, :, 2048:].reshape(64, 128), own_panel)
     corner = pl.BlockSpec((128, 2, 128), lambda i: (0, 0, 0))
     sat_spec = pl.BlockSpec((16, 4, width), lambda i: (0, 0, 0))
     normals = pl.pallas_call(

time: 132 us -> 134 us (1.015)
  starting transfers between devices: 59.4 us -> 71.9 us
  waiting for transfers between devices: 37.3 us -> 29.2 us
  Pallas kernels: 22.9 us -> 18.4 us
  local copies, waits for them, and re-layouts: 8.62 us -> 10.6 us
    all_to_all x1, waiting for transfers between devices: 24.5 us -> 0.01 us  [shards(): lax.all_to_all(panel, 'lat', split_axis=1, concat_axis=2, tiled=True)]
    ppermute x6, waiting for transfers between devices: 4.11 us -> 24.8 us  [the longest x3 21.7 us: shards(): fars.append(lax.ppermute(packed[16 * h:16 * (h + 1)], 'lat', ring))]
    ppermute x6, starting transfers between devices: 20.9 us -> 30.5 us  [the longest x3 21.2 us: shards(): fars.append(lax.ppermute(packed[16 * h:16 * (h + 1)], 'lat', ring))]
    all_to_all x1, starting transfers between devices: 5.72 us -> 11.8 us  [shards(): lax.all_to_all(jnp.stack(fars, axis=1), 'lat', split_axis=0, concat_axis=...]
    pallas_call x3 -> x2, Pallas kernels: 13.5 us -> 9.18 us  [the longest x1 6.7 us: shards(): normals = gram_call(place, own_panel, other_panel, plus, minus)]
    all_to_all x1, waiting for transfers between devices: 8.72 us -> 4.4 us  [shards(): lax.all_to_all(jnp.stack(fars, axis=1), 'lat', split_axis=0, concat_axis=...]
    ppermute x1, starting transfers between devices: 9.38 us -> 5.69 us  [shards(): sat_other = lax.ppermute(sat_own, 'ord', [(0, 1), (1, 0)])]
    slice x2 -> x3, local copies, waits for them, and re-layouts: 1.32 us -> 3.5 us  [the longest x1 1.58 us: shards(): groups.append(lax.ppermute(packed[:, f * 512:(f + 1) * 512], 'orb', ring))]
  transfers between devices with their start and end apart: 10 -> 10, of which waited for: 4 -> 5; matrix products, arithmetic and copies ran while one was open for 6% -> 7% of each run, Pallas kernels for 16% -> 12%
where the time goes in v2:
time: 134 us; the launch traced here: 133 us
  starting transfers between devices  71.9 us (54%)
  waiting for transfers between devices  29.2 us (22%)
  Pallas kernels  18.4 us (14%)
  local copies, waits for them, and re-layouts  10.6 us (8%)
  between operations  1.47 us (1%)
  other arithmetic  1.36 us (1%)
    ppermute x3, waiting for transfers between devices, shards(): fars.append(lax.ppermute(packed[16 * h:16 * (h + 1)], 'lat', ring))  21.7 us
    ppermute x3, starting transfers between devices, shards(): fars.append(lax.ppermute(packed[16 * h:16 * (h + 1)], 'lat', ring))  21.2 us
    all_to_all x1, starting transfers between devices, shards(): lax.all_to_all(panel, 'lat', split_axis=1, concat_axis=2, tiled=True)  19.3 us
    all_to_all x1, starting transfers between devices, shards(): lax.all_to_all(jnp.stack(fars, axis=1), 'lat', split_axis=0, concat_axis=...  11.8 us
    ppermute x3, starting transfers between devices, shards(): groups.append(lax.ppermute(packed[:, f * 512:(f + 1) * 512], 'orb', ring))  9.32 us
    pallas_call x1, Pallas kernels, shards(): normals = gram_call(place, own_panel, other_panel, plus, minus)  6.7 us
    ppermute x1, starting transfers between devices, shards(): sat_other = lax.ppermute(sat_own, 'ord', [(0, 1), (1, 0)])  5.69 us
    ppermute x1, starting transfers between devices, shards(): other_panel = lax.ppermute(own_panel, 'ord', [(0, 1), (1, 0)])  4.65 us
  transfers between devices with their start and end apart: 10, of which 5 were waited for; matrix products, arithmetic and copies ran while one was open for 7% of the time, Pallas kernels for 12%

profile of v2, /device:TPU:1, one launch (start us, length us, event | category | flops | bytes accessed | tf_op | source)
XLA Modules:
  0.0 133.0 jit_solution(4252284683880448798)
XLA Ops:
  0.6 0.0 copy-start.7
  0.6 19.3 %all-to-all-start.1 = ((bf16[1,64,16,1,640]{4,2,3,0,1:T(8,128)(2,1)}), bf16[1,64,16,1,640]{4,2,3,0,1:T(8,128)(2,1)S(1)}, u32[]{:S(2)}, u32[]{:S(2)}) async-start(bf16[1,64,16,1,640]{4,2,3,0,1:T(8,128)(2,1)} %bitcast.22), calls=%async_computation.1 | async-start | bytes 2621440 | tf_op jit(solution)/shard_map/all_to_all | solution.py:194
  20.6 0.8 constant_dynamic-slice_fusion
  21.4 0.7 reshape.25.weight
  22.0 0.0 copy-done.7
  22.0 0.6 constant_dynamic-slice_fusion.1
  22.6 1.2 stack.34.place
  23.8 3.7 %prepare.1 = bf16[64,2176]{1,0:T(8,128)(2,1)} custom-call(s32[6]{0:T(128)} %stack.34.place, bf16[2,16,4320]{2,1,0:T(8,128)(2,1)} %anomaly.1, f32[32,1]{1,0:T(8,128)} %reshape.25.weight, s32[1,64]{1,0:T(1,128)} %order.1, bf16[256,256]{1,0:T(8,128)(2,1)} %rows.1, s32[1,256]{1,0:T(1,128)} %bitcast.28), custom_call_target="tpu_custom_call" | custom-call | tf_op jit(solution)/shard_map/prepare/pallas_call | solution.py:199
  27.5 1.6 %fusion = (bf16[64,512]{1,0:T(8,128)(2,1)S(1)}, bf16[64,512]{1,0:T(8,128)(2,1)S(1)}, bf16[64,512]{1,0:T(8,128)(2,1)S(1)}, bf16[64,512]{1,0:T(8,128)(2,1)}) fusion(bf16[64,2176]{1,0:T(8,128)(2,1)} %prepare.1), kind=kLoop, calls=%fused_computation.4 | loop fusion | bytes 524288 | tf_op jit(solution)/shard_map/slice | solution.py:227
  29.1 4.4 %collective-permute-start.2 = (bf16[64,512]{1,0:T(8,128)(2,1)S(1)}, bf16[64,512]{1,0:T(8,128)(2,1)S(1)}, u32[]{:S(2)}, u32[]{:S(2)}) collective-permute-start(bf16[64,512]{1,0:T(8,128)(2,1)S(1)} %get-tuple-element.10), channel_id=1, source_target_pairs={{0,3},{1,0},{2,1},{3,2},{4,7},{5,4},{6,5},{7,6},{8,11},{9,8},{10,9... | collective-permute-start | bytes 196616 | tf_op jit(solution)/shard_map/ppermute | solution.py:227
  33.4 2.4 %collective-permute-start.1 = (bf16[64,512]{1,0:T(8,128)(2,1)S(1)}, bf16[64,512]{1,0:T(8,128)(2,1)S(1)}, u32[]{:S(2)}, u32[]{:S(2)}) collective-permute-start(bf16[64,512]{1,0:T(8,128)(2,1)S(1)} %get-tuple-element.11), channel_id=1, source_target_pairs={{0,2},{1,3},{2,0},{3,1},{4,6},{5,7},{6,4},{7,5},{8,10},{9,11},{10,... | collective-permute-start | bytes 196616 | tf_op jit(solution)/shard_map/ppermute | solution.py:227
  35.9 2.5 %collective-permute-start = (bf16[64,512]{1,0:T(8,128)(2,1)S(1)}, bf16[64,512]{1,0:T(8,128)(2,1)S(1)}, u32[]{:S(2)}, u32[]{:S(2)}) collective-permute-start(bf16[64,512]{1,0:T(8,128)(2,1)S(1)} %get-tuple-element.12), channel_id=1, source_target_pairs={{0,1},{1,2},{2,3},{3,0},{4,5},{5,6},{6,7},{7,4},{8,9},{9,10},{10,1... | collective-permute-start | bytes 196616 | tf_op jit(solution)/shard_map/ppermute | solution.py:227
  38.4 1.3 slice.44.refs_4_
  39.7 0.0 collective-permute-done.2.refs_3_
  39.7 0.0 copy-start.4
  39.7 0.5 collective-permute-done.1.refs_2_
  40.3 0.0 copy-start.5
  40.3 2.5 %collective-permute-done.refs_1_ = bf16[64,512]{1,0:T(8,128)(2,1)S(1)} collective-permute-done((bf16[64,512]{1,0:T(8,128)(2,1)S(1)}, bf16[64,512]{1,0:T(8,128)(2,1)S(1)}, u32[]{:S(2)}, u32[]{:S(2)}) %collective-permute-start) | collective-permute-done | bytes 65568 | tf_op jit(solution)/shard_map/ppermute | solution.py:227
  42.8 0.0 copy-start.6
  42.8 0.0 copy-done.4
  42.8 0.0 copy-done.5
  42.8 0.6 copy-done.6
  43.4 1.7 %pack.1 = bf16[64,2176]{1,0:T(8,128)(2,1)} custom-call(bf16[64,512]{1,0:T(8,128)(2,1)} %get-tuple-element.13.refs_0_, bf16[64,512]{1,0:T(8,128)(2,1)} %copy-done.6, bf16[64,512]{1,0:T(8,128)(2,1)} %copy-done.5, bf16[64,512]{1,0:T(8,128)(2,1)} %copy-done.4, bf16[64,128]{1,0:T(8,128)(2,1)} %slice.44.refs_4_), custom_call_target="tpu_custom_call" | custom-call | tf_op jit(solution)/shard_map/pack/pallas_call | solution.py:236
  45.1 1.0 slice_bitcast_fusion
  46.1 7.3 %collective-permute-start.5 = (bf16[16,2176]{1,0:T(8,128)(2,1)S(1)}, bf16[16,2176]{1,0:T(8,128)(2,1)S(1)}, u32[]{:S(2)}, u32[]{:S(2)}) collective-permute-start(bf16[16,2176]{1,0:T(8,128)(2,1)S(1)} %get-tuple-element.7), channel_id=1, source_target_pairs={{0,384},{8,392},{16,400},{24,408},{32,416},{40,424},{48,432},{56,4... | collective-permute-start | bytes 208904 | tf_op jit(solution)/shard_map/ppermute | solution.py:240
  53.4 6.8 %collective-permute-start.4 = (bf16[16,2176]{1,0:T(8,128)(2,1)S(1)}, bf16[16,2176]{1,0:T(8,128)(2,1)S(1)}, u32[]{:S(2)}, u32[]{:S(2)}) collective-permute-start(bf16[16,2176]{1,0:T(8,128)(2,1)S(1)} %get-tuple-element.8), channel_id=1, source_target_pairs={{0,256},{8,264},{16,272},{24,280},{32,288},{40,296},{48,304},{56,3... | collective-permute-start | bytes 208904 | tf_op jit(solution)/shard_map/ppermute | solution.py:240
  60.2 7.1 %collective-permute-start.3 = (bf16[16,2176]{1,0:T(8,128)(2,1)S(1)}, bf16[16,2176]{1,0:T(8,128)(2,1)S(1)}, u32[]{:S(2)}, u32[]{:S(2)}) collective-permute-start(bf16[16,2176]{1,0:T(8,128)(2,1)S(1)} %get-tuple-element.9), channel_id=1, source_target_pairs={{0,128},{8,136},{16,144},{24,152},{32,160},{40,168},{48,176},{56,1... | collective-permute-start | bytes 208904 | tf_op jit(solution)/shard_map/ppermute | solution.py:240
  67.3 0.1 copy.17
  67.4 15.8 %collective-permute-done.5 = bf16[16,2176]{1,0:T(8,128)(2,1)S(1)} collective-permute-done((bf16[16,2176]{1,0:T(8,128)(2,1)S(1)}, bf16[16,2176]{1,0:T(8,128)(2,1)S(1)}, u32[]{:S(2)}, u32[]{:S(2)}) %collective-permute-start.5) | collective-permute-done | bytes 69664 | tf_op jit(solution)/shard_map/ppermute | solution.py:240
  83.2 0.1 copy.20
  83.3 5.9 %collective-permute-done.4 = bf16[16,2176]{1,0:T(8,128)(2,1)S(1)} collective-permute-done((bf16[16,2176]{1,0:T(8,128)(2,1)S(1)}, bf16[16,2176]{1,0:T(8,128)(2,1)S(1)}, u32[]{:S(2)}, u32[]{:S(2)}) %collective-permute-start.4) | collective-permute-done | bytes 69664 | tf_op jit(solution)/shard_map/ppermute | solution.py:240
  89.2 0.1 copy.19
  89.3 0.0 collective-permute-done.3
  89.4 0.1 copy.18
  89.5 1.4 %pad_maximum_fusion = bf16[16,4,2176]{2,1,0:T(4,128)(2,1)} fusion(bf16[16,1,2176]{2,1,0:T(2,128)(2,1)S(1)} %copy.20, bf16[16,1,2176]{2,1,0:T(2,128)(2,1)S(1)} %copy.19, bf16[16,1,2176]{2,1,0:T(2,128)(2,1)S(1)} %copy.18, bf16[16,1,2176]{2,1,0:T(2,128)(2,1)S(1)} %copy.17), kind=kLoop, calls=%fused_computation | loop fusion | flops 1114112 | bytes 557056 | tf_op jit(solution)/shard_map/stack | solution.py:243
  90.8 0.0 all-to-all-done.1
  90.8 0.0 copy-start
  90.8 11.8 %all-to-all-start = ((bf16[16,4,2176]{2,1,0:T(4,128)(2,1)}), bf16[16,4,2176]{2,1,0:T(4,128)(2,1)S(1)}, u32[]{:S(2)}, u32[]{:S(2)}) async-start(bf16[16,4,2176]{2,1,0:T(4,128)(2,1)} %pad_maximum_fusion), calls=%async_computation | async-start | bytes 557056 | tf_op jit(solution)/shard_map/all_to_all | solution.py:242
  102.7 4.6 %collective-permute-start.7 = (bf16[1024,640]{1,0:T(8,128)(2,1)S(1)}, bf16[1024,640]{1,0:T(8,128)(2,1)S(1)}, u32[]{:S(2)}, u32[]{:S(2)}) collective-permute-start(bf16[1024,640]{1,0:T(8,128)(2,1)S(1)} %bitcast.19), channel_id=1, source_target_pairs={{0,4},{4,0},{1,5},{5,1},{2,6},{6,2},{3,7},{7,3},{8,12},{12,8},{9,1... | collective-permute-start | bytes 3932168 | tf_op jit(solution)/shard_map/ppermute | solution.py:253
  107.3 4.4 %all-to-all-done.sat_own = bf16[16,4,2176]{2,1,0:T(4,128)(2,1)S(1)} async-done(((bf16[16,4,2176]{2,1,0:T(4,128)(2,1)}), bf16[16,4,2176]{2,1,0:T(4,128)(2,1)S(1)}, u32[]{:S(2)}, u32[]{:S(2)}) %all-to-all-start) | async-done | bytes 278560 | tf_op jit(solution)/shard_map/all_to_all | solution.py:242
  111.7 0.0 copy-start.2
  111.7 5.7 %collective-permute-start.6 = (bf16[16,4,2176]{2,1,0:T(4,128)(2,1)S(1)}, bf16[16,4,2176]{2,1,0:T(4,128)(2,1)S(1)}, u32[]{:S(2)}, u32[]{:S(2)}) collective-permute-start(bf16[16,4,2176]{2,1,0:T(4,128)(2,1)S(1)} %all-to-all-done.sat_own), channel_id=1, source_target_pairs={{0,4},{4,0},{1,5},{5,1},{2,6},{6,2},{3,7},{7,3},{8,12},{12,8},{9,1... | collective-permute-start | bytes 835592 | tf_op jit(solution)/shard_map/ppermute | solution.py:250
  117.4 1.9 %weights.1 = (f32[1024,128]{1,0:T(8,128)}, f32[1024,128]{1,0:T(8,128)}) custom-call(f32[2,1024]{1,0:T(2,128)} %weight.1), custom_call_target="tpu_custom_call" | custom-call | tf_op jit(solution)/shard_map/weights/pallas_call | solution.py:221
  119.3 0.6 slice.49
  119.9 0.0 copy-done
  119.9 2.5 %right.1 = f32[2,1,640]{2,1,0:T(1,128)} custom-call(s32[6]{0:T(128)} %stack.34.place, bf16[64,128]{1,0:T(8,128)(2,1)} %bitcast.26, bf16[1024,640]{1,0:T(8,128)(2,1)} %bitcast.20), custom_call_target="tpu_custom_call" | custom-call | tf_op jit(solution)/shard_map/right/pallas_call | solution.py:277
  122.4 0.0 collective-permute-done.7.other
  122.4 0.0 copy-start.1
  122.4 1.1 copy-done.1
  123.5 6.7 %gram.1.normals = f32[640,2,640]{2,1,0:T(2,128)} custom-call(s32[6]{0:T(128)} %stack.34.place, bf16[1024,640]{1,0:T(8,128)(2,1)} %bitcast.21, bf16[1024,640]{1,0:T(8,128)(2,1)} %copy-done.1, f32[1024,128]{1,0:T(8,128)} %get-tuple-element.4.plus, f32[1024,128]{1,0:T(8,128)} %get-tuple-element.5.minus), custom_call_target="tpu_custom_call" | custom-call | tf_op jit(solution)/shard_map/gram/pallas_call | solution.py:269
  130.2 0.0 copy-done.2
  130.2 0.0 collective-permute-done.6.sat_other
  130.2 0.0 copy-start.3
  130.2 0.7 copy-done.3
  130.9 2.1 %add.15 = f32[640,2,640]{2,1,0:T(2,128)} custom-call(s32[6]{0:T(128)} %stack.34.place, bf16[16,4,2176]{2,1,0:T(4,128)(2,1)} %copy-done.2, bf16[16,4,2176]{2,1,0:T(4,128)(2,1)} %copy-done.3, f32[640,2,640]{2,1,0:T(2,128)} %gram.1.normals), custom_call_target="tpu_custom_call", output_to_operand_aliasing={{}: (3, {})} | custom-call | tf_op jit(solution)/shard_map/add/pallas_call | solution.py:280
Async XLA Ops:
  0.6 21.4 %copy-start.7 = (s32[1,64]{1,0:T(1,128)S(1)}, s32[1,64]{1,0:T(1,128)}, u32[]{:S(2)}) copy-start(s32[1,64]{1,0:T(1,128)} %order.1) | copy-start | bytes 772
  0.6 90.2 %all-to-all-start.1 = ((bf16[1,64,16,1,640]{4,2,3,0,1:T(8,128)(2,1)}), bf16[1,64,16,1,640]{4,2,3,0,1:T(8,128)(2,1)S(1)}, u32[]{:S(2)}, u32[]{:S(2)}) async-start(bf16[1,64,16,1,640]{4,2,3,0,1:T(8,128)(2,1)} %bitcast.22), calls=%async_computation.1 | async-start | bytes 2621440 | tf_op jit(solution)/shard_map/all_to_all | solution.py:194
  29.1 10.7 %collective-permute-start.2 = (bf16[64,512]{1,0:T(8,128)(2,1)S(1)}, bf16[64,512]{1,0:T(8,128)(2,1)S(1)}, u32[]{:S(2)}, u32[]{:S(2)}) collective-permute-start(bf16[64,512]{1,0:T(8,128)(2,1)S(1)} %get-tuple-element.10), channel_id=1, source_target_pairs={{0,3},{1,0},{2,1},{3,2},{4,7},{5,4},{6,5},{7,6},{8,11},{9,8},{10,9... | collective-permute-start | bytes 196616 | tf_op jit(solution)/shard_map/ppermute | solution.py:227
  33.4 6.8 %collective-permute-start.1 = (bf16[64,512]{1,0:T(8,128)(2,1)S(1)}, bf16[64,512]{1,0:T(8,128)(2,1)S(1)}, u32[]{:S(2)}, u32[]{:S(2)}) collective-permute-start(bf16[64,512]{1,0:T(8,128)(2,1)S(1)} %get-tuple-element.11), channel_id=1, source_target_pairs={{0,2},{1,3},{2,0},{3,1},{4,6},{5,7},{6,4},{7,5},{8,10},{9,11},{10,... | collective-permute-start | bytes 196616 | tf_op jit(solution)/shard_map/ppermute | solution.py:227
  35.9 6.9 %collective-permute-start = (bf16[64,512]{1,0:T(8,128)(2,1)S(1)}, bf16[64,512]{1,0:T(8,128)(2,1)S(1)}, u32[]{:S(2)}, u32[]{:S(2)}) collective-permute-start(bf16[64,512]{1,0:T(8,128)(2,1)S(1)} %get-tuple-element.12), channel_id=1, source_target_pairs={{0,1},{1,2},{2,3},{3,0},{4,5},{5,6},{6,7},{7,4},{8,9},{9,10},{10,1... | collective-permute-start | bytes 196616 | tf_op jit(solution)/shard_map/ppermute | solution.py:227
  39.7 3.0 %copy-start.4 = (bf16[64,512]{1,0:T(8,128)(2,1)}, bf16[64,512]{1,0:T(8,128)(2,1)S(1)}, u32[]{:S(2)}) copy-start(bf16[64,512]{1,0:T(8,128)(2,1)S(1)} %collective-permute-done.2.refs_3_) | copy-start | bytes 196612
  40.3 2.5 %copy-start.5 = (bf16[64,512]{1,0:T(8,128)(2,1)}, bf16[64,512]{1,0:T(8,128)(2,1)S(1)}, u32[]{:S(2)}) copy-start(bf16[64,512]{1,0:T(8,128)(2,1)S(1)} %collective-permute-done.1.refs_2_) | copy-start | bytes 196612
  42.8 0.6 copy-start.6
  46.1 37.1 %collective-permute-start.5 = (bf16[16,2176]{1,0:T(8,128)(2,1)S(1)}, bf16[16,2176]{1,0:T(8,128)(2,1)S(1)}, u32[]{:S(2)}, u32[]{:S(2)}) collective-permute-start(bf16[16,2176]{1,0:T(8,128)(2,1)S(1)} %get-tuple-element.7), channel_id=1, source_target_pairs={{0,384},{8,392},{16,400},{24,408},{32,416},{40,424},{48,432},{56,4... | collective-permute-start | bytes 208904 | tf_op jit(solution)/shard_map/ppermute | solution.py:240
  53.4 35.9 %collective-permute-start.4 = (bf16[16,2176]{1,0:T(8,128)(2,1)S(1)}, bf16[16,2176]{1,0:T(8,128)(2,1)S(1)}, u32[]{:S(2)}, u32[]{:S(2)}) collective-permute-start(bf16[16,2176]{1,0:T(8,128)(2,1)S(1)} %get-tuple-element.8), channel_id=1, source_target_pairs={{0,256},{8,264},{16,272},{24,280},{32,288},{40,296},{48,304},{56,3... | collective-permute-start | bytes 208904 | tf_op jit(solution)/shard_map/ppermute | solution.py:240
  60.2 29.2 %collective-permute-start.3 = (bf16[16,2176]{1,0:T(8,128)(2,1)S(1)}, bf16[16,2176]{1,0:T(8,128)(2,1)S(1)}, u32[]{:S(2)}, u32[]{:S(2)}) collective-permute-start(bf16[16,2176]{1,0:T(8,128)(2,1)S(1)} %get-tuple-element.9), channel_id=1, source_target_pairs={{0,128},{8,136},{16,144},{24,152},{32,160},{40,168},{48,176},{56,1... | collective-permute-start | bytes 208904 | tf_op jit(solution)/shard_map/ppermute | solution.py:240
  90.8 29.1 %copy-start = (bf16[1,64,16,1,640]{4,2,3,0,1:T(8,128)(2,1)}, bf16[1,64,16,1,640]{4,2,3,0,1:T(8,128)(2,1)S(1)}, u32[]{:S(2)}) copy-start(bf16[1,64,16,1,640]{4,2,3,0,1:T(8,128)(2,1)S(1)} %all-to-all-done.1) | copy-start | bytes 3932164
  90.8 20.9 %all-to-all-start = ((bf16[16,4,2176]{2,1,0:T(4,128)(2,1)}), bf16[16,4,2176]{2,1,0:T(4,128)(2,1)S(1)}, u32[]{:S(2)}, u32[]{:S(2)}) async-start(bf16[16,4,2176]{2,1,0:T(4,128)(2,1)} %pad_maximum_fusion), calls=%async_computation | async-start | bytes 557056 | tf_op jit(solution)/shard_map/all_to_all | solution.py:242
  102.7 19.7 %collective-permute-start.7 = (bf16[1024,640]{1,0:T(8,128)(2,1)S(1)}, bf16[1024,640]{1,0:T(8,128)(2,1)S(1)}, u32[]{:S(2)}, u32[]{:S(2)}) collective-permute-start(bf16[1024,640]{1,0:T(8,128)(2,1)S(1)} %bitcast.19), channel_id=1, source_target_pairs={{0,4},{4,0},{1,5},{5,1},{2,6},{6,2},{3,7},{7,3},{8,12},{12,8},{9,1... | collective-permute-start | bytes 3932168 | tf_op jit(solution)/shard_map/ppermute | solution.py:253
  111.7 18.4 %copy-start.2 = (bf16[16,4,2176]{2,1,0:T(4,128)(2,1)}, bf16[16,4,2176]{2,1,0:T(4,128)(2,1)S(1)}, u32[]{:S(2)}) copy-start(bf16[16,4,2176]{2,1,0:T(4,128)(2,1)S(1)} %all-to-all-done.sat_own) | copy-start | bytes 835588
  111.7 18.4 %collective-permute-start.6 = (bf16[16,4,2176]{2,1,0:T(4,128)(2,1)S(1)}, bf16[16,4,2176]{2,1,0:T(4,128)(2,1)S(1)}, u32[]{:S(2)}, u32[]{:S(2)}) collective-permute-start(bf16[16,4,2176]{2,1,0:T(4,128)(2,1)S(1)} %all-to-all-done.sat_own), channel_id=1, source_target_pairs={{0,4},{4,0},{1,5},{5,1},{2,6},{6,2},{3,7},{7,3},{8,12},{12,8},{9,1... | collective-permute-start | bytes 835592 | tf_op jit(solution)/shard_map/ppermute | solution.py:250
  122.4 1.1 copy-start.1
  130.2 0.7 copy-start.3

commit v3 on v2

--- a/solution.py
+++ b/solution.py
@@ -29,7 +29,7 @@
 
 
 def prepare_kernel(place, anomaly, weight, order, rows, slot, out, table_high, table_low):
-    far, x = place[0], place[2]
+    y, x = place[1], place[2]
     length = anomaly.shape[2]
     order_pair = jnp.concatenate([order[...], order[...]], axis=1).astype(F32)
     fine = turn(iota((STEP, 128), 0).astype(F32) * order_pair, length)
@@ -52,7 +52,8 @@
     at, own = iota((64, 64), 0), iota((64, 64), 1)
 
     def position(slot_in_group):
-        return (((slot_in_group >> 4) - far) & 3) * 16 + (slot_in_group & 15)
+        side = ((slot_in_group & 3) - y) & 3
+        return side * 16 + (slot_in_group >> 2)
 
     pick = (position(own) == at).astype(F32).astype(BF16)
     out[:, 2048:2176] = jnp.concatenate(
@@ -137,28 +138,42 @@
     out = refs[-1]
     at = 0
     for ref in refs[:-1]:
-        width = ref.shape[1]
-        out[:, at : at + width] = ref[...]
+        width = ref.shape[2]
+        out[:, :, at : at + width] = ref[...]
         at += width
 
 
-def right_kernel(place, coef, own, right):
-    far, p, first, order = place[0], place[3], place[4], place[5]
-    row_all, half = own.shape
-    index = iota((64, row_all), 0)
-    source = ((far - index) & 3) * 16 + (index >> 2)
-    mine = source == (iota((64, row_all), 1) >> 4)
-    spread = ((iota((16, row_all), 1) & 15) == iota((16, row_all), 0)).astype(F32).astype(BF16)
-    lines = []
-    for c in range(4):
-        wide = dot(coef[:, c * 16 : (c + 1) * 16], spread, ((1,), (0,)))
-        lines.append(jnp.sum(jnp.where(mine, wide, 0.0), axis=0, keepdims=True))
-    lines.append(jnp.zeros((4, row_all), F32))
-    terms = jnp.concatenate(lines, axis=0).astype(BF16)
-    product = dot(terms, own[...], ((1,), (0,))) * live_row(first, p, half)
-    sign = 1.0 - 2.0 * ((first + p + order + iota((1, half), 1) * 2) & 1).astype(F32)
-    right[0] = product[0:1] + sign * product[1:2]
-    right[1] = product[2:3] + sign * product[3:4]
+def right_kernel(place, coef, own, right, terms, total):
+    y, p, first, order = place[1], place[3], place[4], place[5]
+    rows, half = own.shape
+    step = pl.program_id(0)
+
+    @pl.when(step == 0)
+    def _():
+        steps = terms.shape[0]
+        flat = coef[...].reshape(64, 128)
+        for k in range(steps):
+            index = iota((64, rows), 0)
+            source = (index & 60) + ((y - index) & 3)
+            mine = source == (iota((64, rows), 1) >> 4) + k * (rows // 16)
+            spread = ((iota((16, rows), 1) & 15) == iota((16, rows), 0)).astype(F32).astype(BF16)
+            lines = []
+            for c in range(4):
+                wide = dot(flat[:, c * 16 : (c + 1) * 16], spread, ((1,), (0,)))
+                lines.append(jnp.sum(jnp.where(mine, wide, 0.0), axis=0, keepdims=True))
+            lines.append(jnp.zeros((4, rows), F32))
+            terms[k] = jnp.concatenate(lines, axis=0).astype(BF16)
+        total[...] = jnp.zeros(total.shape, F32)
+
+    total[...] += dot(terms[step], own[...], ((1,), (0,)))
+
+    @pl.when(step == pl.num_programs(0) - 1)
+    def _():
+        product = total[...] * live_row(first, p, half)
+        degree = first + p + order + 2 * iota((1, half), 1)
+        sign = 1.0 - 2.0 * (degree & 1).astype(F32)
+        right[0] = product[0:1] + sign * product[1:2]
+        right[1] = product[2:3] + sign * product[3:4]
 
 
 def add_kernel(place, sat_own, sat_other, normals, out):
@@ -188,13 +203,13 @@
     row_count = panel.shape[2]
     half = panel.shape[4]
     row_all = row_weight.shape[1]
-    far = lat_index // 16
+    z, y = lat_index // 4, lat_index % 4
     smem = whole(pltpu.SMEM)
 
     arrived = lax.all_to_all(panel, "lat", split_axis=1, concat_axis=2, tiled=True)
 
     own_order = lax.dynamic_slice_in_dim(order_value[0], lat_index, 1, 0)[0]
-    place = jnp.stack([far, lat_index % 16, orb_index, parity, deg_first[0, 0], own_order]).astype(I32)
+    place = jnp.stack([z, y, orb_index, parity, deg_first[0, 0], own_order]).astype(I32)
     local_weight = lax.dynamic_slice_in_dim(row_weight, lat_index * row_count, row_count, 1)
     packed = pl.pallas_call(
         prepare_kernel,
@@ -221,31 +236,28 @@
     plus, minus = weights(row_weight)
 
     width = packed.shape[1]
-    groups = [packed[:, :512]]
+    blocks = packed.reshape(4, 16, width)
+    sides = [blocks[0]]
+    for e in (1, 2, 3):
+        ring = [(a * 4 + b, a * 4 + (b + e) % 4) for a in range(16) for b in range(4)]
+        sides.append(lax.ppermute(blocks[e], "lat", ring))
+    sides = jnp.stack(sides, axis=1)
+    groups = [sides[:, :, :512]]
     for f in (1, 2, 3):
         ring = [(i, (i + f) % 4) for i in range(4)]
-        groups.append(lax.ppermute(packed[:, f * 512 : (f + 1) * 512], "orb", ring))
-    groups.append(packed[:, 2048:])
+        groups.append(lax.ppermute(sides[:, :, f * 512 : (f + 1) * 512], "orb", ring))
+    groups.append(sides[:, :, 2048:])
     pack = pl.pallas_call(
         pack_kernel,
-        out_shape=jax.ShapeDtypeStruct((64, width), BF16),
+        out_shape=jax.ShapeDtypeStruct((16, 4, width), BF16),
         in_specs=[whole()] * 5,
         out_specs=whole(),
         name="pack",
     )
     packed = pack(*groups)
-    fars = [packed[:16]]
-    for h in (1, 2, 3):
-        ring = [(i, (i + 16 * h) % 64) for i in range(64)]
-        fars.append(lax.ppermute(packed[16 * h : 16 * (h + 1)], "lat", ring))
-    blocks = [[16 * g + j for j in range(16)] for g in range(4)]
+    columns = [[a * 4 + b for a in range(16)] for b in range(4)]
     sat_own = lax.all_to_all(
-        jnp.stack(fars, axis=1),
-        "lat",
-        split_axis=0,
-        concat_axis=0,
-        axis_index_groups=blocks,
-        tiled=True,
+        packed, "lat", split_axis=0, concat_axis=0, axis_index_groups=columns, tiled=True
     )
     sat_other = lax.ppermute(sat_own, "ord", [(0, 1), (1, 0)])
 
@@ -267,14 +279,21 @@
         name="gram",
     )
     normals = gram_call(place, own_panel, other_panel, plus, minus)
+    chunk = row_all // 4
     right_call = pl.pallas_call(
         right_kernel,
+        grid=(4,),
         out_shape=jax.ShapeDtypeStruct((2, 1, half), F32),
-        in_specs=[smem] + [whole()] * 2,
-        out_specs=whole(),
+        in_specs=[
+            smem,
+            pl.BlockSpec((16, 4, 128), lambda i: (0, 0, 16)),
+            pl.BlockSpec((chunk, half), lambda i: (i, 0)),
+        ],
+        out_specs=pl.BlockSpec((2, 1, half), lambda i: (0, 0, 0)),
+        scratch_shapes=[pltpu.VMEM((4, 8, chunk), BF16), pltpu.VMEM((8, half), F32)],
         name="right",
     )
-    right = right_call(place, sat_own[:, :, 2048:].reshape(64, 128), own_panel)
+    right = right_call(place, sat_own, own_panel)
     corner = pl.BlockSpec((128, 2, 128), lambda i: (0, 0, 0))
     sat_spec = pl.BlockSpec((16, 4, width), lambda i: (0, 0, 0))
     normals = pl.pallas_call(

time: 134 us -> 128 us (0.955)
  starting transfers between devices: 71.9 us -> 56.9 us
  waiting for transfers between devices: 29.2 us -> 40 us
  local copies, waits for them, and re-layouts: 10.6 us -> 7.78 us
    all_to_all x1, waiting for transfers between devices: 0.01 us -> 23.5 us  [shards(): lax.all_to_all(panel, 'lat', split_axis=1, concat_axis=2, tiled=True)]
    ppermute x6, waiting for transfers between devices: 24.8 us -> 7.81 us  [the longest x3 4.48 us: shards(): sides.append(lax.ppermute(blocks[e], 'lat', ring))]
    ppermute x6, starting transfers between devices: 30.5 us -> 18.4 us  [the longest x3 9.28 us: shards(): groups.append(lax.ppermute(sides[:, :, f * 512:(f + 1) * 512], 'orb', ring))]
    all_to_all x1, starting transfers between devices: 11.8 us -> 5.72 us  [shards(): lax.all_to_all(packed, 'lat', split_axis=0, concat_axis=0, axis_index_gro...]
    all_to_all x1, waiting for transfers between devices: 4.4 us -> 8.71 us  [shards(): lax.all_to_all(packed, 'lat', split_axis=0, concat_axis=0, axis_index_gro...]
    ppermute x1, starting transfers between devices: 5.69 us -> 9.38 us  [shards(): sat_other = lax.ppermute(sat_own, 'ord', [(0, 1), (1, 0)])]
    slice x3 -> x1, local copies, waits for them, and re-layouts: 3.5 us -> 0.72 us  [shards(): groups.append(lax.ppermute(sides[:, :, f * 512:(f + 1) * 512], 'orb', ring))]
  transfers between devices with their start and end apart: 10 -> 10, of which waited for: 5 -> 6; matrix products, arithmetic and copies ran while one was open for 7% -> 5% of each run, Pallas kernels for 12% -> 14%
where the time goes in v3:
time: 128 us; the launch traced here: 127 us
  starting transfers between devices  56.9 us (44%)
  waiting for transfers between devices  40 us (31%)
  Pallas kernels  19.4 us (15%)
  local copies, waits for them, and re-layouts  7.78 us (6%)
  between operations  1.46 us (1%)
  other arithmetic  1.29 us (1%)
    all_to_all x1, waiting for transfers between devices, shards(): lax.all_to_all(panel, 'lat', split_axis=1, concat_axis=2, tiled=True)  23.5 us
    all_to_all x1, starting transfers between devices, shards(): lax.all_to_all(panel, 'lat', split_axis=1, concat_axis=2, tiled=True)  19.3 us
    ppermute x1, starting transfers between devices, shards(): sat_other = lax.ppermute(sat_own, 'ord', [(0, 1), (1, 0)])  9.38 us
    ppermute x3, starting transfers between devices, shards(): groups.append(lax.ppermute(sides[:, :, f * 512:(f + 1) * 512], 'orb', ring))  9.28 us
    ppermute x3, starting transfers between devices, shards(): sides.append(lax.ppermute(blocks[e], 'lat', ring))  9.1 us
    all_to_all x1, waiting for transfers between devices, shards(): lax.all_to_all(packed, 'lat', split_axis=0, concat_axis=0, axis_index_gro...  8.71 us
    pallas_call x1, Pallas kernels, shards(): normals = gram_call(place, own_panel, other_panel, plus, minus)  6.7 us
    all_to_all x1, starting transfers between devices, shards(): lax.all_to_all(packed, 'lat', split_axis=0, concat_axis=0, axis_index_gro...  5.72 us
  transfers between devices with their start and end apart: 10, of which 6 were waited for; matrix products, arithmetic and copies ran while one was open for 5% of the time, Pallas kernels for 14%

profile of v3, /device:TPU:1, one launch (start us, length us, event | category | flops | bytes accessed | tf_op | source)
XLA Modules:
  0.0 126.8 jit_solution(9264903450414091532)
XLA Ops:
  0.6 0.0 copy-start.7
  0.6 19.3 %all-to-all-start.1 = ((bf16[1,64,16,1,640]{4,2,3,0,1:T(8,128)(2,1)}), bf16[1,64,16,1,640]{4,2,3,0,1:T(8,128)(2,1)S(1)}, u32[]{:S(2)}, u32[]{:S(2)}) async-start(bf16[1,64,16,1,640]{4,2,3,0,1:T(8,128)(2,1)} %bitcast.21), calls=%async_computation.1 | async-start | bytes 2621440 | tf_op jit(solution)/shard_map/all_to_all | solution.py:209
  20.6 0.8 constant_dynamic-slice_fusion
  21.4 0.7 reshape.30.weight
  22.0 0.0 copy-done.7
  22.0 0.6 constant_dynamic-slice_fusion.1
  22.6 1.2 stack.31.place
  23.8 3.7 %prepare.1 = bf16[64,2176]{1,0:T(8,128)(2,1)} custom-call(s32[6]{0:T(128)} %stack.31.place, bf16[2,16,4320]{2,1,0:T(8,128)(2,1)} %anomaly.1, f32[32,1]{1,0:T(8,128)} %reshape.30.weight, s32[1,64]{1,0:T(1,128)} %order.1, bf16[256,256]{1,0:T(8,128)(2,1)} %rows.1, s32[1,256]{1,0:T(1,128)} %bitcast.26), custom_call_target="tpu_custom_call" | custom-call | tf_op jit(solution)/shard_map/prepare/pallas_call | solution.py:214
  27.5 1.0 slice_bitcast_fusion
  28.5 4.1 %collective-permute-start.2 = (bf16[16,2176]{1,0:T(8,128)(2,1)S(1)}, bf16[16,2176]{1,0:T(8,128)(2,1)S(1)}, u32[]{:S(2)}, u32[]{:S(2)}) collective-permute-start(bf16[16,2176]{1,0:T(8,128)(2,1)S(1)} %get-tuple-element.11), channel_id=1, source_target_pairs={{0,24},{8,0},{16,8},{24,16},{32,56},{40,32},{48,40},{56,48},{64,88... | collective-permute-start | bytes 208904 | tf_op jit(solution)/shard_map/ppermute | solution.py:243
  32.6 2.5 %collective-permute-start.1 = (bf16[16,2176]{1,0:T(8,128)(2,1)S(1)}, bf16[16,2176]{1,0:T(8,128)(2,1)S(1)}, u32[]{:S(2)}, u32[]{:S(2)}) collective-permute-start(bf16[16,2176]{1,0:T(8,128)(2,1)S(1)} %get-tuple-element.12), channel_id=1, source_target_pairs={{0,16},{8,24},{16,0},{24,8},{32,48},{40,56},{48,32},{56,40},{64,80... | collective-permute-start | bytes 208904 | tf_op jit(solution)/shard_map/ppermute | solution.py:243
  35.1 2.5 %collective-permute-start = (bf16[16,2176]{1,0:T(8,128)(2,1)S(1)}, bf16[16,2176]{1,0:T(8,128)(2,1)S(1)}, u32[]{:S(2)}, u32[]{:S(2)}) collective-permute-start(bf16[16,2176]{1,0:T(8,128)(2,1)S(1)} %get-tuple-element.13), channel_id=1, source_target_pairs={{0,8},{8,16},{16,24},{24,0},{32,40},{40,48},{48,56},{56,32},{64,72... | collective-permute-start | bytes 208904 | tf_op jit(solution)/shard_map/ppermute | solution.py:243
  37.6 0.1 copy.17
  37.7 0.0 collective-permute-done.2
  37.7 0.1 copy.20
  37.9 2.1 %collective-permute-done.1 = bf16[16,2176]{1,0:T(8,128)(2,1)S(1)} collective-permute-done((bf16[16,2176]{1,0:T(8,128)(2,1)S(1)}, bf16[16,2176]{1,0:T(8,128)(2,1)S(1)}, u32[]{:S(2)}, u32[]{:S(2)}) %collective-permute-start.1) | collective-permute-done | bytes 69664 | tf_op jit(solution)/shard_map/ppermute | solution.py:243
  40.0 0.1 copy.19
  40.1 2.4 %collective-permute-done = bf16[16,2176]{1,0:T(8,128)(2,1)S(1)} collective-permute-done((bf16[16,2176]{1,0:T(8,128)(2,1)S(1)}, bf16[16,2176]{1,0:T(8,128)(2,1)S(1)}, u32[]{:S(2)}, u32[]{:S(2)}) %collective-permute-start) | collective-permute-done | bytes 69664 | tf_op jit(solution)/shard_map/ppermute | solution.py:243
  42.5 0.1 copy.18
  42.6 0.7 pad_maximum_fusion
  43.2 0.7 fusion
  43.9 4.4 %collective-permute-start.5 = (bf16[16,4,512]{2,1,0:T(4,128)(2,1)S(1)}, bf16[16,4,512]{2,1,0:T(4,128)(2,1)S(1)}, u32[]{:S(2)}, u32[]{:S(2)}) collective-permute-start(bf16[16,4,512]{2,1,0:T(4,128)(2,1)S(1)} %get-tuple-element.6), channel_id=1, source_target_pairs={{0,3},{1,0},{2,1},{3,2},{4,7},{5,4},{6,5},{7,6},{8,11},{9,8},{10,9... | collective-permute-start | bytes 196616 | tf_op jit(solution)/shard_map/ppermute | solution.py:248
  48.3 2.4 %collective-permute-start.4 = (bf16[16,4,512]{2,1,0:T(4,128)(2,1)S(1)}, bf16[16,4,512]{2,1,0:T(4,128)(2,1)S(1)}, u32[]{:S(2)}, u32[]{:S(2)}) collective-permute-start(bf16[16,4,512]{2,1,0:T(4,128)(2,1)S(1)} %get-tuple-element.7), channel_id=1, source_target_pairs={{0,2},{1,3},{2,0},{3,1},{4,6},{5,7},{6,4},{7,5},{8,10},{9,11},{10,... | collective-permute-start | bytes 196616 | tf_op jit(solution)/shard_map/ppermute | solution.py:248
  50.7 2.5 %collective-permute-start.3 = (bf16[16,4,512]{2,1,0:T(4,128)(2,1)S(1)}, bf16[16,4,512]{2,1,0:T(4,128)(2,1)S(1)}, u32[]{:S(2)}, u32[]{:S(2)}) collective-permute-start(bf16[16,4,512]{2,1,0:T(4,128)(2,1)S(1)} %get-tuple-element.8), channel_id=1, source_target_pairs={{0,1},{1,2},{2,3},{3,0},{4,5},{5,6},{6,7},{7,4},{8,9},{9,10},{10,1... | collective-permute-start | bytes 196616 | tf_op jit(solution)/shard_map/ppermute | solution.py:248
  53.3 0.6 pad_maximum_fusion.1.refs_4_
  53.9 0.0 collective-permute-done.5.refs_3_
  53.9 0.0 copy-start.4
  53.9 1.2 collective-permute-done.4.refs_2_
  55.1 0.0 copy-start.5
  55.1 2.1 %collective-permute-done.3.refs_1_ = bf16[16,4,512]{2,1,0:T(4,128)(2,1)S(1)} collective-permute-done((bf16[16,4,512]{2,1,0:T(4,128)(2,1)S(1)}, bf16[16,4,512]{2,1,0:T(4,128)(2,1)S(1)}, u32[]{:S(2)}, u32[]{:S(2)}) %collective-permute-start.3) | collective-permute-done | bytes 65568 | tf_op jit(solution)/shard_map/ppermute | solution.py:248
  57.2 0.0 copy-start.6
  57.2 0.0 copy-done.4
  57.2 0.0 copy-done.5
  57.2 0.6 copy-done.6
  57.9 1.7 %pack.1 = bf16[16,4,2176]{2,1,0:T(4,128)(2,1)} custom-call(bf16[16,4,512]{2,1,0:T(4,128)(2,1)} %get-tuple-element.9.refs_0_, bf16[16,4,512]{2,1,0:T(4,128)(2,1)} %copy-done.6, bf16[16,4,512]{2,1,0:T(4,128)(2,1)} %copy-done.5, bf16[16,4,512]{2,1,0:T(4,128)(2,1)} %copy-done.4, bf16[16,4,128]{2,1,0:T(4,128)(2,1)} %pad_maximum_fusion.1.refs_4_), custom_call_target="tpu_custom_call" | custom-call | tf_op jit(solution)/shard_map/pack/pallas_call | solution.py:257
  59.5 23.5 %all-to-all-done.1 = bf16[1,64,16,1,640]{4,2,3,0,1:T(8,128)(2,1)S(1)} async-done(((bf16[1,64,16,1,640]{4,2,3,0,1:T(8,128)(2,1)}), bf16[1,64,16,1,640]{4,2,3,0,1:T(8,128)(2,1)S(1)}, u32[]{:S(2)}, u32[]{:S(2)}) %all-to-all-start.1) | async-done | bytes 1310752 | tf_op jit(solution)/shard_map/all_to_all | solution.py:209
  83.0 0.0 copy-start
  83.0 5.7 %all-to-all-start = ((bf16[16,4,2176]{2,1,0:T(4,128)(2,1)}), bf16[16,4,2176]{2,1,0:T(4,128)(2,1)S(1)}, u32[]{:S(2)}, u32[]{:S(2)}) async-start(bf16[16,4,2176]{2,1,0:T(4,128)(2,1)} %pack.1), calls=%async_computation | async-start | bytes 557056 | tf_op jit(solution)/shard_map/all_to_all | solution.py:259
  88.7 4.2 %collective-permute-start.7 = (bf16[1024,640]{1,0:T(8,128)(2,1)S(1)}, bf16[1024,640]{1,0:T(8,128)(2,1)S(1)}, u32[]{:S(2)}, u32[]{:S(2)}) collective-permute-start(bf16[1024,640]{1,0:T(8,128)(2,1)S(1)} %bitcast.18), channel_id=1, source_target_pairs={{0,4},{4,0},{1,5},{5,1},{2,6},{6,2},{3,7},{7,3},{8,12},{12,8},{9,1... | collective-permute-start | bytes 3932168 | tf_op jit(solution)/shard_map/ppermute | solution.py:265
  92.9 8.7 %all-to-all-done.sat_own.coef = bf16[16,4,2176]{2,1,0:T(4,128)(2,1)S(1)} async-done(((bf16[16,4,2176]{2,1,0:T(4,128)(2,1)}), bf16[16,4,2176]{2,1,0:T(4,128)(2,1)S(1)}, u32[]{:S(2)}, u32[]{:S(2)}) %all-to-all-start) | async-done | bytes 278560 | tf_op jit(solution)/shard_map/all_to_all | solution.py:259
  101.6 0.0 copy-start.1
  101.6 9.4 %collective-permute-start.6 = (bf16[16,4,2176]{2,1,0:T(4,128)(2,1)S(1)}, bf16[16,4,2176]{2,1,0:T(4,128)(2,1)S(1)}, u32[]{:S(2)}, u32[]{:S(2)}) collective-permute-start(bf16[16,4,2176]{2,1,0:T(4,128)(2,1)S(1)} %all-to-all-done.sat_own.coef), channel_id=1, source_target_pairs={{0,4},{4,0},{1,5},{5,1},{2,6},{6,2},{3,7},{7,3},{8,12},{12,8},{9,1... | collective-permute-start | bytes 835592 | tf_op jit(solution)/shard_map/ppermute | solution.py:262
  111.0 1.9 %weights.1 = (f32[1024,128]{1,0:T(8,128)}, f32[1024,128]{1,0:T(8,128)}) custom-call(f32[2,1024]{1,0:T(2,128)} %weight.1), custom_call_target="tpu_custom_call" | custom-call | tf_op jit(solution)/shard_map/weights/pallas_call | solution.py:236
  112.8 0.0 copy-done
  112.8 0.0 copy-done.1
  112.8 3.4 %right.1 = f32[2,1,640]{2,1,0:T(1,128)} custom-call(s32[6]{0:T(128)} %stack.31.place, bf16[16,4,2176]{2,1,0:T(4,128)(2,1)} %copy-done.1, bf16[1024,640]{1,0:T(8,128)(2,1)} %bitcast.19), custom_call_target="tpu_custom_call" | custom-call | tf_op jit(solution)/shard_map/right/pallas_call | solution.py:296
  116.3 0.0 collective-permute-done.7.other
  116.3 0.0 copy-start.2
  116.3 1.1 copy-done.2
  117.3 6.7 %gram.1.normals = f32[640,2,640]{2,1,0:T(2,128)} custom-call(s32[6]{0:T(128)} %stack.31.place, bf16[1024,640]{1,0:T(8,128)(2,1)} %bitcast.20, bf16[1024,640]{1,0:T(8,128)(2,1)} %copy-done.2, f32[1024,128]{1,0:T(8,128)} %get-tuple-element.4.plus, f32[1024,128]{1,0:T(8,128)} %get-tuple-element.5.minus), custom_call_target="tpu_custom_call" | custom-call | tf_op jit(solution)/shard_map/gram/pallas_call | solution.py:281
  124.0 0.0 collective-permute-done.6.sat_other
  124.0 0.0 copy-start.3
  124.0 0.7 copy-done.3
  124.7 2.1 %add.15 = f32[640,2,640]{2,1,0:T(2,128)} custom-call(s32[6]{0:T(128)} %stack.31.place, bf16[16,4,2176]{2,1,0:T(4,128)(2,1)} %copy-done.1, bf16[16,4,2176]{2,1,0:T(4,128)(2,1)} %copy-done.3, f32[640,2,640]{2,1,0:T(2,128)} %gram.1.normals), custom_call_target="tpu_custom_call", output_to_operand_aliasing={{}: (3, {})} | custom-call | tf_op jit(solution)/shard_map/add/pallas_call | solution.py:299
Async XLA Ops:
  0.6 21.4 %copy-start.7 = (s32[1,64]{1,0:T(1,128)S(1)}, s32[1,64]{1,0:T(1,128)}, u32[]{:S(2)}) copy-start(s32[1,64]{1,0:T(1,128)} %order.1) | copy-start | bytes 772
  0.6 82.3 %all-to-all-start.1 = ((bf16[1,64,16,1,640]{4,2,3,0,1:T(8,128)(2,1)}), bf16[1,64,16,1,640]{4,2,3,0,1:T(8,128)(2,1)S(1)}, u32[]{:S(2)}, u32[]{:S(2)}) async-start(bf16[1,64,16,1,640]{4,2,3,0,1:T(8,128)(2,1)} %bitcast.21), calls=%async_computation.1 | async-start | bytes 2621440 | tf_op jit(solution)/shard_map/all_to_all | solution.py:209
  28.5 9.2 %collective-permute-start.2 = (bf16[16,2176]{1,0:T(8,128)(2,1)S(1)}, bf16[16,2176]{1,0:T(8,128)(2,1)S(1)}, u32[]{:S(2)}, u32[]{:S(2)}) collective-permute-start(bf16[16,2176]{1,0:T(8,128)(2,1)S(1)} %get-tuple-element.11), channel_id=1, source_target_pairs={{0,24},{8,0},{16,8},{24,16},{32,56},{40,32},{48,40},{56,48},{64,88... | collective-permute-start | bytes 208904 | tf_op jit(solution)/shard_map/ppermute | solution.py:243
  32.6 7.3 %collective-permute-start.1 = (bf16[16,2176]{1,0:T(8,128)(2,1)S(1)}, bf16[16,2176]{1,0:T(8,128)(2,1)S(1)}, u32[]{:S(2)}, u32[]{:S(2)}) collective-permute-start(bf16[16,2176]{1,0:T(8,128)(2,1)S(1)} %get-tuple-element.12), channel_id=1, source_target_pairs={{0,16},{8,24},{16,0},{24,8},{32,48},{40,56},{48,32},{56,40},{64,80... | collective-permute-start | bytes 208904 | tf_op jit(solution)/shard_map/ppermute | solution.py:243
  35.1 7.3 %collective-permute-start = (bf16[16,2176]{1,0:T(8,128)(2,1)S(1)}, bf16[16,2176]{1,0:T(8,128)(2,1)S(1)}, u32[]{:S(2)}, u32[]{:S(2)}) collective-permute-start(bf16[16,2176]{1,0:T(8,128)(2,1)S(1)} %get-tuple-element.13), channel_id=1, source_target_pairs={{0,8},{8,16},{16,24},{24,0},{32,40},{40,48},{48,56},{56,32},{64,72... | collective-permute-start | bytes 208904 | tf_op jit(solution)/shard_map/ppermute | solution.py:243
  43.9 10.0 %collective-permute-start.5 = (bf16[16,4,512]{2,1,0:T(4,128)(2,1)S(1)}, bf16[16,4,512]{2,1,0:T(4,128)(2,1)S(1)}, u32[]{:S(2)}, u32[]{:S(2)}) collective-permute-start(bf16[16,4,512]{2,1,0:T(4,128)(2,1)S(1)} %get-tuple-element.6), channel_id=1, source_target_pairs={{0,3},{1,0},{2,1},{3,2},{4,7},{5,4},{6,5},{7,6},{8,11},{9,8},{10,9... | collective-permute-start | bytes 196616 | tf_op jit(solution)/shard_map/ppermute | solution.py:248
  48.3 6.8 %collective-permute-start.4 = (bf16[16,4,512]{2,1,0:T(4,128)(2,1)S(1)}, bf16[16,4,512]{2,1,0:T(4,128)(2,1)S(1)}, u32[]{:S(2)}, u32[]{:S(2)}) collective-permute-start(bf16[16,4,512]{2,1,0:T(4,128)(2,1)S(1)} %get-tuple-element.7), channel_id=1, source_target_pairs={{0,2},{1,3},{2,0},{3,1},{4,6},{5,7},{6,4},{7,5},{8,10},{9,11},{10,... | collective-permute-start | bytes 196616 | tf_op jit(solution)/shard_map/ppermute | solution.py:248
  50.7 6.5 %collective-permute-start.3 = (bf16[16,4,512]{2,1,0:T(4,128)(2,1)S(1)}, bf16[16,4,512]{2,1,0:T(4,128)(2,1)S(1)}, u32[]{:S(2)}, u32[]{:S(2)}) collective-permute-start(bf16[16,4,512]{2,1,0:T(4,128)(2,1)S(1)} %get-tuple-element.8), channel_id=1, source_target_pairs={{0,1},{1,2},{2,3},{3,0},{4,5},{5,6},{6,7},{7,4},{8,9},{9,10},{10,1... | collective-permute-start | bytes 196616 | tf_op jit(solution)/shard_map/ppermute | solution.py:248
  53.9 3.3 %copy-start.4 = (bf16[16,4,512]{2,1,0:T(4,128)(2,1)}, bf16[16,4,512]{2,1,0:T(4,128)(2,1)S(1)}, u32[]{:S(2)}) copy-start(bf16[16,4,512]{2,1,0:T(4,128)(2,1)S(1)} %collective-permute-done.5.refs_3_) | copy-start | bytes 196612
  55.1 2.1 %copy-start.5 = (bf16[16,4,512]{2,1,0:T(4,128)(2,1)}, bf16[16,4,512]{2,1,0:T(4,128)(2,1)S(1)}, u32[]{:S(2)}) copy-start(bf16[16,4,512]{2,1,0:T(4,128)(2,1)S(1)} %collective-permute-done.4.refs_2_) | copy-start | bytes 196612
  57.2 0.6 copy-start.6
  83.0 29.9 %copy-start = (bf16[1,64,16,1,640]{4,2,3,0,1:T(8,128)(2,1)}, bf16[1,64,16,1,640]{4,2,3,0,1:T(8,128)(2,1)S(1)}, u32[]{:S(2)}) copy-start(bf16[1,64,16,1,640]{4,2,3,0,1:T(8,128)(2,1)S(1)} %all-to-all-done.1) | copy-start | bytes 3932164
  83.0 18.6 %all-to-all-start = ((bf16[16,4,2176]{2,1,0:T(4,128)(2,1)}), bf16[16,4,2176]{2,1,0:T(4,128)(2,1)S(1)}, u32[]{:S(2)}, u32[]{:S(2)}) async-start(bf16[16,4,2176]{2,1,0:T(4,128)(2,1)} %pack.1), calls=%async_computation | async-start | bytes 557056 | tf_op jit(solution)/shard_map/all_to_all | solution.py:259
  88.7 27.5 %collective-permute-start.7 = (bf16[1024,640]{1,0:T(8,128)(2,1)S(1)}, bf16[1024,640]{1,0:T(8,128)(2,1)S(1)}, u32[]{:S(2)}, u32[]{:S(2)}) collective-permute-start(bf16[1024,640]{1,0:T(8,128)(2,1)S(1)} %bitcast.18), channel_id=1, source_target_pairs={{0,4},{4,0},{1,5},{5,1},{2,6},{6,2},{3,7},{7,3},{8,12},{12,8},{9,1... | collective-permute-start | bytes 3932168 | tf_op jit(solution)/shard_map/ppermute | solution.py:265
  101.6 11.3 %copy-start.1 = (bf16[16,4,2176]{2,1,0:T(4,128)(2,1)}, bf16[16,4,2176]{2,1,0:T(4,128)(2,1)S(1)}, u32[]{:S(2)}) copy-start(bf16[16,4,2176]{2,1,0:T(4,128)(2,1)S(1)} %all-to-all-done.sat_own.coef) | copy-start | bytes 835588
  101.6 22.4 %collective-permute-start.6 = (bf16[16,4,2176]{2,1,0:T(4,128)(2,1)S(1)}, bf16[16,4,2176]{2,1,0:T(4,128)(2,1)S(1)}, u32[]{:S(2)}, u32[]{:S(2)}) collective-permute-start(bf16[16,4,2176]{2,1,0:T(4,128)(2,1)S(1)} %all-to-all-done.sat_own.coef), channel_id=1, source_target_pairs={{0,4},{4,0},{1,5},{5,1},{2,6},{6,2},{3,7},{7,3},{8,12},{12,8},{9,1... | collective-permute-start | bytes 835592 | tf_op jit(solution)/shard_map/ppermute | solution.py:262
  116.3 1.1 copy-start.2
  124.0 0.7 copy-start.3

commit v4 on v3

--- a/solution.py
+++ b/solution.py
@@ -9,6 +9,7 @@
 
 
 LMAX = 2190
+LEAD = 10
 F32 = jnp.float32
 BF16 = jnp.bfloat16
 I32 = jnp.int32
@@ -53,7 +54,7 @@
 
     def position(slot_in_group):
         side = ((slot_in_group & 3) - y) & 3
-        return side * 16 + (slot_in_group >> 2)
+        return side * 16 + (((slot_in_group >> 2) - LEAD) & 15)
 
     pick = (position(own) == at).astype(F32).astype(BF16)
     out[:, 2048:2176] = jnp.concatenate(
@@ -143,37 +144,46 @@
         at += width
 
 
-def right_kernel(place, coef, own, right, terms, total):
+def roll_kernel(panel, out, here, sems):
+    rows = panel.shape[0]
+    count = sems.shape[1]
+    size = rows // count
+    inward, outward = [], []
+    for k in range(count):
+        to = pl.ds(k * size, size)
+        source = panel.at[pl.ds((rows // 16 * LEAD + k * size) % rows, size)]
+        inward.append(pltpu.make_async_copy(source, here.at[to], sems.at[0, k]))
+        outward.append(pltpu.make_async_copy(here.at[to], out.at[to], sems.at[1, k]))
+    for copy in inward:
+        copy.start()
+    for arrival, copy in zip(inward, outward):
+        arrival.wait()
+        copy.start()
+    for copy in outward:
+        copy.wait()
+
+
+def right_kernel(place, coef, own, right, own_here, sem):
     y, p, first, order = place[1], place[3], place[4], place[5]
     rows, half = own.shape
-    step = pl.program_id(0)
-
-    @pl.when(step == 0)
-    def _():
-        steps = terms.shape[0]
-        flat = coef[...].reshape(64, 128)
-        for k in range(steps):
-            index = iota((64, rows), 0)
-            source = (index & 60) + ((y - index) & 3)
-            mine = source == (iota((64, rows), 1) >> 4) + k * (rows // 16)
-            spread = ((iota((16, rows), 1) & 15) == iota((16, rows), 0)).astype(F32).astype(BF16)
-            lines = []
-            for c in range(4):
-                wide = dot(flat[:, c * 16 : (c + 1) * 16], spread, ((1,), (0,)))
-                lines.append(jnp.sum(jnp.where(mine, wide, 0.0), axis=0, keepdims=True))
-            lines.append(jnp.zeros((4, rows), F32))
-            terms[k] = jnp.concatenate(lines, axis=0).astype(BF16)
-        total[...] = jnp.zeros(total.shape, F32)
-
-    total[...] += dot(terms[step], own[...], ((1,), (0,)))
-
-    @pl.when(step == pl.num_programs(0) - 1)
-    def _():
-        product = total[...] * live_row(first, p, half)
-        degree = first + p + order + 2 * iota((1, half), 1)
-        sign = 1.0 - 2.0 * (degree & 1).astype(F32)
-        right[0] = product[0:1] + sign * product[1:2]
-        right[1] = product[2:3] + sign * product[3:4]
+    fetch = pltpu.make_async_copy(own, own_here, sem)
+    fetch.start()
+    flat = coef[...].reshape(64, 128)
+    index = iota((64, rows), 0)
+    source = (index & 60) + ((y - index) & 3)
+    mine = source == (iota((64, rows), 1) >> 4)
+    spread = ((iota((16, rows), 1) & 15) == iota((16, rows), 0)).astype(F32).astype(BF16)
+    lines = []
+    for c in range(4):
+        wide = dot(flat[:, c * 16 : (c + 1) * 16], spread, ((1,), (0,)))
+        lines.append(jnp.sum(jnp.where(mine, wide, 0.0), axis=0, keepdims=True))
+    lines.append(jnp.zeros((4, rows), F32))
+    terms = jnp.concatenate(lines, axis=0).astype(BF16)
+    fetch.wait()
+    product = dot(terms, own_here[...], ((1,), (0,))) * live_row(first, p, half)
+    sign = 1.0 - 2.0 * ((first + p + order + 2 * iota((1, half), 1)) & 1).astype(F32)
+    right[0] = product[0:1] + sign * product[1:2]
+    right[1] = product[2:3] + sign * product[3:4]
 
 
 def add_kernel(place, sat_own, sat_other, normals, out):
@@ -206,7 +216,23 @@
     z, y = lat_index // 4, lat_index % 4
     smem = whole(pltpu.SMEM)
 
-    arrived = lax.all_to_all(panel, "lat", split_axis=1, concat_axis=2, tiled=True)
+    flat = (panel.shape[1] * row_count, half)
+    rolled = pl.pallas_call(
+        roll_kernel,
+        out_shape=jax.ShapeDtypeStruct(flat, panel.dtype),
+        in_specs=[whole(pl.ANY)],
+        out_specs=whole(pl.ANY),
+        scratch_shapes=[pltpu.VMEM(flat, panel.dtype), pltpu.SemaphoreType.DMA((2, 8))],
+        name="roll",
+    )(panel.reshape(flat)).reshape(panel.shape)
+    arrived = lax.all_to_all(
+        rolled,
+        "lat",
+        split_axis=1,
+        concat_axis=2,
+        axis_index_groups=[[(4 * LEAD + k) % 64 for k in range(64)]],
+        tiled=True,
+    )
 
     own_order = lax.dynamic_slice_in_dim(order_value[0], lat_index, 1, 0)[0]
     place = jnp.stack([z, y, orb_index, parity, deg_first[0, 0], own_order]).astype(I32)
@@ -233,7 +259,7 @@
         out_specs=(whole(),) * 2,
         name="weights",
     )
-    plus, minus = weights(row_weight)
+    plus, minus = weights(jnp.roll(row_weight, -4 * LEAD * row_count, axis=1))
 
     width = packed.shape[1]
     blocks = packed.reshape(4, 16, width)
@@ -255,7 +281,7 @@
         name="pack",
     )
     packed = pack(*groups)
-    columns = [[a * 4 + b for a in range(16)] for b in range(4)]
+    columns = [[(LEAD + a) % 16 * 4 + b for a in range(16)] for b in range(4)]
     sat_own = lax.all_to_all(
         packed, "lat", split_axis=0, concat_axis=0, axis_index_groups=columns, tiled=True
     )
@@ -279,18 +305,17 @@
         name="gram",
     )
     normals = gram_call(place, own_panel, other_panel, plus, minus)
-    chunk = row_all // 4
     right_call = pl.pallas_call(
         right_kernel,
-        grid=(4,),
+        grid=(1,),
         out_shape=jax.ShapeDtypeStruct((2, 1, half), F32),
         in_specs=[
             smem,
             pl.BlockSpec((16, 4, 128), lambda i: (0, 0, 16)),
-            pl.BlockSpec((chunk, half), lambda i: (i, 0)),
+            whole(pl.ANY),
         ],
         out_specs=pl.BlockSpec((2, 1, half), lambda i: (0, 0, 0)),
-        scratch_shapes=[pltpu.VMEM((4, 8, chunk), BF16), pltpu.VMEM((8, half), F32)],
+        scratch_shapes=[pltpu.VMEM((row_all, half), BF16), pltpu.SemaphoreType.DMA],
         name="right",
     )
     right = right_call(place, sat_own, own_panel)

time: 128 us -> 126 us (0.984)
  waiting for transfers between devices: 40 us -> 33.3 us
  starting transfers between devices: 56.9 us -> 60.3 us
  Pallas kernels: 19.4 us -> 21.1 us
    all_to_all x1, waiting for transfers between devices: 23.5 us -> 17.1 us  [shards(): lax.all_to_all(rolled, 'lat', split_axis=1, concat_axis=2, axis_index_gro...]
    all_to_all x1, starting transfers between devices: 5.72 us -> 11.5 us  [shards(): lax.all_to_all(packed, 'lat', split_axis=0, concat_axis=0, axis_index_gro...]
    ppermute x1, starting transfers between devices: 9.38 us -> 4.9 us  [shards(): sat_other = lax.ppermute(sat_own, 'ord', [(0, 1), (1, 0)])]
    pallas_call x1 -> x2, Pallas kernels: 1.86 us -> 4.08 us  [the longest x1 2.2 us: shards(): pl.pallas_call(roll_kernel, out_shape=jax.ShapeDtypeStruct(flat, panel.dt...]
  transfers between devices with their start and end apart: 10 -> 10, of which waited for: 6 -> 6; matrix products, arithmetic and copies ran while one was open for 5% -> 5% of each run, Pallas kernels for 14% -> 13%
where the time goes in v4:
time: 126 us
  starting transfers between devices  60.3 us (48%)
  waiting for transfers between devices  33.3 us (26%)
  Pallas kernels  21.1 us (17%)
  local copies, waits for them, and re-layouts  7.36 us (6%)
  other arithmetic  1.9 us (2%)
  between operations  1.53 us (1%)
    all_to_all x1, starting transfers between devices, shards(): lax.all_to_all(rolled, 'lat', split_axis=1, concat_axis=2, axis_index_gro...  20.5 us
    all_to_all x1, waiting for transfers between devices, shards(): lax.all_to_all(rolled, 'lat', split_axis=1, concat_axis=2, axis_index_gro...  17.1 us
    all_to_all x1, starting transfers between devices, shards(): lax.all_to_all(packed, 'lat', split_axis=0, concat_axis=0, axis_index_gro...  11.5 us
    ppermute x3, starting transfers between devices, shards(): groups.append(lax.ppermute(sides[:, :, f * 512:(f + 1) * 512], 'orb', ring))  9.31 us
    ppermute x3, starting transfers between devices, shards(): sides.append(lax.ppermute(blocks[e], 'lat', ring))  9.29 us
    all_to_all x1, waiting for transfers between devices, shards(): lax.all_to_all(packed, 'lat', split_axis=0, concat_axis=0, axis_index_gro...  7.76 us
    pallas_call x1, Pallas kernels, shards(): normals = gram_call(place, own_panel, other_panel, plus, minus)  6.7 us
    ppermute x1, starting transfers between devices, shards(): sat_other = lax.ppermute(sat_own, 'ord', [(0, 1), (1, 0)])  4.9 us
  transfers between devices with their start and end apart: 10, of which 6 were waited for; matrix products, arithmetic and copies ran while one was open for 5% of the time, Pallas kernels for 13%

profile of v4, /device:TPU:1, one launch (start us, length us, event | category | flops | bytes accessed | tf_op | source)
XLA Modules:
  0.0 125.6 jit_solution(15707321221978632973)
XLA Ops:
  0.6 2.2 %roll.1 = bf16[1024,640]{1,0:T(8,128)(2,1)} custom-call(bf16[1024,640]{1,0:T(8,128)(2,1)} %bitcast.25), custom_call_target="tpu_custom_call" | custom-call | tf_op jit(solution)/shard_map/roll/pallas_call | solution.py:220
  2.8 0.0 copy-start.7
  2.9 0.0 copy-start.8
  2.9 20.5 %all-to-all-start.1 = ((bf16[1,64,16,1,640]{4,2,3,0,1:T(8,128)(2,1)}), bf16[1,64,16,1,640]{4,2,3,0,1:T(8,128)(2,1)S(1)}, u32[]{:S(2)}, u32[]{:S(2)}) async-start(bf16[1,64,16,1,640]{4,2,3,0,1:T(8,128)(2,1)} %bitcast.24), calls=%async_computation.1 | async-start | bytes 2621440 | tf_op jit(solution)/shard_map/all_to_all | solution.py:228
  24.1 0.0 copy-done.7
  24.1 0.1 constant_dynamic-slice_fusion
  24.2 0.7 reshape.38.weight
  24.9 0.0 copy-done.8
  24.9 0.7 constant_dynamic-slice_fusion.1
  25.5 1.4 %stack.31.place = s32[6]{0:T(128)} concatenate(s32[1]{0:T(128)} %bitcast, s32[1]{0:T(128)} %bitcast.1, s32[1]{0:T(128)} %bitcast.2, s32[1]{0:T(128)} %bitcast.3, s32[1]{0:T(128)} %bitcast.19, s32[1]{0:T(128)} %bitcast.5), dimensions={0} | concatenate | bytes 48 | tf_op jit(solution)/shard_map/stack | solution.py:238
  26.9 3.7 %prepare.1 = bf16[64,2176]{1,0:T(8,128)(2,1)} custom-call(s32[6]{0:T(128)} %stack.31.place, bf16[2,16,4320]{2,1,0:T(8,128)(2,1)} %anomaly.1, f32[32,1]{1,0:T(8,128)} %reshape.38.weight, s32[1,64]{1,0:T(1,128)} %order.1, bf16[256,256]{1,0:T(8,128)(2,1)} %rows.1, s32[1,256]{1,0:T(1,128)} %bitcast.30), custom_call_target="tpu_custom_call" | custom-call | tf_op jit(solution)/shard_map/prepare/pallas_call | solution.py:240
  30.6 1.0 slice_bitcast_fusion
  31.6 4.3 %collective-permute-start.2 = (bf16[16,2176]{1,0:T(8,128)(2,1)S(1)}, bf16[16,2176]{1,0:T(8,128)(2,1)S(1)}, u32[]{:S(2)}, u32[]{:S(2)}) collective-permute-start(bf16[16,2176]{1,0:T(8,128)(2,1)S(1)} %get-tuple-element.11), channel_id=1, source_target_pairs={{0,24},{8,0},{16,8},{24,16},{32,56},{40,32},{48,40},{56,48},{64,88... | collective-permute-start | bytes 208904 | tf_op jit(solution)/shard_map/ppermute | solution.py:269
  35.9 2.5 %collective-permute-start.1 = (bf16[16,2176]{1,0:T(8,128)(2,1)S(1)}, bf16[16,2176]{1,0:T(8,128)(2,1)S(1)}, u32[]{:S(2)}, u32[]{:S(2)}) collective-permute-start(bf16[16,2176]{1,0:T(8,128)(2,1)S(1)} %get-tuple-element.12), channel_id=1, source_target_pairs={{0,16},{8,24},{16,0},{24,8},{32,48},{40,56},{48,32},{56,40},{64,80... | collective-permute-start | bytes 208904 | tf_op jit(solution)/shard_map/ppermute | solution.py:269
  38.4 2.5 %collective-permute-start = (bf16[16,2176]{1,0:T(8,128)(2,1)S(1)}, bf16[16,2176]{1,0:T(8,128)(2,1)S(1)}, u32[]{:S(2)}, u32[]{:S(2)}) collective-permute-start(bf16[16,2176]{1,0:T(8,128)(2,1)S(1)} %get-tuple-element.13), channel_id=1, source_target_pairs={{0,8},{8,16},{16,24},{24,0},{32,40},{40,48},{48,56},{56,32},{64,72... | collective-permute-start | bytes 208904 | tf_op jit(solution)/shard_map/ppermute | solution.py:269
  40.9 0.1 copy.17
  41.0 0.0 collective-permute-done.2
  41.0 0.1 copy.20
  41.1 1.6 %collective-permute-done.1 = bf16[16,2176]{1,0:T(8,128)(2,1)S(1)} collective-permute-done((bf16[16,2176]{1,0:T(8,128)(2,1)S(1)}, bf16[16,2176]{1,0:T(8,128)(2,1)S(1)}, u32[]{:S(2)}, u32[]{:S(2)}) %collective-permute-start.1) | collective-permute-done | bytes 69664 | tf_op jit(solution)/shard_map/ppermute | solution.py:269
  42.7 0.1 copy.19
  42.8 2.8 %collective-permute-done = bf16[16,2176]{1,0:T(8,128)(2,1)S(1)} collective-permute-done((bf16[16,2176]{1,0:T(8,128)(2,1)S(1)}, bf16[16,2176]{1,0:T(8,128)(2,1)S(1)}, u32[]{:S(2)}, u32[]{:S(2)}) %collective-permute-start) | collective-permute-done | bytes 69664 | tf_op jit(solution)/shard_map/ppermute | solution.py:269
  45.6 0.1 copy.18
  45.7 0.7 pad_maximum_fusion
  46.4 0.0 slice-start
  46.4 0.0 slice-start.1
  46.4 0.7 fusion
  47.1 4.4 %collective-permute-start.5 = (bf16[16,4,512]{2,1,0:T(4,128)(2,1)S(1)}, bf16[16,4,512]{2,1,0:T(4,128)(2,1)S(1)}, u32[]{:S(2)}, u32[]{:S(2)}) collective-permute-start(bf16[16,4,512]{2,1,0:T(4,128)(2,1)S(1)} %get-tuple-element.6), channel_id=1, source_target_pairs={{0,3},{1,0},{2,1},{3,2},{4,7},{5,4},{6,5},{7,6},{8,11},{9,8},{10,9... | collective-permute-start | bytes 196616 | tf_op jit(solution)/shard_map/ppermute | solution.py:274
  51.5 2.4 %collective-permute-start.4 = (bf16[16,4,512]{2,1,0:T(4,128)(2,1)S(1)}, bf16[16,4,512]{2,1,0:T(4,128)(2,1)S(1)}, u32[]{:S(2)}, u32[]{:S(2)}) collective-permute-start(bf16[16,4,512]{2,1,0:T(4,128)(2,1)S(1)} %get-tuple-element.7), channel_id=1, source_target_pairs={{0,2},{1,3},{2,0},{3,1},{4,6},{5,7},{6,4},{7,5},{8,10},{9,11},{10,... | collective-permute-start | bytes 196616 | tf_op jit(solution)/shard_map/ppermute | solution.py:274
  53.9 2.5 %collective-permute-start.3 = (bf16[16,4,512]{2,1,0:T(4,128)(2,1)S(1)}, bf16[16,4,512]{2,1,0:T(4,128)(2,1)S(1)}, u32[]{:S(2)}, u32[]{:S(2)}) collective-permute-start(bf16[16,4,512]{2,1,0:T(4,128)(2,1)S(1)} %get-tuple-element.8), channel_id=1, source_target_pairs={{0,1},{1,2},{2,3},{3,0},{4,5},{5,6},{6,7},{7,4},{8,9},{9,10},{10,1... | collective-permute-start | bytes 196616 | tf_op jit(solution)/shard_map/ppermute | solution.py:274
  56.5 0.6 pad_maximum_fusion.1.refs_4_
  57.1 0.0 collective-permute-done.5.refs_3_
  57.1 0.0 copy-start.4
  57.1 1.2 collective-permute-done.4.refs_2_
  58.3 0.0 copy-start.5
  58.3 2.8 %collective-permute-done.3.refs_1_ = bf16[16,4,512]{2,1,0:T(4,128)(2,1)S(1)} collective-permute-done((bf16[16,4,512]{2,1,0:T(4,128)(2,1)S(1)}, bf16[16,4,512]{2,1,0:T(4,128)(2,1)S(1)}, u32[]{:S(2)}, u32[]{:S(2)}) %collective-permute-start.3) | collective-permute-done | bytes 65568 | tf_op jit(solution)/shard_map/ppermute | solution.py:274
  61.2 0.0 copy-start.6
  61.2 0.0 copy-done.4
  61.2 0.0 copy-done.5
  61.2 0.6 copy-done.6
  61.8 1.7 %pack.1 = bf16[16,4,2176]{2,1,0:T(4,128)(2,1)} custom-call(bf16[16,4,512]{2,1,0:T(4,128)(2,1)} %get-tuple-element.9.refs_0_, bf16[16,4,512]{2,1,0:T(4,128)(2,1)} %copy-done.6, bf16[16,4,512]{2,1,0:T(4,128)(2,1)} %copy-done.5, bf16[16,4,512]{2,1,0:T(4,128)(2,1)} %copy-done.4, bf16[16,4,128]{2,1,0:T(4,128)(2,1)} %pad_maximum_fusion.1.refs_4_), custom_call_target="tpu_custom_call" | custom-call | tf_op jit(solution)/shard_map/pack/pallas_call | solution.py:283
  63.5 17.1 %all-to-all-done.1 = bf16[1,64,16,1,640]{4,2,3,0,1:T(8,128)(2,1)S(1)} async-done(((bf16[1,64,16,1,640]{4,2,3,0,1:T(8,128)(2,1)}), bf16[1,64,16,1,640]{4,2,3,0,1:T(8,128)(2,1)S(1)}, u32[]{:S(2)}, u32[]{:S(2)}) %all-to-all-start.1) | async-done | bytes 1310752 | tf_op jit(solution)/shard_map/all_to_all | solution.py:228
  80.6 0.0 copy-start
  80.6 11.5 %all-to-all-start = ((bf16[16,4,2176]{2,1,0:T(4,128)(2,1)}), bf16[16,4,2176]{2,1,0:T(4,128)(2,1)S(1)}, u32[]{:S(2)}, u32[]{:S(2)}) async-start(bf16[16,4,2176]{2,1,0:T(4,128)(2,1)} %pack.1), calls=%async_computation | async-start | bytes 557056 | tf_op jit(solution)/shard_map/all_to_all | solution.py:285
  92.1 4.7 %collective-permute-start.7 = (bf16[1024,640]{1,0:T(8,128)(2,1)S(1)}, bf16[1024,640]{1,0:T(8,128)(2,1)S(1)}, u32[]{:S(2)}, u32[]{:S(2)}) collective-permute-start(bf16[1024,640]{1,0:T(8,128)(2,1)S(1)} %bitcast.21), channel_id=1, source_target_pairs={{0,4},{4,0},{1,5},{5,1},{2,6},{6,2},{3,7},{7,3},{8,12},{12,8},{9,1... | collective-permute-start | bytes 3932168 | tf_op jit(solution)/shard_map/ppermute | solution.py:291
  96.8 7.8 %all-to-all-done.sat_own.coef = bf16[16,4,2176]{2,1,0:T(4,128)(2,1)S(1)} async-done(((bf16[16,4,2176]{2,1,0:T(4,128)(2,1)}), bf16[16,4,2176]{2,1,0:T(4,128)(2,1)S(1)}, u32[]{:S(2)}, u32[]{:S(2)}) %all-to-all-start) | async-done | bytes 278560 | tf_op jit(solution)/shard_map/all_to_all | solution.py:285
  104.6 0.0 copy-start.1
  104.6 4.9 %collective-permute-start.6 = (bf16[16,4,2176]{2,1,0:T(4,128)(2,1)S(1)}, bf16[16,4,2176]{2,1,0:T(4,128)(2,1)S(1)}, u32[]{:S(2)}, u32[]{:S(2)}) collective-permute-start(bf16[16,4,2176]{2,1,0:T(4,128)(2,1)S(1)} %all-to-all-done.sat_own.coef), channel_id=1, source_target_pairs={{0,4},{4,0},{1,5},{5,1},{2,6},{6,2},{3,7},{7,3},{8,12},{12,8},{9,1... | collective-permute-start | bytes 835592 | tf_op jit(solution)/shard_map/ppermute | solution.py:288
  109.5 0.0 slice-done
  109.5 0.0 slice-done.1
  109.5 0.6 pad_maximum_fusion.2.weight
  110.1 1.9 %weights.1 = (f32[1024,128]{1,0:T(8,128)}, f32[1024,128]{1,0:T(8,128)}) custom-call(f32[2,1024]{1,0:T(2,128)} %pad_maximum_fusion.2.weight), custom_call_target="tpu_custom_call" | custom-call | tf_op jit(solution)/shard_map/weights/pallas_call | solution.py:262
  112.0 0.0 copy-done
  112.0 0.0 copy-done.1
  112.0 2.9 %right.1 = f32[2,1,640]{2,1,0:T(1,128)} custom-call(s32[6]{0:T(128)} %stack.31.place, bf16[16,4,2176]{2,1,0:T(4,128)(2,1)} %copy-done.1, bf16[1024,640]{1,0:T(8,128)(2,1)} %bitcast.22), custom_call_target="tpu_custom_call" | custom-call | tf_op jit(solution)/shard_map/right/pallas_call | solution.py:321
  115.0 0.0 collective-permute-done.7.other
  115.0 0.0 copy-start.2
  115.0 1.1 copy-done.2
  116.1 6.7 %gram.1.normals = f32[640,2,640]{2,1,0:T(2,128)} custom-call(s32[6]{0:T(128)} %stack.31.place, bf16[1024,640]{1,0:T(8,128)(2,1)} %bitcast.23, bf16[1024,640]{1,0:T(8,128)(2,1)} %copy-done.2, f32[1024,128]{1,0:T(8,128)} %get-tuple-element.4.plus, f32[1024,128]{1,0:T(8,128)} %get-tuple-element.5.minus), custom_call_target="tpu_custom_call" | custom-call | tf_op jit(solution)/shard_map/gram/pallas_call | solution.py:307
  122.8 0.0 collective-permute-done.6.sat_other
  122.8 0.0 copy-start.3
  122.8 0.7 copy-done.3
  123.5 2.1 %add.15 = f32[640,2,640]{2,1,0:T(2,128)} custom-call(s32[6]{0:T(128)} %stack.31.place, bf16[16,4,2176]{2,1,0:T(4,128)(2,1)} %copy-done.1, bf16[16,4,2176]{2,1,0:T(4,128)(2,1)} %copy-done.3, f32[640,2,640]{2,1,0:T(2,128)} %gram.1.normals), custom_call_target="tpu_custom_call", output_to_operand_aliasing={{}: (3, {})} | custom-call | tf_op jit(solution)/shard_map/add/pallas_call | solution.py:324
Async XLA Ops:
  2.8 21.2 %copy-start.7 = (f32[2,1024]{1,0:T(2,128)S(1)}, f32[2,1024]{1,0:T(2,128)}, u32[]{:S(2)}) copy-start(f32[2,1024]{1,0:T(2,128)} %param.8) | copy-start | bytes 24580
  2.9 22.0 %copy-start.8 = (s32[1,64]{1,0:T(1,128)S(1)}, s32[1,64]{1,0:T(1,128)}, u32[]{:S(2)}) copy-start(s32[1,64]{1,0:T(1,128)} %order.1) | copy-start | bytes 772
  2.9 77.7 %all-to-all-start.1 = ((bf16[1,64,16,1,640]{4,2,3,0,1:T(8,128)(2,1)}), bf16[1,64,16,1,640]{4,2,3,0,1:T(8,128)(2,1)S(1)}, u32[]{:S(2)}, u32[]{:S(2)}) async-start(bf16[1,64,16,1,640]{4,2,3,0,1:T(8,128)(2,1)} %bitcast.24), calls=%async_computation.1 | async-start | bytes 2621440 | tf_op jit(solution)/shard_map/all_to_all | solution.py:228
  31.6 9.4 %collective-permute-start.2 = (bf16[16,2176]{1,0:T(8,128)(2,1)S(1)}, bf16[16,2176]{1,0:T(8,128)(2,1)S(1)}, u32[]{:S(2)}, u32[]{:S(2)}) collective-permute-start(bf16[16,2176]{1,0:T(8,128)(2,1)S(1)} %get-tuple-element.11), channel_id=1, source_target_pairs={{0,24},{8,0},{16,8},{24,16},{32,56},{40,32},{48,40},{56,48},{64,88... | collective-permute-start | bytes 208904 | tf_op jit(solution)/shard_map/ppermute | solution.py:269
  35.9 6.9 %collective-permute-start.1 = (bf16[16,2176]{1,0:T(8,128)(2,1)S(1)}, bf16[16,2176]{1,0:T(8,128)(2,1)S(1)}, u32[]{:S(2)}, u32[]{:S(2)}) collective-permute-start(bf16[16,2176]{1,0:T(8,128)(2,1)S(1)} %get-tuple-element.12), channel_id=1, source_target_pairs={{0,16},{8,24},{16,0},{24,8},{32,48},{40,56},{48,32},{56,40},{64,80... | collective-permute-start | bytes 208904 | tf_op jit(solution)/shard_map/ppermute | solution.py:269
  38.4 7.3 %collective-permute-start = (bf16[16,2176]{1,0:T(8,128)(2,1)S(1)}, bf16[16,2176]{1,0:T(8,128)(2,1)S(1)}, u32[]{:S(2)}, u32[]{:S(2)}) collective-permute-start(bf16[16,2176]{1,0:T(8,128)(2,1)S(1)} %get-tuple-element.13), channel_id=1, source_target_pairs={{0,8},{8,16},{16,24},{24,0},{32,40},{40,48},{48,56},{56,32},{64,72... | collective-permute-start | bytes 208904 | tf_op jit(solution)/shard_map/ppermute | solution.py:269
  46.4 63.1 %slice-start = ((f32[2,1024]{1,0:T(2,128)}), f32[2,384]{1,0:T(2,128)S(1)}, s32[]{:S(2)}) async-start(f32[2,1024]{1,0:T(2,128)} %param.8), calls=%async_computation.2 | async-start | bytes 6144 | tf_op jit(solution)/shard_map/jit(_roll_static)/slice | solution.py:262
  46.4 63.1 %slice-start.1 = ((f32[2,1024]{1,0:T(2,128)}), f32[2,640]{1,0:T(2,128)S(1)}, s32[]{:S(2)}) async-start(f32[2,1024]{1,0:T(2,128)} %param.8), calls=%async_computation.3 | async-start | bytes 10240 | tf_op jit(solution)/shard_map/jit(_roll_static)/slice | solution.py:262
  47.1 10.0 %collective-permute-start.5 = (bf16[16,4,512]{2,1,0:T(4,128)(2,1)S(1)}, bf16[16,4,512]{2,1,0:T(4,128)(2,1)S(1)}, u32[]{:S(2)}, u32[]{:S(2)}) collective-permute-start(bf16[16,4,512]{2,1,0:T(4,128)(2,1)S(1)} %get-tuple-element.6), channel_id=1, source_target_pairs={{0,3},{1,0},{2,1},{3,2},{4,7},{5,4},{6,5},{7,6},{8,11},{9,8},{10,9... | collective-permute-start | bytes 196616 | tf_op jit(solution)/shard_map/ppermute | solution.py:274
  51.5 6.8 %collective-permute-start.4 = (bf16[16,4,512]{2,1,0:T(4,128)(2,1)S(1)}, bf16[16,4,512]{2,1,0:T(4,128)(2,1)S(1)}, u32[]{:S(2)}, u32[]{:S(2)}) collective-permute-start(bf16[16,4,512]{2,1,0:T(4,128)(2,1)S(1)} %get-tuple-element.7), channel_id=1, source_target_pairs={{0,2},{1,3},{2,0},{3,1},{4,6},{5,7},{6,4},{7,5},{8,10},{9,11},{10,... | collective-permute-start | bytes 196616 | tf_op jit(solution)/shard_map/ppermute | solution.py:274
  53.9 7.2 %collective-permute-start.3 = (bf16[16,4,512]{2,1,0:T(4,128)(2,1)S(1)}, bf16[16,4,512]{2,1,0:T(4,128)(2,1)S(1)}, u32[]{:S(2)}, u32[]{:S(2)}) collective-permute-start(bf16[16,4,512]{2,1,0:T(4,128)(2,1)S(1)} %get-tuple-element.8), channel_id=1, source_target_pairs={{0,1},{1,2},{2,3},{3,0},{4,5},{5,6},{6,7},{7,4},{8,9},{9,10},{10,1... | collective-permute-start | bytes 196616 | tf_op jit(solution)/shard_map/ppermute | solution.py:274
  57.1 4.1 %copy-start.4 = (bf16[16,4,512]{2,1,0:T(4,128)(2,1)}, bf16[16,4,512]{2,1,0:T(4,128)(2,1)S(1)}, u32[]{:S(2)}) copy-start(bf16[16,4,512]{2,1,0:T(4,128)(2,1)S(1)} %collective-permute-done.5.refs_3_) | copy-start | bytes 196612
  58.3 2.8 %copy-start.5 = (bf16[16,4,512]{2,1,0:T(4,128)(2,1)}, bf16[16,4,512]{2,1,0:T(4,128)(2,1)S(1)}, u32[]{:S(2)}) copy-start(bf16[16,4,512]{2,1,0:T(4,128)(2,1)S(1)} %collective-permute-done.4.refs_2_) | copy-start | bytes 196612
  61.2 0.6 copy-start.6
  80.6 31.4 %copy-start = (bf16[1,64,16,1,640]{4,2,3,0,1:T(8,128)(2,1)}, bf16[1,64,16,1,640]{4,2,3,0,1:T(8,128)(2,1)S(1)}, u32[]{:S(2)}) copy-start(bf16[1,64,16,1,640]{4,2,3,0,1:T(8,128)(2,1)S(1)} %all-to-all-done.1) | copy-start | bytes 3932164
  80.6 24.0 %all-to-all-start = ((bf16[16,4,2176]{2,1,0:T(4,128)(2,1)}), bf16[16,4,2176]{2,1,0:T(4,128)(2,1)S(1)}, u32[]{:S(2)}, u32[]{:S(2)}) async-start(bf16[16,4,2176]{2,1,0:T(4,128)(2,1)} %pack.1), calls=%async_computation | async-start | bytes 557056 | tf_op jit(solution)/shard_map/all_to_all | solution.py:285
  92.1 22.9 %collective-permute-start.7 = (bf16[1024,640]{1,0:T(8,128)(2,1)S(1)}, bf16[1024,640]{1,0:T(8,128)(2,1)S(1)}, u32[]{:S(2)}, u32[]{:S(2)}) collective-permute-start(bf16[1024,640]{1,0:T(8,128)(2,1)S(1)} %bitcast.21), channel_id=1, source_target_pairs={{0,4},{4,0},{1,5},{5,1},{2,6},{6,2},{3,7},{7,3},{8,12},{12,8},{9,1... | collective-permute-start | bytes 3932168 | tf_op jit(solution)/shard_map/ppermute | solution.py:291
  104.6 7.4 %copy-start.1 = (bf16[16,4,2176]{2,1,0:T(4,128)(2,1)}, bf16[16,4,2176]{2,1,0:T(4,128)(2,1)S(1)}, u32[]{:S(2)}) copy-start(bf16[16,4,2176]{2,1,0:T(4,128)(2,1)S(1)} %all-to-all-done.sat_own.coef) | copy-start | bytes 835588
  104.6 18.1 %collective-permute-start.6 = (bf16[16,4,2176]{2,1,0:T(4,128)(2,1)S(1)}, bf16[16,4,2176]{2,1,0:T(4,128)(2,1)S(1)}, u32[]{:S(2)}, u32[]{:S(2)}) collective-permute-start(bf16[16,4,2176]{2,1,0:T(4,128)(2,1)S(1)} %all-to-all-done.sat_own.coef), channel_id=1, source_target_pairs={{0,4},{4,0},{1,5},{5,1},{2,6},{6,2},{3,7},{7,3},{8,12},{12,8},{9,1... | collective-permute-start | bytes 835592 | tf_op jit(solution)/shard_map/ppermute | solution.py:288
  115.0 1.1 copy-start.2
  122.8 0.7 copy-start.3

commit v5 on v4

--- a/solution.py
+++ b/solution.py
@@ -10,6 +10,7 @@
 
 LMAX = 2190
 LEAD = 10
+SAT_LEAD = 10
 F32 = jnp.float32
 BF16 = jnp.bfloat16
 I32 = jnp.int32
@@ -54,7 +55,7 @@
 
     def position(slot_in_group):
         side = ((slot_in_group & 3) - y) & 3
-        return side * 16 + (((slot_in_group >> 2) - LEAD) & 15)
+        return side * 16 + (((slot_in_group >> 2) - SAT_LEAD) & 15)
 
     pick = (position(own) == at).astype(F32).astype(BF16)
     out[:, 2048:2176] = jnp.concatenate(
@@ -91,19 +92,11 @@
     return (first + 2 * iota((1, half), 1) + parity <= LMAX).astype(F32)
 
 
-def gram_kernel(place, own, other, plus, minus, out, own_here, other_here, scaled, stage, sems):
+def gram_kernel(place, own, other, plus, minus, out, corner, scaled, stage, sems):
     p, first = place[3], place[4]
     _, half = own.shape
     tiles = half // 128
-    fetch = [
-        pltpu.make_async_copy(own, own_here, sems.at[0]),
-        pltpu.make_async_copy(other, other_here, sems.at[1]),
-    ]
-    for copy in fetch:
-        copy.start()
-    scaled_as = ((own_here, plus, p), (other_here, minus, 1 - p))
-    for (here, weight, parity), copy in zip(scaled_as, fetch):
-        copy.wait()
+    for here, weight, parity in ((own, plus, p), (other, minus, 1 - p)):
         live = live_row(first, parity, half)
         scale = jnp.concatenate([weight[...]] * tiles, axis=1)
         scaled[:, pl.ds(pl.multiple_of(parity * half, 128), half)] = (
@@ -113,7 +106,7 @@
     sent = []
     for k, (low, high) in enumerate(((0, 3), (3, tiles))):
         cols = slice(low * 128, high * 128)
-        left = (own_here[:, cols].astype(F32) * live[:, cols]).astype(BF16).T
+        left = (own[:, cols].astype(F32) * live[:, cols]).astype(BF16).T
         block = dot(left, scaled[...], ((1,), (0,)))
         count = (high - low) * 128
         for q in range(2):
@@ -121,13 +114,16 @@
                 at = q * half + tile * 128
                 where = pl.ds((tile * half + low * 128) * 2 + q, count, stride=2)
                 stage[where, :] = block[:, at : at + 128]
+        if low == 0:
+            for q in range(2):
+                corner[:, q * 128 : (q + 1) * 128] = block[:128, q * half : q * half + 128]
         pairs = stage.reshape(tiles, half, 2, 128)
         span = pl.ds(low * 128, count)
         for tile in range(tiles):
             copy = pltpu.make_async_copy(
                 pairs.at[tile, span],
                 out.at[span, :, pl.ds(tile * 128, 128)],
-                sems.at[2 + k * tiles + tile],
+                sems.at[k * tiles + tile],
             )
             copy.start()
             sent.append(copy)
@@ -163,30 +159,26 @@
         copy.wait()
 
 
-def right_kernel(place, coef, own, right, own_here, sem):
+def right_kernel(place, sat, own, right):
     y, p, first, order = place[1], place[3], place[4], place[5]
     rows, half = own.shape
-    fetch = pltpu.make_async_copy(own, own_here, sem)
-    fetch.start()
-    flat = coef[...].reshape(64, 128)
-    index = iota((64, rows), 0)
-    source = (index & 60) + ((y - index) & 3)
-    mine = source == (iota((64, rows), 1) >> 4)
-    spread = ((iota((16, rows), 1) & 15) == iota((16, rows), 0)).astype(F32).astype(BF16)
-    lines = []
-    for c in range(4):
-        wide = dot(flat[:, c * 16 : (c + 1) * 16], spread, ((1,), (0,)))
-        lines.append(jnp.sum(jnp.where(mine, wide, 0.0), axis=0, keepdims=True))
-    lines.append(jnp.zeros((4, rows), F32))
-    terms = jnp.concatenate(lines, axis=0).astype(BF16)
-    fetch.wait()
-    product = dot(terms, own_here[...], ((1,), (0,))) * live_row(first, p, half)
+    flat = sat[:, :, 2048:].reshape(64, 128)
+    index = iota((64, 1), 0)
+    z = (index >> 2) + (SAT_LEAD - LEAD)
+    source = (z & 15) * 4 + ((y - index) & 3)
+    mine = (source == (iota((64, rows), 1) >> 4)).astype(F32).astype(BF16)
+    wide = dot(flat[:, :64], mine, ((0,), (0,)))
+    keep = (iota((64, rows), 0) & 15) == (iota((64, rows), 1) & 15)
+    narrow = jnp.where(keep, wide, 0.0).astype(BF16)
+    line = ((iota((8, 64), 1) >> 4) == iota((8, 64), 0)).astype(F32).astype(BF16)
+    terms = dot(line, narrow, ((1,), (0,))).astype(BF16)
+    product = dot(terms, own[...], ((1,), (0,))) * live_row(first, p, half)
     sign = 1.0 - 2.0 * ((first + p + order + 2 * iota((1, half), 1)) & 1).astype(F32)
     right[0] = product[0:1] + sign * product[1:2]
     right[1] = product[2:3] + sign * product[3:4]
 
 
-def add_kernel(place, sat_own, sat_other, normals, out):
+def add_kernel(place, sat_own, sat_other, corner, normals, out, stage, sem):
     p, first = place[3], place[4]
     parts = []
     for sat in (sat_own, sat_other):
@@ -197,13 +189,20 @@
     gram = dot(own, block, ((0,), (0,)))
     live_left = (first + 2 * iota((128, 128), 0) + p <= LMAX).astype(F32)
     for q in range(2):
+        at = slice(q * 128, (q + 1) * 128)
         live_top = (first + 2 * iota((128, 128), 1) + q <= LMAX).astype(F32)
-        add = gram[:, q * 128 : (q + 1) * 128] * (live_left * live_top)
-        out[:, q, :] = normals[:, q, :] + add
+        stage[:, q, :] = corner[:, at] + gram[:, at] * (live_left * live_top)
+    copy = pltpu.make_async_copy(stage, out.at[pl.ds(0, 128), :, pl.ds(0, 128)], sem)
+    copy.start()
+    copy.wait()
 
 
 def whole(memory_space=pltpu.VMEM):
     return pl.BlockSpec(memory_space=memory_space)
+
+
+def near(array):
+    return pltpu.with_memory_space_constraint(array, pltpu.VMEM)
 
 
 def shards(anomaly, row_weight, panel, order_value, deg_first, sat_rows, sat_slot):
@@ -281,7 +280,7 @@
         name="pack",
     )
     packed = pack(*groups)
-    columns = [[(LEAD + a) % 16 * 4 + b for a in range(16)] for b in range(4)]
+    columns = [[(SAT_LEAD + a) % 16 * 4 + b for a in range(16)] for b in range(4)]
     sat_own = lax.all_to_all(
         packed, "lat", split_axis=0, concat_axis=0, axis_index_groups=columns, tiled=True
     )
@@ -292,44 +291,37 @@
     lines = half * 2 * (half // 128)
     gram_call = pl.pallas_call(
         gram_kernel,
-        out_shape=jax.ShapeDtypeStruct((half, 2, half), F32),
-        in_specs=[smem, whole(pl.ANY), whole(pl.ANY), whole(), whole()],
-        out_specs=whole(pl.ANY),
+        out_shape=(
+            jax.ShapeDtypeStruct((half, 2, half), F32),
+            pltpu.VMEM((128, 256), F32),
+        ),
+        in_specs=[smem] + [whole()] * 4,
+        out_specs=(whole(pl.ANY), whole()),
         scratch_shapes=[
-            pltpu.VMEM((row_all, half), BF16),
-            pltpu.VMEM((row_all, half), BF16),
             pltpu.VMEM((row_all, 2 * half), BF16),
             pltpu.VMEM((lines, 128), F32),
-            pltpu.SemaphoreType.DMA((2 + 2 * (half // 128),)),
+            pltpu.SemaphoreType.DMA((2 * (half // 128),)),
         ],
         name="gram",
     )
-    normals = gram_call(place, own_panel, other_panel, plus, minus)
+    normals, corner = gram_call(place, near(own_panel), near(other_panel), plus, minus)
     right_call = pl.pallas_call(
         right_kernel,
-        grid=(1,),
         out_shape=jax.ShapeDtypeStruct((2, 1, half), F32),
-        in_specs=[
-            smem,
-            pl.BlockSpec((16, 4, 128), lambda i: (0, 0, 16)),
-            whole(pl.ANY),
-        ],
-        out_specs=pl.BlockSpec((2, 1, half), lambda i: (0, 0, 0)),
-        scratch_shapes=[pltpu.VMEM((row_all, half), BF16), pltpu.SemaphoreType.DMA],
+        in_specs=[smem] + [whole()] * 2,
+        out_specs=whole(),
         name="right",
     )
-    right = right_call(place, sat_own, own_panel)
-    corner = pl.BlockSpec((128, 2, 128), lambda i: (0, 0, 0))
-    sat_spec = pl.BlockSpec((16, 4, width), lambda i: (0, 0, 0))
+    right = right_call(place, near(sat_own), near(own_panel))
     normals = pl.pallas_call(
         add_kernel,
-        grid=(1,),
         out_shape=jax.ShapeDtypeStruct((half, 2, half), F32),
-        in_specs=[smem, sat_spec, sat_spec, corner],
-        out_specs=corner,
-        input_output_aliases={3: 0},
+        in_specs=[smem] + [whole()] * 3 + [whole(pl.ANY)],
+        out_specs=whole(pl.ANY),
+        scratch_shapes=[pltpu.VMEM((128, 2, 128), F32), pltpu.SemaphoreType.DMA],
+        input_output_aliases={4: 0},
         name="add",
-    )(place, sat_own, sat_other, normals)
+    )(place, near(sat_own), near(sat_other), near(corner), normals)
     return (normals[None, None, None], right[None, None])
 
 

time: 126 us -> 127 us (level)
  local copies, waits for them, and re-layouts: 7.36 us -> 10 us
  Pallas kernels: 21.1 us -> 18.6 us
    unnamed x18, local copies, waits for them, and re-layouts: 2.4 us -> 5.4 us
    pallas_call x3, Pallas kernels: 11.7 us -> 9.19 us  [the longest x1 5.7 us: shards(): gram_call(place, near(own_panel), near(other_panel), plus, minus)]
  transfers between devices with their start and end apart: 10 -> 10, of which waited for: 6 -> 6; matrix products, arithmetic and copies ran while one was open for 5% -> 5% of each run, Pallas kernels for 13% -> 12%
where the time goes in v5:
time: 127 us; the launch traced here: 126 us
  starting transfers between devices  60.3 us (47%)
  waiting for transfers between devices  33.6 us (26%)
  Pallas kernels  18.6 us (15%)
  local copies, waits for them, and re-layouts  10 us (8%)
  other arithmetic  1.91 us (2%)
  between operations  1.5 us (1%)
    all_to_all x1, starting transfers between devices, shards(): lax.all_to_all(rolled, 'lat', split_axis=1, concat_axis=2, axis_index_gro...  20.5 us
    all_to_all x1, waiting for transfers between devices, shards(): lax.all_to_all(rolled, 'lat', split_axis=1, concat_axis=2, axis_index_gro...  17.4 us
    all_to_all x1, starting transfers between devices, shards(): lax.all_to_all(packed, 'lat', split_axis=0, concat_axis=0, axis_index_gro...  11.5 us
    ppermute x3, starting transfers between devices, shards(): groups.append(lax.ppermute(sides[:, :, f * 512:(f + 1) * 512], 'orb', ring))  9.31 us
    ppermute x3, starting transfers between devices, shards(): sides.append(lax.ppermute(blocks[e], 'lat', ring))  9.29 us
    all_to_all x1, waiting for transfers between devices, shards(): lax.all_to_all(packed, 'lat', split_axis=0, concat_axis=0, axis_index_gro...  7.76 us
    pallas_call x1, Pallas kernels, shards(): gram_call(place, near(own_panel), near(other_panel), plus, minus)  5.7 us
    unnamed x18, local copies, waits for them, and re-layouts  5.4 us
  transfers between devices with their start and end apart: 10, of which 6 were waited for; matrix products, arithmetic and copies ran while one was open for 5% of the time, Pallas kernels for 12%

profile of v5, /device:TPU:1, one launch (start us, length us, event | category | flops | bytes accessed | tf_op | source)
XLA Modules:
  0.0 126.0 jit_solution(11052347560611968757)
XLA Ops:
  0.6 2.2 %roll.1 = bf16[1024,640]{1,0:T(8,128)(2,1)} custom-call(bf16[1024,640]{1,0:T(8,128)(2,1)} %bitcast.25), custom_call_target="tpu_custom_call" | custom-call | tf_op jit(solution)/shard_map/roll/pallas_call | solution.py:219
  2.8 0.0 copy-start.7
  2.9 0.0 copy-start.8
  2.9 20.5 %all-to-all-start.1 = ((bf16[1,64,16,1,640]{4,2,3,0,1:T(8,128)(2,1)}), bf16[1,64,16,1,640]{4,2,3,0,1:T(8,128)(2,1)S(1)}, u32[]{:S(2)}, u32[]{:S(2)}) async-start(bf16[1,64,16,1,640]{4,2,3,0,1:T(8,128)(2,1)} %bitcast.23), calls=%async_computation.1 | async-start | bytes 2621440 | tf_op jit(solution)/shard_map/all_to_all | solution.py:227
  24.1 0.0 copy-done.7
  24.1 0.1 constant_dynamic-slice_fusion
  24.2 0.7 reshape.38.weight
  24.9 0.0 copy-done.8
  24.9 0.6 constant_dynamic-slice_fusion.1
  25.4 1.2 stack.31.place
  26.6 3.7 %prepare.1 = bf16[64,2176]{1,0:T(8,128)(2,1)} custom-call(s32[6]{0:T(128)} %stack.31.place, bf16[2,16,4320]{2,1,0:T(8,128)(2,1)} %anomaly.1, f32[32,1]{1,0:T(8,128)} %reshape.38.weight, s32[1,64]{1,0:T(1,128)} %order.1, bf16[256,256]{1,0:T(8,128)(2,1)} %rows.1, s32[1,256]{1,0:T(1,128)} %bitcast.30), custom_call_target="tpu_custom_call" | custom-call | tf_op jit(solution)/shard_map/prepare/pallas_call | solution.py:239
  30.3 1.0 slice_bitcast_fusion
  31.3 4.3 %collective-permute-start.2 = (bf16[16,2176]{1,0:T(8,128)(2,1)S(1)}, bf16[16,2176]{1,0:T(8,128)(2,1)S(1)}, u32[]{:S(2)}, u32[]{:S(2)}) collective-permute-start(bf16[16,2176]{1,0:T(8,128)(2,1)S(1)} %get-tuple-element.15), channel_id=1, source_target_pairs={{0,24},{8,0},{16,8},{24,16},{32,56},{40,32},{48,40},{56,48},{64,88... | collective-permute-start | bytes 208904 | tf_op jit(solution)/shard_map/ppermute | solution.py:268
  35.6 2.5 %collective-permute-start.1 = (bf16[16,2176]{1,0:T(8,128)(2,1)S(1)}, bf16[16,2176]{1,0:T(8,128)(2,1)S(1)}, u32[]{:S(2)}, u32[]{:S(2)}) collective-permute-start(bf16[16,2176]{1,0:T(8,128)(2,1)S(1)} %get-tuple-element.16), channel_id=1, source_target_pairs={{0,16},{8,24},{16,0},{24,8},{32,48},{40,56},{48,32},{56,40},{64,80... | collective-permute-start | bytes 208904 | tf_op jit(solution)/shard_map/ppermute | solution.py:268
  38.1 2.5 %collective-permute-start = (bf16[16,2176]{1,0:T(8,128)(2,1)S(1)}, bf16[16,2176]{1,0:T(8,128)(2,1)S(1)}, u32[]{:S(2)}, u32[]{:S(2)}) collective-permute-start(bf16[16,2176]{1,0:T(8,128)(2,1)S(1)} %get-tuple-element.17), channel_id=1, source_target_pairs={{0,8},{8,16},{16,24},{24,0},{32,40},{40,48},{48,56},{56,32},{64,72... | collective-permute-start | bytes 208904 | tf_op jit(solution)/shard_map/ppermute | solution.py:268
  40.6 0.1 copy.17
  40.7 0.0 collective-permute-done.2
  40.7 0.1 copy.20
  40.8 1.6 %collective-permute-done.1 = bf16[16,2176]{1,0:T(8,128)(2,1)S(1)} collective-permute-done((bf16[16,2176]{1,0:T(8,128)(2,1)S(1)}, bf16[16,2176]{1,0:T(8,128)(2,1)S(1)}, u32[]{:S(2)}, u32[]{:S(2)}) %collective-permute-start.1) | collective-permute-done | bytes 69664 | tf_op jit(solution)/shard_map/ppermute | solution.py:268
  42.4 0.1 copy.19
  42.6 2.8 %collective-permute-done = bf16[16,2176]{1,0:T(8,128)(2,1)S(1)} collective-permute-done((bf16[16,2176]{1,0:T(8,128)(2,1)S(1)}, bf16[16,2176]{1,0:T(8,128)(2,1)S(1)}, u32[]{:S(2)}, u32[]{:S(2)}) %collective-permute-start) | collective-permute-done | bytes 69664 | tf_op jit(solution)/shard_map/ppermute | solution.py:268
  45.4 0.1 copy.18
  45.5 0.7 pad_maximum_fusion
  46.1 0.0 slice-start
  46.2 0.0 slice-start.1
  46.2 0.7 fusion
  46.9 4.4 %collective-permute-start.5 = (bf16[16,4,512]{2,1,0:T(4,128)(2,1)S(1)}, bf16[16,4,512]{2,1,0:T(4,128)(2,1)S(1)}, u32[]{:S(2)}, u32[]{:S(2)}) collective-permute-start(bf16[16,4,512]{2,1,0:T(4,128)(2,1)S(1)} %get-tuple-element.10), channel_id=1, source_target_pairs={{0,3},{1,0},{2,1},{3,2},{4,7},{5,4},{6,5},{7,6},{8,11},{9,8},{10,9... | collective-permute-start | bytes 196616 | tf_op jit(solution)/shard_map/ppermute | solution.py:273
  51.3 2.4 %collective-permute-start.4 = (bf16[16,4,512]{2,1,0:T(4,128)(2,1)S(1)}, bf16[16,4,512]{2,1,0:T(4,128)(2,1)S(1)}, u32[]{:S(2)}, u32[]{:S(2)}) collective-permute-start(bf16[16,4,512]{2,1,0:T(4,128)(2,1)S(1)} %get-tuple-element.11), channel_id=1, source_target_pairs={{0,2},{1,3},{2,0},{3,1},{4,6},{5,7},{6,4},{7,5},{8,10},{9,11},{10,... | collective-permute-start | bytes 196616 | tf_op jit(solution)/shard_map/ppermute | solution.py:273
  53.7 2.5 %collective-permute-start.3 = (bf16[16,4,512]{2,1,0:T(4,128)(2,1)S(1)}, bf16[16,4,512]{2,1,0:T(4,128)(2,1)S(1)}, u32[]{:S(2)}, u32[]{:S(2)}) collective-permute-start(bf16[16,4,512]{2,1,0:T(4,128)(2,1)S(1)} %get-tuple-element.12), channel_id=1, source_target_pairs={{0,1},{1,2},{2,3},{3,0},{4,5},{5,6},{6,7},{7,4},{8,9},{9,10},{10,1... | collective-permute-start | bytes 196616 | tf_op jit(solution)/shard_map/ppermute | solution.py:273
  56.2 0.7 pad_maximum_fusion.1.refs_4_
  56.9 0.0 collective-permute-done.5.refs_3_
  56.9 0.0 copy-start.4
  56.9 1.2 collective-permute-done.4.refs_2_
  58.1 0.0 copy-start.5
  58.1 2.8 %collective-permute-done.3.refs_1_ = bf16[16,4,512]{2,1,0:T(4,128)(2,1)S(1)} collective-permute-done((bf16[16,4,512]{2,1,0:T(4,128)(2,1)S(1)}, bf16[16,4,512]{2,1,0:T(4,128)(2,1)S(1)}, u32[]{:S(2)}, u32[]{:S(2)}) %collective-permute-start.3) | collective-permute-done | bytes 65568 | tf_op jit(solution)/shard_map/ppermute | solution.py:273
  60.9 0.0 copy-start.6
  60.9 0.0 copy-done.4
  60.9 0.0 copy-done.5
  60.9 0.6 copy-done.6
  61.5 1.7 %pack.1 = bf16[16,4,2176]{2,1,0:T(4,128)(2,1)} custom-call(bf16[16,4,512]{2,1,0:T(4,128)(2,1)} %get-tuple-element.13.refs_0_, bf16[16,4,512]{2,1,0:T(4,128)(2,1)} %copy-done.6, bf16[16,4,512]{2,1,0:T(4,128)(2,1)} %copy-done.5, bf16[16,4,512]{2,1,0:T(4,128)(2,1)} %copy-done.4, bf16[16,4,128]{2,1,0:T(4,128)(2,1)} %pad_maximum_fusion.1.refs_4_), custom_call_target="tpu_custom_call" | custom-call | tf_op jit(solution)/shard_map/pack/pallas_call | solution.py:282
  63.2 17.4 %all-to-all-done.1 = bf16[1,64,16,1,640]{4,2,3,0,1:T(8,128)(2,1)S(1)} async-done(((bf16[1,64,16,1,640]{4,2,3,0,1:T(8,128)(2,1)}), bf16[1,64,16,1,640]{4,2,3,0,1:T(8,128)(2,1)S(1)}, u32[]{:S(2)}, u32[]{:S(2)}) %all-to-all-start.1) | async-done | bytes 1310752 | tf_op jit(solution)/shard_map/all_to_all | solution.py:227
  80.6 11.5 %all-to-all-start = ((bf16[16,4,2176]{2,1,0:T(4,128)(2,1)}), bf16[16,4,2176]{2,1,0:T(4,128)(2,1)S(1)}, u32[]{:S(2)}, u32[]{:S(2)}) async-start(bf16[16,4,2176]{2,1,0:T(4,128)(2,1)} %pack.1), calls=%async_computation | async-start | bytes 557056 | tf_op jit(solution)/shard_map/all_to_all | solution.py:284
  92.1 4.7 %collective-permute-start.7 = (bf16[1024,640]{1,0:T(8,128)(2,1)S(1)}, bf16[1024,640]{1,0:T(8,128)(2,1)S(1)}, u32[]{:S(2)}, u32[]{:S(2)}) collective-permute-start(bf16[1024,640]{1,0:T(8,128)(2,1)S(1)} %bitcast.20), channel_id=1, source_target_pairs={{0,4},{4,0},{1,5},{5,1},{2,6},{6,2},{3,7},{7,3},{8,12},{12,8},{9,1... | collective-permute-start | bytes 3932168 | tf_op jit(solution)/shard_map/ppermute | solution.py:290
  96.8 7.8 %all-to-all-done.sat_own.sat = bf16[16,4,2176]{2,1,0:T(4,128)(2,1)S(1)} async-done(((bf16[16,4,2176]{2,1,0:T(4,128)(2,1)}), bf16[16,4,2176]{2,1,0:T(4,128)(2,1)S(1)}, u32[]{:S(2)}, u32[]{:S(2)}) %all-to-all-start) | async-done | bytes 278560 | tf_op jit(solution)/shard_map/all_to_all | solution.py:284
  104.6 4.9 %collective-permute-start.6 = (bf16[16,4,2176]{2,1,0:T(4,128)(2,1)S(1)}, bf16[16,4,2176]{2,1,0:T(4,128)(2,1)S(1)}, u32[]{:S(2)}, u32[]{:S(2)}) collective-permute-start(bf16[16,4,2176]{2,1,0:T(4,128)(2,1)S(1)} %all-to-all-done.sat_own.sat), channel_id=1, source_target_pairs={{0,4},{4,0},{1,5},{5,1},{2,6},{6,2},{3,7},{7,3},{8,12},{12,8},{9,1... | collective-permute-start | bytes 835592 | tf_op jit(solution)/shard_map/ppermute | solution.py:287
  109.5 0.0 slice-done
  109.5 0.0 slice-done.1
  109.5 0.6 pad_maximum_fusion.2.weight
  110.1 1.9 %weights.1 = (f32[1024,128]{1,0:T(8,128)}, f32[1024,128]{1,0:T(8,128)}) custom-call(f32[2,1024]{1,0:T(2,128)} %pad_maximum_fusion.2.weight), custom_call_target="tpu_custom_call" | custom-call | tf_op jit(solution)/shard_map/weights/pallas_call | solution.py:261
  112.0 1.8 %right.1 = f32[2,1,640]{2,1,0:T(1,128)} custom-call(s32[6]{0:T(128)} %stack.31.place, bf16[16,4,2176]{2,1,0:T(4,128)(2,1)S(1)} %all-to-all-done.sat_own.sat, bf16[1024,640]{1,0:T(8,128)(2,1)S(1)} %bitcast.21), custom_call_target="tpu_custom_call" | custom-call | tf_op jit(solution)/shard_map/right/pallas_call | solution.py:315
  113.9 0.0 copy-start
  113.9 1.1 copy-done
  114.9 0.0 collective-permute-done.7.other
  114.9 0.0 copy-start.2
  114.9 1.1 copy-done.2
  116.0 0.0 copy-start.1
  116.0 1.3 %copy-done.1 = bf16[1,64,16,1,640]{4,2,3,0,1:T(8,128)(2,1)S(1)} copy-done((bf16[1,64,16,1,640]{4,2,3,0,1:T(8,128)(2,1)S(1)}, bf16[1,64,16,1,640]{4,2,3,0,1:T(8,128)(2,1)}, u32[]{:S(2)}) %copy-start.1) | copy-done | bytes 1310744
  117.3 0.0 copy-start.3
  117.3 1.3 %copy-done.3 = bf16[1024,640]{1,0:T(8,128)(2,1)S(1)} copy-done((bf16[1024,640]{1,0:T(8,128)(2,1)S(1)}, bf16[1024,640]{1,0:T(8,128)(2,1)}, u32[]{:S(2)}) %copy-start.3) | copy-done | bytes 1310744
  118.6 5.7 %gram.1 = (f32[640,2,640]{2,1,0:T(2,128)}, f32[128,256]{1,0:T(8,128)S(1)}) custom-call(s32[6]{0:T(128)} %stack.31.place, bf16[1024,640]{1,0:T(8,128)(2,1)S(1)} %bitcast.22, bf16[1024,640]{1,0:T(8,128)(2,1)S(1)} %copy-done.3, f32[1024,128]{1,0:T(8,128)} %get-tuple-element.6.plus, f32[1024,128]{1,0:T(8,128)} %get-tuple-element.7.minus), custom_call_target="tpu_custom_call" | custom-call | tf_op jit(solution)/shard_map/gram/pallas_call | solution.py:307
  124.3 0.0 collective-permute-done.6.sat_other
  124.3 1.7 %add.15 = f32[640,2,640]{2,1,0:T(2,128)} custom-call(s32[6]{0:T(128)} %stack.31.place, bf16[16,4,2176]{2,1,0:T(4,128)(2,1)S(1)} %all-to-all-done.sat_own.sat, bf16[16,4,2176]{2,1,0:T(4,128)(2,1)S(1)} %collective-permute-done.6.sat_other, f32[128,256]{1,0:T(8,128)S(1)} %get-tuple-element.8.corner, ...), custom_call_target="tpu_custom_call", output_to_operand_aliasing={{}: (4, {})} | custom-call | tf_op jit(solution)/shard_map/add/pallas_call | solution.py:316
Async XLA Ops:
  2.8 21.2 %copy-start.7 = (f32[2,1024]{1,0:T(2,128)S(1)}, f32[2,1024]{1,0:T(2,128)}, u32[]{:S(2)}) copy-start(f32[2,1024]{1,0:T(2,128)} %param.8) | copy-start | bytes 24580
  2.9 22.0 %copy-start.8 = (s32[1,64]{1,0:T(1,128)S(1)}, s32[1,64]{1,0:T(1,128)}, u32[]{:S(2)}) copy-start(s32[1,64]{1,0:T(1,128)} %order.1) | copy-start | bytes 772
  2.9 77.7 %all-to-all-start.1 = ((bf16[1,64,16,1,640]{4,2,3,0,1:T(8,128)(2,1)}), bf16[1,64,16,1,640]{4,2,3,0,1:T(8,128)(2,1)S(1)}, u32[]{:S(2)}, u32[]{:S(2)}) async-start(bf16[1,64,16,1,640]{4,2,3,0,1:T(8,128)(2,1)} %bitcast.23), calls=%async_computation.1 | async-start | bytes 2621440 | tf_op jit(solution)/shard_map/all_to_all | solution.py:227
  31.3 9.4 %collective-permute-start.2 = (bf16[16,2176]{1,0:T(8,128)(2,1)S(1)}, bf16[16,2176]{1,0:T(8,128)(2,1)S(1)}, u32[]{:S(2)}, u32[]{:S(2)}) collective-permute-start(bf16[16,2176]{1,0:T(8,128)(2,1)S(1)} %get-tuple-element.15), channel_id=1, source_target_pairs={{0,24},{8,0},{16,8},{24,16},{32,56},{40,32},{48,40},{56,48},{64,88... | collective-permute-start | bytes 208904 | tf_op jit(solution)/shard_map/ppermute | solution.py:268
  35.6 6.9 %collective-permute-start.1 = (bf16[16,2176]{1,0:T(8,128)(2,1)S(1)}, bf16[16,2176]{1,0:T(8,128)(2,1)S(1)}, u32[]{:S(2)}, u32[]{:S(2)}) collective-permute-start(bf16[16,2176]{1,0:T(8,128)(2,1)S(1)} %get-tuple-element.16), channel_id=1, source_target_pairs={{0,16},{8,24},{16,0},{24,8},{32,48},{40,56},{48,32},{56,40},{64,80... | collective-permute-start | bytes 208904 | tf_op jit(solution)/shard_map/ppermute | solution.py:268
  38.1 7.3 %collective-permute-start = (bf16[16,2176]{1,0:T(8,128)(2,1)S(1)}, bf16[16,2176]{1,0:T(8,128)(2,1)S(1)}, u32[]{:S(2)}, u32[]{:S(2)}) collective-permute-start(bf16[16,2176]{1,0:T(8,128)(2,1)S(1)} %get-tuple-element.17), channel_id=1, source_target_pairs={{0,8},{8,16},{16,24},{24,0},{32,40},{40,48},{48,56},{56,32},{64,72... | collective-permute-start | bytes 208904 | tf_op jit(solution)/shard_map/ppermute | solution.py:268
  46.1 63.4 %slice-start = ((f32[2,1024]{1,0:T(2,128)}), f32[2,384]{1,0:T(2,128)S(1)}, s32[]{:S(2)}) async-start(f32[2,1024]{1,0:T(2,128)} %param.8), calls=%async_computation.2 | async-start | bytes 6144 | tf_op jit(solution)/shard_map/jit(_roll_static)/slice | solution.py:261
  46.2 63.4 %slice-start.1 = ((f32[2,1024]{1,0:T(2,128)}), f32[2,640]{1,0:T(2,128)S(1)}, s32[]{:S(2)}) async-start(f32[2,1024]{1,0:T(2,128)} %param.8), calls=%async_computation.3 | async-start | bytes 10240 | tf_op jit(solution)/shard_map/jit(_roll_static)/slice | solution.py:261
  46.9 10.0 %collective-permute-start.5 = (bf16[16,4,512]{2,1,0:T(4,128)(2,1)S(1)}, bf16[16,4,512]{2,1,0:T(4,128)(2,1)S(1)}, u32[]{:S(2)}, u32[]{:S(2)}) collective-permute-start(bf16[16,4,512]{2,1,0:T(4,128)(2,1)S(1)} %get-tuple-element.10), channel_id=1, source_target_pairs={{0,3},{1,0},{2,1},{3,2},{4,7},{5,4},{6,5},{7,6},{8,11},{9,8},{10,9... | collective-permute-start | bytes 196616 | tf_op jit(solution)/shard_map/ppermute | solution.py:273
  51.3 6.8 %collective-permute-start.4 = (bf16[16,4,512]{2,1,0:T(4,128)(2,1)S(1)}, bf16[16,4,512]{2,1,0:T(4,128)(2,1)S(1)}, u32[]{:S(2)}, u32[]{:S(2)}) collective-permute-start(bf16[16,4,512]{2,1,0:T(4,128)(2,1)S(1)} %get-tuple-element.11), channel_id=1, source_target_pairs={{0,2},{1,3},{2,0},{3,1},{4,6},{5,7},{6,4},{7,5},{8,10},{9,11},{10,... | collective-permute-start | bytes 196616 | tf_op jit(solution)/shard_map/ppermute | solution.py:273
  53.7 7.2 %collective-permute-start.3 = (bf16[16,4,512]{2,1,0:T(4,128)(2,1)S(1)}, bf16[16,4,512]{2,1,0:T(4,128)(2,1)S(1)}, u32[]{:S(2)}, u32[]{:S(2)}) collective-permute-start(bf16[16,4,512]{2,1,0:T(4,128)(2,1)S(1)} %get-tuple-element.12), channel_id=1, source_target_pairs={{0,1},{1,2},{2,3},{3,0},{4,5},{5,6},{6,7},{7,4},{8,9},{9,10},{10,1... | collective-permute-start | bytes 196616 | tf_op jit(solution)/shard_map/ppermute | solution.py:273
  56.9 4.0 %copy-start.4 = (bf16[16,4,512]{2,1,0:T(4,128)(2,1)}, bf16[16,4,512]{2,1,0:T(4,128)(2,1)S(1)}, u32[]{:S(2)}) copy-start(bf16[16,4,512]{2,1,0:T(4,128)(2,1)S(1)} %collective-permute-done.5.refs_3_) | copy-start | bytes 196612
  58.1 2.8 %copy-start.5 = (bf16[16,4,512]{2,1,0:T(4,128)(2,1)}, bf16[16,4,512]{2,1,0:T(4,128)(2,1)S(1)}, u32[]{:S(2)}) copy-start(bf16[16,4,512]{2,1,0:T(4,128)(2,1)S(1)} %collective-permute-done.4.refs_2_) | copy-start | bytes 196612
  60.9 0.6 copy-start.6
  80.6 24.0 %all-to-all-start = ((bf16[16,4,2176]{2,1,0:T(4,128)(2,1)}), bf16[16,4,2176]{2,1,0:T(4,128)(2,1)S(1)}, u32[]{:S(2)}, u32[]{:S(2)}) async-start(bf16[16,4,2176]{2,1,0:T(4,128)(2,1)} %pack.1), calls=%async_computation | async-start | bytes 557056 | tf_op jit(solution)/shard_map/all_to_all | solution.py:284
  92.1 22.8 %collective-permute-start.7 = (bf16[1024,640]{1,0:T(8,128)(2,1)S(1)}, bf16[1024,640]{1,0:T(8,128)(2,1)S(1)}, u32[]{:S(2)}, u32[]{:S(2)}) collective-permute-start(bf16[1024,640]{1,0:T(8,128)(2,1)S(1)} %bitcast.20), channel_id=1, source_target_pairs={{0,4},{4,0},{1,5},{5,1},{2,6},{6,2},{3,7},{7,3},{8,12},{12,8},{9,1... | collective-permute-start | bytes 3932168 | tf_op jit(solution)/shard_map/ppermute | solution.py:290
  104.6 19.7 %collective-permute-start.6 = (bf16[16,4,2176]{2,1,0:T(4,128)(2,1)S(1)}, bf16[16,4,2176]{2,1,0:T(4,128)(2,1)S(1)}, u32[]{:S(2)}, u32[]{:S(2)}) collective-permute-start(bf16[16,4,2176]{2,1,0:T(4,128)(2,1)S(1)} %all-to-all-done.sat_own.sat), channel_id=1, source_target_pairs={{0,4},{4,0},{1,5},{5,1},{2,6},{6,2},{3,7},{7,3},{8,12},{12,8},{9,1... | collective-permute-start | bytes 835592 | tf_op jit(solution)/shard_map/ppermute | solution.py:287
  113.9 1.1 copy-start
  114.9 1.1 copy-start.2
  116.0 1.3 %copy-start.1 = (bf16[1,64,16,1,640]{4,2,3,0,1:T(8,128)(2,1)S(1)}, bf16[1,64,16,1,640]{4,2,3,0,1:T(8,128)(2,1)}, u32[]{:S(2)}) copy-start(bf16[1,64,16,1,640]{4,2,3,0,1:T(8,128)(2,1)} %copy-done) | copy-start | bytes 3932164
  117.3 1.3 %copy-start.3 = (bf16[1024,640]{1,0:T(8,128)(2,1)S(1)}, bf16[1024,640]{1,0:T(8,128)(2,1)}, u32[]{:S(2)}) copy-start(bf16[1024,640]{1,0:T(8,128)(2,1)} %copy-done.2) | copy-start | bytes 3932164

commit v6 on v5

--- a/solution.py
+++ b/solution.py
@@ -159,7 +159,19 @@
         copy.wait()
 
 
-def right_kernel(place, sat, own, right):
+def sat_gram(place, sat):
+    p, first = place[3], place[4]
+    flat = sat[...].reshape(64, sat.shape[2])
+    block = jnp.concatenate([flat[:, c * 256 : (c + 1) * 256] for c in range(8)], axis=0)
+    own = jnp.where(p == 0, block[:, :128], block[:, 128:])
+    gram = dot(own, block, ((0,), (0,)))
+    left = (first + 2 * iota((128, 256), 0) + p <= LMAX).astype(F32)
+    column = iota((128, 256), 1)
+    top = (first + 2 * (column & 127) + (column >> 7) <= LMAX).astype(F32)
+    return gram * (left * top)
+
+
+def right_kernel(place, sat, own, corner, right, partial):
     y, p, first, order = place[1], place[3], place[4], place[5]
     rows, half = own.shape
     flat = sat[:, :, 2048:].reshape(64, 128)
@@ -176,25 +188,25 @@
     sign = 1.0 - 2.0 * ((first + p + order + 2 * iota((1, half), 1)) & 1).astype(F32)
     right[0] = product[0:1] + sign * product[1:2]
     right[1] = product[2:3] + sign * product[3:4]
-
-
-def add_kernel(place, sat_own, sat_other, corner, normals, out, stage, sem):
-    p, first = place[3], place[4]
-    parts = []
-    for sat in (sat_own, sat_other):
-        flat = sat[...].reshape(64, sat.shape[2])
-        parts += [flat[:, c * 256 : (c + 1) * 256] for c in range(8)]
-    block = jnp.concatenate(parts, axis=0)
-    own = jnp.where(p == 0, block[:, :128], block[:, 128:])
-    gram = dot(own, block, ((0,), (0,)))
-    live_left = (first + 2 * iota((128, 128), 0) + p <= LMAX).astype(F32)
+    partial[...] = corner[...] + sat_gram(place, sat)
+
+
+def add_kernel(place, sat, partial, right, normals, out, right_out, stage, sems):
+    first_copy = pltpu.make_async_copy(right, right_out, sems.at[0])
+    first_copy.start()
+    total = partial[...] + sat_gram(place, sat)
     for q in range(2):
-        at = slice(q * 128, (q + 1) * 128)
-        live_top = (first + 2 * iota((128, 128), 1) + q <= LMAX).astype(F32)
-        stage[:, q, :] = corner[:, at] + gram[:, at] * (live_left * live_top)
-    copy = pltpu.make_async_copy(stage, out.at[pl.ds(0, 128), :, pl.ds(0, 128)], sem)
-    copy.start()
-    copy.wait()
+        stage[:, q, :] = total[:, q * 128 : (q + 1) * 128]
+    copies = [first_copy]
+    for k in range(4):
+        span = pl.ds(k * 32, 32)
+        copy = pltpu.make_async_copy(
+            stage.at[span], out.at[span, :, pl.ds(0, 128)], sems.at[1 + k]
+        )
+        copy.start()
+        copies.append(copy)
+    for copy in copies:
+        copy.wait()
 
 
 def whole(memory_space=pltpu.VMEM):
@@ -307,21 +319,24 @@
     normals, corner = gram_call(place, near(own_panel), near(other_panel), plus, minus)
     right_call = pl.pallas_call(
         right_kernel,
-        out_shape=jax.ShapeDtypeStruct((2, 1, half), F32),
-        in_specs=[smem] + [whole()] * 2,
-        out_specs=whole(),
+        out_shape=(pltpu.VMEM((2, 1, half), F32), pltpu.VMEM((128, 256), F32)),
+        in_specs=[smem] + [whole()] * 3,
+        out_specs=(whole(),) * 2,
         name="right",
     )
-    right = right_call(place, near(sat_own), near(own_panel))
-    normals = pl.pallas_call(
+    right, partial = right_call(place, near(sat_own), near(own_panel), near(corner))
+    normals, right = pl.pallas_call(
         add_kernel,
-        out_shape=jax.ShapeDtypeStruct((half, 2, half), F32),
+        out_shape=(
+            jax.ShapeDtypeStruct((half, 2, half), F32),
+            jax.ShapeDtypeStruct((2, 1, half), F32),
+        ),
         in_specs=[smem] + [whole()] * 3 + [whole(pl.ANY)],
-        out_specs=whole(pl.ANY),
-        scratch_shapes=[pltpu.VMEM((128, 2, 128), F32), pltpu.SemaphoreType.DMA],
+        out_specs=(whole(pl.ANY),) * 2,
+        scratch_shapes=[pltpu.VMEM((128, 2, 128), F32), pltpu.SemaphoreType.DMA((5,))],
         input_output_aliases={4: 0},
         name="add",
-    )(place, near(sat_own), near(sat_other), near(corner), normals)
+    )(place, near(sat_other), near(partial), near(right), normals)
     return (normals[None, None, None], right[None, None])
 
 

time: 127 us -> 122 us (0.961)
  local copies, waits for them, and re-layouts: 10 us -> 5.44 us
  waiting for transfers between devices: 33.6 us -> 31.1 us
  starting transfers between devices: 60.3 us -> 62.7 us
    unnamed x18 -> x10, local copies, waits for them, and re-layouts: 5.4 us -> 0.64 us
    ppermute x3, waiting for transfers between devices: 4.04 us -> 1.58 us  [shards(): groups.append(lax.ppermute(sides[:, :, f * 512:(f + 1) * 512], 'orb', ring))]
    ppermute x3, waiting for transfers between devices: 4.45 us -> 2.18 us  [shards(): sides.append(lax.ppermute(blocks[e], 'lat', ring))]
    all_to_all x1, waiting for transfers between devices: 17.4 us -> 19.5 us  [shards(): lax.all_to_all(rolled, 'lat', split_axis=1, concat_axis=2, axis_index_gro...]
  transfers between devices with their start and end apart: 10 -> 10, of which waited for: 6 -> 4; matrix products, arithmetic and copies ran while one was open for 5% -> 6% of each run, Pallas kernels for 12% -> 12%
where the time goes in v6:
time: 122 us; the launch traced here: 121 us
  starting transfers between devices  62.7 us (51%)
  waiting for transfers between devices  31.1 us (25%)
  Pallas kernels  18.1 us (15%)
  local copies, waits for them, and re-layouts  5.44 us (4%)
  other arithmetic  1.9 us (2%)
  between operations  1.53 us (1%)
    all_to_all x1, starting transfers between devices, shards(): lax.all_to_all(rolled, 'lat', split_axis=1, concat_axis=2, axis_index_gro...  20.5 us
    all_to_all x1, waiting for transfers between devices, shards(): lax.all_to_all(rolled, 'lat', split_axis=1, concat_axis=2, axis_index_gro...  19.5 us
    all_to_all x1, starting transfers between devices, shards(): lax.all_to_all(packed, 'lat', split_axis=0, concat_axis=0, axis_index_gro...  11.5 us
    ppermute x3, starting transfers between devices, shards(): groups.append(lax.ppermute(sides[:, :, f * 512:(f + 1) * 512], 'orb', ring))  10.5 us
    ppermute x3, starting transfers between devices, shards(): sides.append(lax.ppermute(blocks[e], 'lat', ring))  10.5 us
    all_to_all x1, waiting for transfers between devices, shards(): lax.all_to_all(packed, 'lat', split_axis=0, concat_axis=0, axis_index_gro...  7.76 us
    pallas_call x1, Pallas kernels, shards(): gram_call(place, near(own_panel), near(other_panel), plus, minus)  5.7 us
    ppermute x1, starting transfers between devices, shards(): sat_other = lax.ppermute(sat_own, 'ord', [(0, 1), (1, 0)])  4.9 us
  transfers between devices with their start and end apart: 10, of which 4 were waited for; matrix products, arithmetic and copies ran while one was open for 6% of the time, Pallas kernels for 12%

profile of v6, /device:TPU:1, one launch (start us, length us, event | category | flops | bytes accessed | tf_op | source)
XLA Modules:
  0.0 120.8 jit_solution(15215733352430809605)
XLA Ops:
  0.6 2.2 %roll.1 = bf16[1024,640]{1,0:T(8,128)(2,1)} custom-call(bf16[1024,640]{1,0:T(8,128)(2,1)} %bitcast.25), custom_call_target="tpu_custom_call" | custom-call | tf_op jit(solution)/shard_map/roll/pallas_call | solution.py:231
  2.8 0.0 copy-start.3
  2.9 0.0 copy-start.4
  2.9 20.5 %all-to-all-start.1 = ((bf16[1,64,16,1,640]{4,2,3,0,1:T(8,128)(2,1)}), bf16[1,64,16,1,640]{4,2,3,0,1:T(8,128)(2,1)S(1)}, u32[]{:S(2)}, u32[]{:S(2)}) async-start(bf16[1,64,16,1,640]{4,2,3,0,1:T(8,128)(2,1)} %bitcast.23), calls=%async_computation.1 | async-start | bytes 2621440 | tf_op jit(solution)/shard_map/all_to_all | solution.py:239
  24.1 0.0 copy-done.3
  24.1 0.1 constant_dynamic-slice_fusion
  24.2 0.7 reshape.38.weight
  24.9 0.0 copy-done.4
  24.9 0.6 constant_dynamic-slice_fusion.1
  25.5 1.3 %stack.31.place = s32[6]{0:T(128)} concatenate(s32[1]{0:T(128)} %bitcast, s32[1]{0:T(128)} %bitcast.1, s32[1]{0:T(128)} %bitcast.2, s32[1]{0:T(128)} %bitcast.3, s32[1]{0:T(128)} %bitcast.19, s32[1]{0:T(128)} %bitcast.5), dimensions={0} | concatenate | bytes 48 | tf_op jit(solution)/shard_map/stack | solution.py:249
  26.7 3.7 %prepare.1 = bf16[64,2176]{1,0:T(8,128)(2,1)} custom-call(s32[6]{0:T(128)} %stack.31.place, bf16[2,16,4320]{2,1,0:T(8,128)(2,1)} %anomaly.1, f32[32,1]{1,0:T(8,128)} %reshape.38.weight, s32[1,64]{1,0:T(1,128)} %order.1, bf16[256,256]{1,0:T(8,128)(2,1)} %rows.1, s32[1,256]{1,0:T(1,128)} %bitcast.29), custom_call_target="tpu_custom_call" | custom-call | tf_op jit(solution)/shard_map/prepare/pallas_call | solution.py:251
  30.4 1.0 slice_bitcast_fusion
  31.4 3.1 %collective-permute-start = (bf16[16,2176]{1,0:T(8,128)(2,1)S(1)}, bf16[16,2176]{1,0:T(8,128)(2,1)S(1)}, u32[]{:S(2)}, u32[]{:S(2)}) collective-permute-start(bf16[16,2176]{1,0:T(8,128)(2,1)S(1)} %get-tuple-element.25), channel_id=1, source_target_pairs={{0,8},{8,16},{16,24},{24,0},{32,40},{40,48},{48,56},{56,32},{64,72... | collective-permute-start | bytes 208904 | tf_op jit(solution)/shard_map/ppermute | solution.py:280
  34.5 4.3 %collective-permute-start.1 = (bf16[16,2176]{1,0:T(8,128)(2,1)S(1)}, bf16[16,2176]{1,0:T(8,128)(2,1)S(1)}, u32[]{:S(2)}, u32[]{:S(2)}) collective-permute-start(bf16[16,2176]{1,0:T(8,128)(2,1)S(1)} %get-tuple-element.24), channel_id=1, source_target_pairs={{0,16},{8,24},{16,0},{24,8},{32,48},{40,56},{48,32},{56,40},{64,80... | collective-permute-start | bytes 208904 | tf_op jit(solution)/shard_map/ppermute | solution.py:280
  38.8 3.1 %collective-permute-start.2 = (bf16[16,2176]{1,0:T(8,128)(2,1)S(1)}, bf16[16,2176]{1,0:T(8,128)(2,1)S(1)}, u32[]{:S(2)}, u32[]{:S(2)}) collective-permute-start(bf16[16,2176]{1,0:T(8,128)(2,1)S(1)} %get-tuple-element.23), channel_id=1, source_target_pairs={{0,24},{8,0},{16,8},{24,16},{32,56},{40,32},{48,40},{56,48},{64,88... | collective-permute-start | bytes 208904 | tf_op jit(solution)/shard_map/ppermute | solution.py:280
  41.9 0.1 copy.17
  42.0 0.0 collective-permute-done
  42.1 0.1 copy.18
  42.2 0.0 collective-permute-done.1
  42.2 0.1 copy.19
  42.3 2.2 %collective-permute-done.2 = bf16[16,2176]{1,0:T(8,128)(2,1)S(1)} collective-permute-done((bf16[16,2176]{1,0:T(8,128)(2,1)S(1)}, bf16[16,2176]{1,0:T(8,128)(2,1)S(1)}, u32[]{:S(2)}, u32[]{:S(2)}) %collective-permute-start.2) | collective-permute-done | bytes 69664 | tf_op jit(solution)/shard_map/ppermute | solution.py:280
  44.5 0.1 copy.20
  44.6 0.7 pad_maximum_fusion
  45.2 0.0 slice-start
  45.3 0.0 slice-start.1
  45.3 0.7 fusion
  46.0 3.1 %collective-permute-start.3 = (bf16[16,4,512]{2,1,0:T(4,128)(2,1)S(1)}, bf16[16,4,512]{2,1,0:T(4,128)(2,1)S(1)}, u32[]{:S(2)}, u32[]{:S(2)}) collective-permute-start(bf16[16,4,512]{2,1,0:T(4,128)(2,1)S(1)} %get-tuple-element.20), channel_id=1, source_target_pairs={{0,1},{1,2},{2,3},{3,0},{4,5},{5,6},{6,7},{7,4},{8,9},{9,10},{10,1... | collective-permute-start | bytes 196616 | tf_op jit(solution)/shard_map/ppermute | solution.py:285
  49.1 4.4 %collective-permute-start.4 = (bf16[16,4,512]{2,1,0:T(4,128)(2,1)S(1)}, bf16[16,4,512]{2,1,0:T(4,128)(2,1)S(1)}, u32[]{:S(2)}, u32[]{:S(2)}) collective-permute-start(bf16[16,4,512]{2,1,0:T(4,128)(2,1)S(1)} %get-tuple-element.19), channel_id=1, source_target_pairs={{0,2},{1,3},{2,0},{3,1},{4,6},{5,7},{6,4},{7,5},{8,10},{9,11},{10,... | collective-permute-start | bytes 196616 | tf_op jit(solution)/shard_map/ppermute | solution.py:285
  53.5 3.1 %collective-permute-start.5 = (bf16[16,4,512]{2,1,0:T(4,128)(2,1)S(1)}, bf16[16,4,512]{2,1,0:T(4,128)(2,1)S(1)}, u32[]{:S(2)}, u32[]{:S(2)}) collective-permute-start(bf16[16,4,512]{2,1,0:T(4,128)(2,1)S(1)} %get-tuple-element.18), channel_id=1, source_target_pairs={{0,3},{1,0},{2,1},{3,2},{4,7},{5,4},{6,5},{7,6},{8,11},{9,8},{10,9... | collective-permute-start | bytes 196616 | tf_op jit(solution)/shard_map/ppermute | solution.py:285
  56.5 0.6 pad_maximum_fusion.1.refs_4_
  57.2 0.0 collective-permute-done.3.refs_1_
  57.2 0.0 copy-start
  57.2 0.0 collective-permute-done.4.refs_2_
  57.2 0.0 copy-start.1
  57.2 1.6 %collective-permute-done.5.refs_3_ = bf16[16,4,512]{2,1,0:T(4,128)(2,1)S(1)} collective-permute-done((bf16[16,4,512]{2,1,0:T(4,128)(2,1)S(1)}, bf16[16,4,512]{2,1,0:T(4,128)(2,1)S(1)}, u32[]{:S(2)}, u32[]{:S(2)}) %collective-permute-start.5) | collective-permute-done | bytes 65568 | tf_op jit(solution)/shard_map/ppermute | solution.py:285
  58.8 0.0 copy-start.2
  58.8 0.0 copy-done
  58.8 0.0 copy-done.1
  58.8 0.6 copy-done.2
  59.4 1.7 %pack.1 = bf16[16,4,2176]{2,1,0:T(4,128)(2,1)} custom-call(bf16[16,4,512]{2,1,0:T(4,128)(2,1)} %get-tuple-element.21.refs_0_, bf16[16,4,512]{2,1,0:T(4,128)(2,1)} %copy-done, bf16[16,4,512]{2,1,0:T(4,128)(2,1)} %copy-done.1, bf16[16,4,512]{2,1,0:T(4,128)(2,1)} %copy-done.2, bf16[16,4,128]{2,1,0:T(4,128)(2,1)} %pad_maximum_fusion.1.refs_4_), custom_call_target="tpu_custom_call" | custom-call | tf_op jit(solution)/shard_map/pack/pallas_call | solution.py:294
  61.1 19.5 %all-to-all-done.1 = bf16[1,64,16,1,640]{4,2,3,0,1:T(8,128)(2,1)S(1)} async-done(((bf16[1,64,16,1,640]{4,2,3,0,1:T(8,128)(2,1)}), bf16[1,64,16,1,640]{4,2,3,0,1:T(8,128)(2,1)S(1)}, u32[]{:S(2)}, u32[]{:S(2)}) %all-to-all-start.1) | async-done | bytes 1310752 | tf_op jit(solution)/shard_map/all_to_all | solution.py:239
  80.6 11.5 %all-to-all-start = ((bf16[16,4,2176]{2,1,0:T(4,128)(2,1)}), bf16[16,4,2176]{2,1,0:T(4,128)(2,1)S(1)}, u32[]{:S(2)}, u32[]{:S(2)}) async-start(bf16[16,4,2176]{2,1,0:T(4,128)(2,1)} %pack.1), calls=%async_computation | async-start | bytes 557056 | tf_op jit(solution)/shard_map/all_to_all | solution.py:296
  92.1 4.7 %collective-permute-start.7 = (bf16[1024,640]{1,0:T(8,128)(2,1)S(1)}, bf16[1024,640]{1,0:T(8,128)(2,1)S(1)}, u32[]{:S(2)}, u32[]{:S(2)}) collective-permute-start(bf16[1024,640]{1,0:T(8,128)(2,1)S(1)} %bitcast.20), channel_id=1, source_target_pairs={{0,4},{4,0},{1,5},{5,1},{2,6},{6,2},{3,7},{7,3},{8,12},{12,8},{9,1... | collective-permute-start | bytes 3932168 | tf_op jit(solution)/shard_map/ppermute | solution.py:302
  96.8 7.8 %all-to-all-done.sat = bf16[16,4,2176]{2,1,0:T(4,128)(2,1)S(1)} async-done(((bf16[16,4,2176]{2,1,0:T(4,128)(2,1)}), bf16[16,4,2176]{2,1,0:T(4,128)(2,1)S(1)}, u32[]{:S(2)}, u32[]{:S(2)}) %all-to-all-start) | async-done | bytes 278560 | tf_op jit(solution)/shard_map/all_to_all | solution.py:296
  104.6 4.9 %collective-permute-start.6 = (bf16[16,4,2176]{2,1,0:T(4,128)(2,1)S(1)}, bf16[16,4,2176]{2,1,0:T(4,128)(2,1)S(1)}, u32[]{:S(2)}, u32[]{:S(2)}) collective-permute-start(bf16[16,4,2176]{2,1,0:T(4,128)(2,1)S(1)} %all-to-all-done.sat), channel_id=1, source_target_pairs={{0,4},{4,0},{1,5},{5,1},{2,6},{6,2},{3,7},{7,3},{8,12},{12,8},{9,1... | collective-permute-start | bytes 835592 | tf_op jit(solution)/shard_map/ppermute | solution.py:299
  109.5 0.0 slice-done
  109.5 0.0 slice-done.1
  109.5 0.6 pad_maximum_fusion.2.weight
  110.1 1.9 %weights.1 = (f32[1024,128]{1,0:T(8,128)}, f32[1024,128]{1,0:T(8,128)}) custom-call(f32[2,1024]{1,0:T(2,128)} %pad_maximum_fusion.2.weight), custom_call_target="tpu_custom_call" | custom-call | tf_op jit(solution)/shard_map/weights/pallas_call | solution.py:273
  112.1 0.0 collective-permute-done.7.other
  112.1 5.7 %gram.1 = (f32[640,2,640]{2,1,0:T(2,128)}, f32[128,256]{1,0:T(8,128)S(1)}) custom-call(s32[6]{0:T(128)} %stack.31.place, bf16[1024,640]{1,0:T(8,128)(2,1)S(1)} %bitcast.21, bf16[1024,640]{1,0:T(8,128)(2,1)S(1)} %collective-permute-done.7.other, f32[1024,128]{1,0:T(8,128)} %get-tuple-element.10.plus, f32[1024,128]{1,0:T(8,128)} %get-tuple-element.11.minus), custom_call_target="tpu_custom_call" | custom-call | tf_op jit(solution)/shard_map/gram/pallas_call | solution.py:319
  117.8 1.3 %right.1 = (f32[2,1,640]{2,1,0:T(1,128)S(1)}, f32[128,256]{1,0:T(8,128)S(1)}) custom-call(s32[6]{0:T(128)} %stack.31.place, bf16[16,4,2176]{2,1,0:T(4,128)(2,1)S(1)} %all-to-all-done.sat, bf16[1024,640]{1,0:T(8,128)(2,1)S(1)} %bitcast.22, f32[128,256]{1,0:T(8,128)S(1)} %get-tuple-element.12.corner), custom_call_target="tpu_custom_call" | custom-call | tf_op jit(solution)/shard_map/right/pallas_call | solution.py:327
  119.1 0.0 collective-permute-done.6.sat
  119.1 1.6 %add.15 = (f32[640,2,640]{2,1,0:T(2,128)}, f32[2,1,640]{2,1,0:T(1,128)}) custom-call(s32[6]{0:T(128)} %stack.31.place, bf16[16,4,2176]{2,1,0:T(4,128)(2,1)S(1)} %collective-permute-done.6.sat, f32[128,256]{1,0:T(8,128)S(1)} %get-tuple-element.13.partial, f32[2,1,640]{2,1,0:T(1,128)S(1)} %get-tuple-element.14.right, ...), custom_call_target="tpu_custom_call", output_to_operand_aliasing={{0}: (4, {})} | custom-call | tf_op jit(solution)/shard_map/add/pallas_call | solution.py:328
Async XLA Ops:
  2.8 21.2 %copy-start.3 = (f32[2,1024]{1,0:T(2,128)S(1)}, f32[2,1024]{1,0:T(2,128)}, u32[]{:S(2)}) copy-start(f32[2,1024]{1,0:T(2,128)} %param.8) | copy-start | bytes 24580
  2.9 22.0 %copy-start.4 = (s32[1,64]{1,0:T(1,128)S(1)}, s32[1,64]{1,0:T(1,128)}, u32[]{:S(2)}) copy-start(s32[1,64]{1,0:T(1,128)} %order.1) | copy-start | bytes 772
  2.9 77.7 %all-to-all-start.1 = ((bf16[1,64,16,1,640]{4,2,3,0,1:T(8,128)(2,1)}), bf16[1,64,16,1,640]{4,2,3,0,1:T(8,128)(2,1)S(1)}, u32[]{:S(2)}, u32[]{:S(2)}) async-start(bf16[1,64,16,1,640]{4,2,3,0,1:T(8,128)(2,1)} %bitcast.23), calls=%async_computation.1 | async-start | bytes 2621440 | tf_op jit(solution)/shard_map/all_to_all | solution.py:239
  31.4 10.6 %collective-permute-start = (bf16[16,2176]{1,0:T(8,128)(2,1)S(1)}, bf16[16,2176]{1,0:T(8,128)(2,1)S(1)}, u32[]{:S(2)}, u32[]{:S(2)}) collective-permute-start(bf16[16,2176]{1,0:T(8,128)(2,1)S(1)} %get-tuple-element.25), channel_id=1, source_target_pairs={{0,8},{8,16},{16,24},{24,0},{32,40},{40,48},{48,56},{56,32},{64,72... | collective-permute-start | bytes 208904 | tf_op jit(solution)/shard_map/ppermute | solution.py:280
  34.5 7.7 %collective-permute-start.1 = (bf16[16,2176]{1,0:T(8,128)(2,1)S(1)}, bf16[16,2176]{1,0:T(8,128)(2,1)S(1)}, u32[]{:S(2)}, u32[]{:S(2)}) collective-permute-start(bf16[16,2176]{1,0:T(8,128)(2,1)S(1)} %get-tuple-element.24), channel_id=1, source_target_pairs={{0,16},{8,24},{16,0},{24,8},{32,48},{40,56},{48,32},{56,40},{64,80... | collective-permute-start | bytes 208904 | tf_op jit(solution)/shard_map/ppermute | solution.py:280
  38.8 5.6 %collective-permute-start.2 = (bf16[16,2176]{1,0:T(8,128)(2,1)S(1)}, bf16[16,2176]{1,0:T(8,128)(2,1)S(1)}, u32[]{:S(2)}, u32[]{:S(2)}) collective-permute-start(bf16[16,2176]{1,0:T(8,128)(2,1)S(1)} %get-tuple-element.23), channel_id=1, source_target_pairs={{0,24},{8,0},{16,8},{24,16},{32,56},{40,32},{48,40},{56,48},{64,88... | collective-permute-start | bytes 208904 | tf_op jit(solution)/shard_map/ppermute | solution.py:280
  45.2 64.3 %slice-start = ((f32[2,1024]{1,0:T(2,128)}), f32[2,640]{1,0:T(2,128)S(1)}, s32[]{:S(2)}) async-start(f32[2,1024]{1,0:T(2,128)} %param.8), calls=%async_computation.2 | async-start | bytes 10240 | tf_op jit(solution)/shard_map/jit(_roll_static)/slice | solution.py:273
  45.3 64.3 %slice-start.1 = ((f32[2,1024]{1,0:T(2,128)}), f32[2,384]{1,0:T(2,128)S(1)}, s32[]{:S(2)}) async-start(f32[2,1024]{1,0:T(2,128)} %param.8), calls=%async_computation.3 | async-start | bytes 6144 | tf_op jit(solution)/shard_map/jit(_roll_static)/slice | solution.py:273
  46.0 11.2 %collective-permute-start.3 = (bf16[16,4,512]{2,1,0:T(4,128)(2,1)S(1)}, bf16[16,4,512]{2,1,0:T(4,128)(2,1)S(1)}, u32[]{:S(2)}, u32[]{:S(2)}) collective-permute-start(bf16[16,4,512]{2,1,0:T(4,128)(2,1)S(1)} %get-tuple-element.20), channel_id=1, source_target_pairs={{0,1},{1,2},{2,3},{3,0},{4,5},{5,6},{6,7},{7,4},{8,9},{9,10},{10,1... | collective-permute-start | bytes 196616 | tf_op jit(solution)/shard_map/ppermute | solution.py:285
  49.1 8.1 %collective-permute-start.4 = (bf16[16,4,512]{2,1,0:T(4,128)(2,1)S(1)}, bf16[16,4,512]{2,1,0:T(4,128)(2,1)S(1)}, u32[]{:S(2)}, u32[]{:S(2)}) collective-permute-start(bf16[16,4,512]{2,1,0:T(4,128)(2,1)S(1)} %get-tuple-element.19), channel_id=1, source_target_pairs={{0,2},{1,3},{2,0},{3,1},{4,6},{5,7},{6,4},{7,5},{8,10},{9,11},{10,... | collective-permute-start | bytes 196616 | tf_op jit(solution)/shard_map/ppermute | solution.py:285
  53.5 5.3 %collective-permute-start.5 = (bf16[16,4,512]{2,1,0:T(4,128)(2,1)S(1)}, bf16[16,4,512]{2,1,0:T(4,128)(2,1)S(1)}, u32[]{:S(2)}, u32[]{:S(2)}) collective-permute-start(bf16[16,4,512]{2,1,0:T(4,128)(2,1)S(1)} %get-tuple-element.18), channel_id=1, source_target_pairs={{0,3},{1,0},{2,1},{3,2},{4,7},{5,4},{6,5},{7,6},{8,11},{9,8},{10,9... | collective-permute-start | bytes 196616 | tf_op jit(solution)/shard_map/ppermute | solution.py:285
  57.2 1.6 %copy-start = (bf16[16,4,512]{2,1,0:T(4,128)(2,1)}, bf16[16,4,512]{2,1,0:T(4,128)(2,1)S(1)}, u32[]{:S(2)}) copy-start(bf16[16,4,512]{2,1,0:T(4,128)(2,1)S(1)} %collective-permute-done.3.refs_1_) | copy-start | bytes 196612
  57.2 1.6 %copy-start.1 = (bf16[16,4,512]{2,1,0:T(4,128)(2,1)}, bf16[16,4,512]{2,1,0:T(4,128)(2,1)S(1)}, u32[]{:S(2)}) copy-start(bf16[16,4,512]{2,1,0:T(4,128)(2,1)S(1)} %collective-permute-done.4.refs_2_) | copy-start | bytes 196612
  58.8 0.6 copy-start.2
  80.6 24.0 %all-to-all-start = ((bf16[16,4,2176]{2,1,0:T(4,128)(2,1)}), bf16[16,4,2176]{2,1,0:T(4,128)(2,1)S(1)}, u32[]{:S(2)}, u32[]{:S(2)}) async-start(bf16[16,4,2176]{2,1,0:T(4,128)(2,1)} %pack.1), calls=%async_computation | async-start | bytes 557056 | tf_op jit(solution)/shard_map/all_to_all | solution.py:296
  92.1 19.9 %collective-permute-start.7 = (bf16[1024,640]{1,0:T(8,128)(2,1)S(1)}, bf16[1024,640]{1,0:T(8,128)(2,1)S(1)}, u32[]{:S(2)}, u32[]{:S(2)}) collective-permute-start(bf16[1024,640]{1,0:T(8,128)(2,1)S(1)} %bitcast.20), channel_id=1, source_target_pairs={{0,4},{4,0},{1,5},{5,1},{2,6},{6,2},{3,7},{7,3},{8,12},{12,8},{9,1... | collective-permute-start | bytes 3932168 | tf_op jit(solution)/shard_map/ppermute | solution.py:302
  104.6 14.5 %collective-permute-start.6 = (bf16[16,4,2176]{2,1,0:T(4,128)(2,1)S(1)}, bf16[16,4,2176]{2,1,0:T(4,128)(2,1)S(1)}, u32[]{:S(2)}, u32[]{:S(2)}) collective-permute-start(bf16[16,4,2176]{2,1,0:T(4,128)(2,1)S(1)} %all-to-all-done.sat), channel_id=1, source_target_pairs={{0,4},{4,0},{1,5},{5,1},{2,6},{6,2},{3,7},{7,3},{8,12},{12,8},{9,1... | collective-permute-start | bytes 835592 | tf_op jit(solution)/shard_map/ppermute | solution.py:299
